TPU v7x, 128 devices: a whole 4x4x4 slice. The times are simulated.
128 devices in a mesh: seq: 64 (over x_hi, z, y, core), tensor: 2 (over x_lo).
Axes of the slice: x: 4 (x_hi: 2, x_lo: 2; x = x_hi * 2 + x_lo), y: 4, z: 4, core: 2. Of those that a mesh axis runs over, the one named last changes fastest.
Arguments:
- hidden: bfloat16 [4096, 7168], P('seq', 'tensor'), may hold values from -200 to 200
- attn_gain: float32 [7168], P('tensor'), may hold values from 0.25 to 1.75
- kv_down: bfloat16 [7168, 576], P('tensor'), may hold values from -0.0625 to 0.0625
- kv_gain: float32 [512], replicated, may hold values from 0.25 to 1.75
- q_nope: bfloat16 [4096, 16384], P('seq', 'tensor'), may hold values from -90 to 90
- q_pe: bfloat16 [4096, 8192], P('seq', 'tensor'), may hold values from -6 to 6
- w_uk: bfloat16 [128, 128, 512], P('tensor'), may hold values from -0.5 to 0.5
- w_uv: bfloat16 [128, 512, 128], P('tensor'), may hold values from -1 to 1
- doc_ids: int32 [4096], replicated, may hold values from 0 to 3, never falling along the last dimension, each value on 1 to 3072 neighbouring positions
- slot_table: int32 [256], replicated, may hold values from 0 to 255, each once
Outputs:
- attn_values: bfloat16 [4096, 16384], P('seq', 'tensor')
- latent_cache: bfloat16 [4096, 576], P('seq')
Inputs may be any that keep to these rules, and one draw needn't show every extreme that they name: `doc_ids`: 4 documents packed in order, the longest exactly 3072 tokens. `slot_table`: each cache slot receives exactly one token block.
All inputs are finite; a program needn't handle non-finite values.
Results may differ from a plain program's by a relative error of at most 0.0093.
Values may be sent and summed in bfloat16 or wider, within the bound.
No kernel may reach another device: no remote copies, remote signals or barrier semaphores. Data moves between devices by JAX's collectives and lax.ppermute only.
A program may use at most 128 MiB of HBM per device.

v0:
```python
import functools
import math

import jax
import jax.numpy as jnp
from jax import lax
from jax.experimental import pallas as pl
from jax.experimental.pallas import tpu as pltpu
from jax.sharding import PartitionSpec as P


D = 7168
HEADS = 128
LATENT = 512
ROPE = 64
NOPE = 128
VD = 128
BLOCK = 16
WIDTH = 640

EPSILON = 1e-06
MASKED = -1e30
FLOOR = -1e20
SCALE = (NOPE + ROPE) ** (-0.5) * math.log2(math.e)

ROWS = 64
GROUP = 8
STEP = 256
PARTS = 7
ATTEND_MIB = 20


def params(mib, **kw):
    return pltpu.CompilerParams(vmem_limit_bytes=mib << 20, **kw)


def swap_halves(x, lane):
    return jnp.where(
        (lane & 63) < 32, pltpu.roll(x, 96, axis=1), pltpu.roll(x, 32, axis=1)
    )


def project_kernel(hidden_ref, gain_ref, down_ref, out_ref):
    k = pl.program_id(0)

    @pl.when(k == 0)
    def _():
        out_ref[...] = jnp.zeros_like(out_ref)

    widened = hidden_ref[...].astype(jnp.float32)
    normed = (widened * gain_ref[...].reshape(1, -1)).astype(jnp.bfloat16)
    product = lax.dot_general(
        normed, down_ref[...], (((1,), (1,)), ((), ())), preferred_element_type=jnp.float32
    )
    out_ref[:, : LATENT + ROPE] += product
    squares = jnp.sum(widened * widened, axis=1, keepdims=True)
    out_ref[:, LATENT + ROPE :] += jnp.broadcast_to(squares, (ROWS, WIDTH - LATENT - ROPE))


def project(hidden, attn_gain, kv_down):
    width = hidden.shape[1]
    tile = width // PARTS
    return pl.pallas_call(
        project_kernel,
        out_shape=jax.ShapeDtypeStruct((ROWS, WIDTH), jnp.float32),
        grid=(PARTS,),
        in_specs=[
            pl.BlockSpec((ROWS, tile), lambda k: (0, k)),
            pl.BlockSpec((tile,), lambda k: (k,)),
            pl.BlockSpec((LATENT + ROPE, tile), lambda k: (0, k)),
        ],
        out_specs=pl.BlockSpec((ROWS, WIDTH), lambda k: (0, 0)),
        compiler_params=params(8, dimension_semantics=("arbitrary",)),
        name="project",
    )(hidden, attn_gain, kv_down.T)


def finish_kernel(mine_ref, theirs_ref, cos_ref, sin_ref, gain_ref, out_ref):
    total = mine_ref[...] + theirs_ref[...]
    squares = total[:, WIDTH - 1 :]
    scaled = total * lax.rsqrt(squares / D + EPSILON)
    raw = scaled[:, :LATENT]
    mean = jnp.mean(raw * raw, axis=1, keepdims=True)
    latent = raw * lax.rsqrt(mean + EPSILON) * gain_ref[...]
    out_ref[:, :LATENT] = latent.astype(jnp.bfloat16)
    key = scaled[:, LATENT:]
    lane = lax.broadcasted_iota(jnp.int32, key.shape, 1)
    key = jnp.where(lane < ROPE, key, pltpu.roll(key, ROPE, axis=1))
    turned = key * cos_ref[...] + swap_halves(key, lane) * sin_ref[...]
    out_ref[:, LATENT:] = turned.astype(jnp.bfloat16)


def finish(mine, theirs, cosines, sines, kv_gain):
    return pl.pallas_call(
        finish_kernel,
        out_shape=jax.ShapeDtypeStruct((ROWS, WIDTH), jnp.bfloat16),
        compiler_params=params(4),
        name="finish",
    )(mine, theirs, cosines, sines, kv_gain.reshape(1, -1))


def queries_kernel(nope_ref, pe_ref, cos_ref, sin_ref, uk_ref, out_ref):
    lane = lax.broadcasted_iota(jnp.int32, (ROWS, 128), 1)
    for pair in range(GROUP // 2):
        pe = pe_ref[:, pair * 128 : (pair + 1) * 128].astype(jnp.float32)
        turned = pe * cos_ref[...] + swap_halves(pe, lane) * sin_ref[...]
        for side in range(2):
            head = 2 * pair + side
            rows = slice(head * ROWS, (head + 1) * ROWS)
            keep = (lane < ROPE) if side == 0 else (lane >= ROPE)
            out_ref[rows, LATENT:] = jnp.where(keep, turned, 0.0).astype(jnp.bfloat16)
            out_ref[rows, :LATENT] = jnp.dot(
                nope_ref[:, head * NOPE : (head + 1) * NOPE],
                uk_ref[head],
                preferred_element_type=jnp.float32,
            ).astype(jnp.bfloat16)


def make_queries(q_nope, q_pe, cosines, sines, w_uk):
    heads = w_uk.shape[0]
    return pl.pallas_call(
        queries_kernel,
        out_shape=jax.ShapeDtypeStruct((heads * ROWS, WIDTH), jnp.bfloat16),
        grid=(heads // GROUP,),
        in_specs=[
            pl.BlockSpec((ROWS, GROUP * NOPE), lambda g: (0, g)),
            pl.BlockSpec((ROWS, GROUP * ROPE), lambda g: (0, g)),
            pl.BlockSpec((ROWS, 128), lambda g: (0, 0)),
            pl.BlockSpec((ROWS, 128), lambda g: (0, 0)),
            pl.BlockSpec((GROUP, NOPE, LATENT), lambda g: (g, 0, 0)),
        ],
        out_specs=pl.BlockSpec((GROUP * ROWS, WIDTH), lambda g: (g, 0)),
        compiler_params=params(16, dimension_semantics=("arbitrary",)),
        name="queries",
    )(q_nope, q_pe, cosines, sines, w_uk)


def start_of(scalars, position):
    start = jnp.int32(0)
    for i in range(3):
        start = jnp.maximum(start, jnp.where(scalars[i] <= position, scalars[i], 0))
    return start


def attend_kernel(offsets, first, last, *refs):
    n = len(offsets)
    refs = list(refs)
    scalars = refs.pop(0)
    q_ref = refs.pop(0)
    sets = [refs.pop(0) for _ in range(n)]
    if last:
        uv_ref = refs.pop(0)
    if not first:
        before, refs = refs[:3], refs[3:]
    if last:
        out_ref = refs.pop(0)
        kv, ids, counts, even, odd, acc, m, l = refs
    else:
        acc, m, l = refs[:3]
        kv, ids, counts, even, odd = refs[3:]
    me = scalars[3]
    blocks = STEP // ROWS
    rows = GROUP * ROWS
    groups = q_ref.shape[0] // rows

    x, z, y, c = me // 32, (me // 8) & 3, (me // 2) & 3, me & 1
    lowest = start_of(scalars, me * ROWS)
    counts[0] = 0
    for a, (dy, dc) in enumerate(offsets):
        for b in range(8):
            dz, dx = b // 2, b % 2
            block = (x ^ dx) * 32 + ((z + dz) & 3) * 8 + ((y + dy) & 3) * 2 + (c ^ dc)
            needed = (block <= me) & (block * ROWS + ROWS - 1 >= lowest)

            @pl.when(needed)
            def _(a=a, b=b, block=block):
                at = counts[0]
                ids[at] = block
                kv[pl.ds(pl.multiple_of(at * ROWS, ROWS), ROWS), :] = sets[a][
                    b * ROWS : (b + 1) * ROWS, :
                ]
                counts[0] = at + 1

    found = counts[0]
    for i in range(blocks - 1):
        ids[found + i] = HEADS * 1024
        kv[pl.ds(pl.multiple_of((found + i) * ROWS, ROWS), ROWS), :] = jnp.zeros(
            (ROWS, WIDTH), jnp.bfloat16
        )
    steps = (found + blocks - 1) // blocks

    def ready(g, carry):
        at = pl.ds(pl.multiple_of(g * rows, rows), rows)
        if first:
            acc[at, :] = jnp.zeros((rows, LATENT), jnp.float32)
            m[at, :] = jnp.full((rows, 128), FLOOR, jnp.float32)
            l[at, :] = jnp.zeros((rows, 128), jnp.float32)
        else:
            for new, old in zip((acc, m, l), before):
                new[at, :] = old[at, :]
        return carry

    lax.fori_loop(0, groups, ready, 0)

    def keys_of(j):
        return kv[pl.ds(pl.multiple_of(j * STEP, STEP), STEP), :]

    def score(g, j, into):
        into[...] = lax.dot_general(
            q_ref[pl.ds(pl.multiple_of(g * rows, rows), rows), :],
            keys_of(j),
            (((1,), (1,)), ((), ())),
            preferred_element_type=jnp.float32,
        )

    def gather(g, j, scores):
        at = pl.ds(pl.multiple_of(g * rows, rows), rows)
        lane = lax.broadcasted_iota(jnp.int32, (ROWS, STEP), 1)
        key_block = jnp.full((ROWS, STEP), ids[blocks * j], jnp.int32)
        for i in range(1, blocks):
            key_block = jnp.where(lane >= i * ROWS, ids[blocks * j + i], key_block)
        key_position = key_block * ROWS + (lane & (ROWS - 1))
        position = me * ROWS + lax.broadcasted_iota(jnp.int32, (ROWS, STEP), 0)
        allowed = (key_position <= position) & (key_position >= start_of(scalars, position))
        s = jnp.where(allowed[None], scores[...].reshape(GROUP, ROWS, STEP), MASKED)
        s = s.reshape(rows, STEP)
        m_old = m[at, :]
        m_new = jnp.maximum(m_old, jnp.max(s, axis=1, keepdims=True))
        weights = jnp.exp2((s - jnp.tile(m_new, (1, STEP // 128))) * SCALE)
        factor = jnp.exp2((m_old - m_new) * SCALE)
        part = weights[:, :128]
        for i in range(1, STEP // 128):
            part = part + weights[:, i * 128 : (i + 1) * 128]
        l[at, :] = l[at, :] * factor + part
        m[at, :] = m_new
        acc[at, :] = acc[at, :] * jnp.tile(factor, (1, LATENT // 128)) + jnp.dot(
            weights.astype(jnp.bfloat16),
            keys_of(j)[:, :LATENT],
            preferred_element_type=jnp.float32,
        )

    def after(g, j):
        done = g + 1 == groups
        return jnp.where(done, 0, g + 1), jnp.where(done, j + 1, j)

    @pl.when(steps > 0)
    def _():
        score(0, 0, even)

        def two(i, at):
            later = after(*at)
            score(*later, odd)
            gather(*at, even)
            at = after(*later)
            score(*at, even)
            gather(*later, odd)
            return at

        lax.fori_loop(0, steps * (groups // 2), two, (jnp.int32(0), jnp.int32(0)))

    if last:
        def give(g, carry):
            for head in range(GROUP):
                at = pl.ds(pl.multiple_of(g * rows + head * ROWS, ROWS), ROWS)
                total = jnp.sum(l[at, :], axis=1, keepdims=True)
                mixed = (acc[at, :] * (1.0 / total)).astype(jnp.bfloat16)
                out_ref[:, pl.ds(pl.multiple_of((g * GROUP + head) * VD, VD), VD)] = jnp.dot(
                    mixed, uv_ref[g * GROUP + head], preferred_element_type=jnp.float32
                ).astype(jnp.bfloat16)
            return carry

        lax.fori_loop(0, groups, give, 0)


def attend(scalars, queries, sets, offsets, state, w_uv):
    first, last = state is None, w_uv is not None
    n = len(sets)
    rows = GROUP * ROWS
    total = queries.shape[0]
    operands = [queries, *sets]
    if last:
        operands.append(w_uv)
    widths = (LATENT, 128, 128)
    aliases = {}
    if not first:
        if not last:
            aliases = {1 + len(operands) + i: i for i in range(len(widths))}
        operands += list(state)
    room = 8 * n + 2 * STEP // ROWS
    scratch = [
        pltpu.VMEM((room * ROWS, WIDTH), jnp.bfloat16),
        pltpu.SMEM((room,), jnp.int32),
        pltpu.SMEM((4,), jnp.int32),
        pltpu.VMEM((rows, STEP), jnp.float32),
        pltpu.VMEM((rows, STEP), jnp.float32),
    ]
    whole = pl.BlockSpec(memory_space=pltpu.VMEM)
    if last:
        out_shape = jax.ShapeDtypeStruct((ROWS, total // ROWS * VD), jnp.bfloat16)
        out_specs = whole
        scratch += [pltpu.VMEM((total, w), jnp.float32) for w in widths]
    else:
        out_shape = [jax.ShapeDtypeStruct((total, w), jnp.float32) for w in widths]
        out_specs = [whole] * len(widths)
    flops = 2 * total * 8 * n * ROWS * (WIDTH + LATENT)
    return pl.pallas_call(
        functools.partial(attend_kernel, offsets, first, last),
        out_shape=out_shape,
        in_specs=[pl.BlockSpec(memory_space=pltpu.SMEM)] + [whole] * len(operands),
        out_specs=out_specs,
        scratch_shapes=scratch,
        input_output_aliases=aliases,
        compiler_params=params(ATTEND_MIB),
        cost_estimate=pl.CostEstimate(
            flops=flops, transcendentals=total * 8 * n * ROWS, bytes_accessed=24 << 20
        ),
    )(scalars, *operands)


def cache_kernel(scalars, *refs):
    sets, (out_ref, buffer, sems) = refs[:8], refs[8:]
    me = scalars[3]
    x, z, y, c = me // 32, (me // 8) & 3, (me // 2) & 3, me & 1
    for slot in range(ROWS // BLOCK):
        group = scalars[4 + slot]
        block = group // 4
        dx, dz = (block // 32) ^ x, ((block // 8) - z) & 3
        dy, dc = ((block // 2) - y) & 3, (block & 1) ^ c
        row = (dz * 2 + dx) * ROWS + (group & 3) * BLOCK
        which = dc * 4 + dy
        for a in range(8):

            @pl.when(which == a)
            def _(a=a, row=row, slot=slot):
                pltpu.make_async_copy(
                    sets[a].at[pl.ds(pl.multiple_of(row, BLOCK), BLOCK), :],
                    buffer.at[slot * BLOCK : (slot + 1) * BLOCK, :],
                    sems.at[slot],
                ).start()

    for slot in range(ROWS // BLOCK):
        pltpu.make_async_copy(
            sets[0].at[:BLOCK, :],
            buffer.at[slot * BLOCK : (slot + 1) * BLOCK, :],
            sems.at[slot],
        ).wait()
    out_ref[...] = buffer[:, : LATENT + ROPE]


def cache_rows(scalars, sets):
    return pl.pallas_call(
        cache_kernel,
        out_shape=jax.ShapeDtypeStruct((ROWS, LATENT + ROPE), jnp.bfloat16),
        grid_spec=pltpu.PrefetchScalarGridSpec(
            num_scalar_prefetch=1,
            grid=(),
            in_specs=[pl.BlockSpec(memory_space=pl.ANY)] * 8,
            out_specs=pl.BlockSpec(memory_space=pltpu.VMEM),
            scratch_shapes=[
                pltpu.VMEM((ROWS, WIDTH), jnp.bfloat16),
                pltpu.SemaphoreType.DMA((ROWS // BLOCK,)),
            ],
        ),
        compiler_params=params(4),
        name="cache_rows",
    )(scalars, *sets)


def shard_of(x, z, y, c):
    return (x % 2) * 32 + (z % 4) * 8 + (y % 4) * 2 + c % 2


def fetch(array, dx=0, dz=0, dy=0, dc=0):
    everyone = [
        (x, z, y, c) for x in range(2) for z in range(4) for y in range(4) for c in range(2)
    ]
    pairs = [
        (shard_of(x + dx, z + dz, y + dy, c + dc), shard_of(x, z, y, c))
        for x, z, y, c in everyone
    ]
    return lax.ppermute(array, "seq", pairs)


def local(hidden, attn_gain, kv_down, kv_gain, q_nope, q_pe, w_uk, w_uv, doc_ids, slot_table):
    me = lax.axis_index("seq")
    positions = (me * ROWS + jnp.arange(ROWS, dtype=jnp.int32)).astype(jnp.float32)
    half = ROPE // 2
    frequency = jnp.exp(jnp.arange(half, dtype=jnp.float32) * (-2.0 * math.log(10000.0) / ROPE))
    angle = positions[:, None] * jnp.tile(frequency, 4)[None, :]
    sign = jnp.where((jnp.arange(128) & 63) < half, -1.0, 1.0).astype(jnp.float32)
    cosines, sines = jnp.cos(angle), jnp.sin(angle) * sign[None, :]

    starts = jnp.sum(
        (doc_ids[None, :] < jnp.arange(1, 4, dtype=jnp.int32)[:, None]).astype(jnp.int32), axis=1
    )
    slots = me * (ROWS // BLOCK) + jnp.arange(ROWS // BLOCK, dtype=jnp.int32)
    groups = jnp.arange(slot_table.shape[0], dtype=jnp.int32)
    held = jnp.sum(jnp.where(slot_table[None, :] == slots[:, None], groups[None, :], 0), axis=1)
    scalars = jnp.concatenate([starts, me[None].astype(jnp.int32), held])

    mine = project(hidden, attn_gain, kv_down)
    theirs = lax.ppermute(mine, "tensor", [(0, 1), (1, 0)])
    queries = make_queries(q_nope, q_pe, cosines, sines, w_uk)
    own = finish(mine, theirs, cosines, sines, kv_gain)

    two = jnp.concatenate([own, fetch(own, dx=1)], axis=0)
    eight = jnp.concatenate([two] + [fetch(two, dz=d) for d in (1, 2, 3)], axis=0)
    across = {0: eight}
    for d in (1, 3, 2):
        across[d] = fetch(eight, dy=d)
    beside = {d: fetch(across[d], dc=1) for d in (0, 1, 3, 2)}

    state = attend(
        scalars, queries, [across[0], beside[0]], [(0, 0), (0, 1)], None, None
    )
    state = attend(
        scalars,
        queries,
        [across[1], across[3], beside[1], beside[3]],
        [(1, 0), (3, 0), (1, 1), (3, 1)],
        state,
        None,
    )
    attn_values = attend(scalars, queries, [across[2], beside[2]], [(2, 0), (2, 1)], state, w_uv)
    latent_cache = cache_rows(
        scalars, [across[d] for d in range(4)] + [beside[d] for d in range(4)]
    )
    return attn_values, latent_cache


def solution(mesh):
    placed = (
        P("seq", "tensor"),
        P("tensor"),
        P("tensor", None),
        P(),
        P("seq", "tensor"),
        P("seq", "tensor"),
        P("tensor", None, None),
        P("tensor", None, None),
        P(),
        P(),
    )
    return jax.shard_map(
        local,
        mesh=mesh,
        in_specs=placed,
        out_specs=(P("seq", "tensor"), P("seq", None)),
        check_vma=False,
    )
```

profile of v0, /device:TPU:103, one launch (start us, length us, event | category | flops | bytes accessed | tf_op | source)
XLA Modules:
  0.0 125.7 jit_solution(18052685972800406832)
XLA Ops:
  0.6 2.2 %copy-done.1 = bf16[3584,576]{0,1:T(8,128)(2,1)S(1)} copy-done((bf16[3584,576]{0,1:T(8,128)(2,1)S(1)}, bf16[3584,576]{0,1:T(8,128)(2,1)}, u32[]{:S(2)}) %copy-start.1) | copy-done | bytes 4128792
  2.8 1.0 copy-done.4
  3.8 0.7 copy-done.9
  4.5 2.6 %project.1.mine_ref = f32[64,640]{1,0:T(8,128)S(1)} custom-call(bf16[64,3584]{1,0:T(8,128)(2,1)S(1)} %copy-done.4, f32[3584]{0:T(1024)S(1)} %copy-done.9, bf16[576,3584]{1,0:T(8,128)(2,1)S(1)} %bitcast.3), custom_call_target="tpu_custom_call" | custom-call | tf_op jit(solution)/shard_map/project/pallas_call | solution.py:63
  7.2 0.6 collective-permute-start
  7.9 0.2 fusion
  8.1 4.2 %collective-permute-done.theirs_ref = f32[64,640]{1,0:T(8,128)S(1)} collective-permute-done((f32[64,640]{1,0:T(8,128)S(1)}, f32[64,640]{1,0:T(8,128)S(1)}, u32[]{:S(2)}, u32[]{:S(2)}) %collective-permute-start) | collective-permute-done | bytes 163872 | tf_op jit(solution)/shard_map/ppermute | solution.py:402
  12.3 0.7 copy-done.10
  13.0 0.2 finish.1
  13.2 1.2 collective-permute-start.1
  14.4 3.7 %collective-permute-done.1 = bf16[64,640]{1,0:T(8,128)(2,1)S(1)} collective-permute-done((bf16[64,640]{1,0:T(8,128)(2,1)S(1)}, bf16[64,640]{1,0:T(8,128)(2,1)S(1)}, u32[]{:S(2)}, u32[]{:S(2)}) %collective-permute-start.1) | collective-permute-done | bytes 81952 | tf_op jit(solution)/shard_map/ppermute | solution.py:381
  18.2 0.2 collective-permute-start.2
  18.4 2.6 %collective-permute-start.4 = (bf16[128,640]{1,0:T(8,128)(2,1)S(1)}, bf16[128,640]{1,0:T(8,128)(2,1)S(1)}, u32[]{:S(2)}, u32[]{:S(2)}) collective-permute-start(bf16[128,640]{1,0:T(8,128)(2,1)S(1)} %pad_maximum_fusion), channel_id=1, source_target_pairs={{48,0},{50,2},{52,4},{54,6},{56,8},{58,10},{60,12},{62,14},{0,16},... | collective-permute-start | bytes 491528 | tf_op jit(solution)/shard_map/ppermute | solution.py:381
  21.0 2.6 %collective-permute-done.2 = bf16[128,640]{1,0:T(8,128)(2,1)S(1)} collective-permute-done((bf16[128,640]{1,0:T(8,128)(2,1)S(1)}, bf16[128,640]{1,0:T(8,128)(2,1)S(1)}, u32[]{:S(2)}, u32[]{:S(2)}) %collective-permute-start.2) | collective-permute-done | bytes 163872 | tf_op jit(solution)/shard_map/ppermute | solution.py:381
  23.6 3.1 %collective-permute-done.3 = bf16[128,640]{1,0:T(8,128)(2,1)S(1)} collective-permute-done((bf16[128,640]{1,0:T(8,128)(2,1)S(1)}, bf16[128,640]{1,0:T(8,128)(2,1)S(1)}, u32[]{:S(2)}, u32[]{:S(2)}) %collective-permute-start.3) | collective-permute-done | bytes 163872 | tf_op jit(solution)/shard_map/ppermute | solution.py:381
  26.8 1.4 %collective-permute-start.8 = (bf16[512,640]{1,0:T(8,128)(2,1)S(1)}, bf16[512,640]{1,0:T(8,128)(2,1)S(1)}, u32[]{:S(2)}, u32[]{:S(2)}) collective-permute-start(bf16[512,640]{1,0:T(8,128)(2,1)S(1)} %constant_dynamic-update-slice_fusion.refs_2_.refs_0_), channel_id=1, source_target_pairs={{12,0},{14,2},{0,4},{2,6},{4,8},{6,10},{8,12},{10,14},{28,16},{30,... | collective-permute-start | bytes 1966088 | tf_op jit(solution)/shard_map/ppermute | solution.py:381
  28.2 1.5 %collective-permute-start.7 = (bf16[512,640]{1,0:T(8,128)(2,1)S(1)}, bf16[512,640]{1,0:T(8,128)(2,1)}, u32[]{:S(2)}, u32[]{:S(2)}) collective-permute-start(bf16[512,640]{1,0:T(8,128)(2,1)S(1)} %constant_dynamic-update-slice_fusion.refs_2_.refs_0_), channel_id=1, source_target_pairs={{4,0},{6,2},{8,4},{10,6},{12,8},{14,10},{0,12},{2,14},{20,16},{22,... | collective-permute-start | bytes 1966088 | tf_op jit(solution)/shard_map/ppermute | solution.py:381
  29.7 1.6 %collective-permute-start.5 = (bf16[512,640]{1,0:T(8,128)(2,1)S(1)}, bf16[512,640]{1,0:T(8,128)(2,1)S(1)}, u32[]{:S(2)}, u32[]{:S(2)}) collective-permute-start(bf16[512,640]{1,0:T(8,128)(2,1)S(1)} %constant_dynamic-update-slice_fusion.refs_2_.refs_0_), channel_id=1, source_target_pairs={{8,0},{10,2},{12,4},{14,6},{0,8},{2,10},{4,12},{6,14},{24,16},{26,... | collective-permute-start | bytes 1966088 | tf_op jit(solution)/shard_map/ppermute | solution.py:381
  31.3 5.1 %collective-permute-start.11 = (bf16[512,640]{1,0:T(8,128)(2,1)S(1)}, bf16[512,640]{1,0:T(8,128)(2,1)}, u32[]{:S(2)}, u32[]{:S(2)}) collective-permute-start(bf16[512,640]{1,0:T(8,128)(2,1)S(1)} %constant_dynamic-update-slice_fusion.refs_2_.refs_0_), channel_id=1, source_target_pairs={{2,0},{0,2},{6,4},{4,6},{10,8},{8,10},{14,12},{12,14},{18,16},{16,... | collective-permute-start | bytes 1966088 | tf_op jit(solution)/shard_map/ppermute | solution.py:381
  36.4 3.4 %copy-done = bf16[64,128,512]{2,1,0:T(8,128)(2,1)S(1)} copy-done((bf16[64,128,512]{2,1,0:T(8,128)(2,1)S(1)}, bf16[64,128,512]{2,1,0:T(8,128)(2,1)}, u32[]{:S(2)}) %copy-start) | copy-done | bytes 8388632
  39.8 0.8 copy-done.6
  40.6 0.8 copy-done.8
  41.3 2.6 %queries.1.refs_1_ = bf16[4096,640]{1,0:T(8,128)(2,1)S(1)} custom-call(bf16[64,8192]{1,0:T(8,128)(2,1)S(1)} %copy-done.2, bf16[64,4096]{1,0:T(8,128)(2,1)S(1)} %copy-done.3, f32[64,128]{1,0:T(8,128)S(1)} %copy-done.8, f32[64,128]{1,0:T(8,128)S(1)} %copy-done.6, bf16[64,128,512]{2,1,0:T(8,128)(2,1)S(1)} %copy-done), custom_call_target="tpu_custom_call" | custom-call | tf_op jit(solution)/shard_map/queries/pallas_call | solution.py:121
  43.9 0.2 select_reduce_fusion
  44.1 0.2 convert_reduce_fusion
  44.4 4.4 %collective-permute-start.10 = (bf16[512,640]{1,0:T(8,128)(2,1)S(1)}, bf16[512,640]{1,0:T(8,128)(2,1)S(1)}, u32[]{:S(2)}, u32[]{:S(2)}) collective-permute-start(bf16[512,640]{1,0:T(8,128)(2,1)S(1)} %collective-permute-done.8.refs_3_), channel_id=1, source_target_pairs={{2,0},{0,2},{6,4},{4,6},{10,8},{8,10},{14,12},{12,14},{18,16},{16,... | collective-permute-start | bytes 1966088 | tf_op jit(solution)/shard_map/ppermute | solution.py:381
  48.9 9.8 %collective-permute-start.9 = (bf16[512,640]{1,0:T(8,128)(2,1)}, bf16[512,640]{1,0:T(8,128)(2,1)S(1)}, u32[]{:S(2)}, u32[]{:S(2)}) collective-permute-start(bf16[512,640]{1,0:T(8,128)(2,1)} %collective-permute-done.7.refs_2_.refs_1_), channel_id=1, source_target_pairs={{2,0},{0,2},{6,4},{4,6},{10,8},{8,10},{14,12},{12,14},{18,16},{16,... | collective-permute-start | bytes 1966088 | tf_op jit(solution)/shard_map/ppermute | solution.py:381
  58.7 1.8 %collective-permute-start.6 = (bf16[512,640]{1,0:T(8,128)(2,1)S(1)}, bf16[512,640]{1,0:T(8,128)(2,1)S(1)}, u32[]{:S(2)}, u32[]{:S(2)}) collective-permute-start(bf16[512,640]{1,0:T(8,128)(2,1)S(1)} %collective-permute-done.5.refs_2_), channel_id=1, source_target_pairs={{2,0},{0,2},{6,4},{4,6},{10,8},{8,10},{14,12},{12,14},{18,16},{16,... | collective-permute-start | bytes 1966088 | tf_op jit(solution)/shard_map/ppermute | solution.py:381
  60.5 15.2 %shard_map.113 = (f32[4096,512]{1,0:T(8,128)S(1)}, f32[4096,128]{1,0:T(8,128)S(1)}, f32[4096,128]{1,0:T(8,128)S(1)}) custom-call(s32[8]{0:T(128)S(1)} %pad_add_fusion.refs_0_.scalars, bf16[4096,640]{1,0:T(8,128)(2,1)S(1)} %queries.1.refs_1_, bf16[512,640]{1,0:T(8,128)(2,1)S(1)} %constant_dynamic-update-slice_fusion.refs_2_.refs_0_, ...), custom_call_target="tpu_custom_call" | custom-call | flops 9663676416 | bytes 25165824 | tf_op jit(solution)/shard_map/pallas_call | solution.py:306
  75.8 2.6 %cache_rows.1 = bf16[64,576]{1,0:T(8,128)(2,1)} custom-call(s32[8]{0:T(128)S(1)} %pad_add_fusion.refs_0_.scalars, bf16[512,640]{1,0:T(8,128)(2,1)S(1)} %constant_dynamic-update-slice_fusion.refs_2_.refs_0_, bf16[512,640]{1,0:T(8,128)(2,1)} %collective-permute-done.7.refs_2_.refs_1_, bf16[512,640]{1,0:T(8,128)(2,1)S(1)} %collective-permute-done.5.refs_2_, ...), custom_call_target="tpu_custom_call" | custom-call | tf_op jit(solution)/shard_map/cache_rows/pallas_call | solution.py:351
  78.4 28.8 %shard_map.114 = (f32[4096,512]{1,0:T(8,128)S(1)}, f32[4096,128]{1,0:T(8,128)S(1)}, f32[4096,128]{1,0:T(8,128)S(1)}) custom-call(s32[8]{0:T(128)S(1)} %pad_add_fusion.refs_0_.scalars, bf16[4096,640]{1,0:T(8,128)(2,1)S(1)} %queries.1.refs_1_, ...), custom_call_target="tpu_custom_call", output_to_operand_aliasing={{0}: (6, {}), {1}: (7, {}), {2}: (8, {})} | custom-call | flops 19327352832 | bytes 25165824 | tf_op jit(solution)/shard_map/pallas_call | solution.py:306
  107.3 18.4 %shard_map.115 = bf16[64,8192]{1,0:T(8,128)(2,1)} custom-call(s32[8]{0:T(128)S(1)} %pad_add_fusion.refs_0_.scalars, bf16[4096,640]{1,0:T(8,128)(2,1)S(1)} %queries.1.refs_1_, bf16[512,640]{1,0:T(8,128)(2,1)S(1)} %collective-permute-done.5.refs_2_, bf16[512,640]{1,0:T(8,128)(2,1)S(1)} %collective-permute-done.6.refs_3_.refs_6_, ...), custom_call_target="tpu_custom_call" | custom-call | flops 9663676416 | bytes 25165824 | tf_op jit(solution)/shard_map/pallas_call | solution.py:306
  (47 shorter events, 0.4 us)
Async XLA Ops:
  0.6 2.2 %copy-start.1 = (bf16[3584,576]{0,1:T(8,128)(2,1)S(1)}, bf16[3584,576]{0,1:T(8,128)(2,1)}, u32[]{:S(2)}) copy-start(bf16[3584,576]{0,1:T(8,128)(2,1)} %param.12) | copy-start | bytes 12386308
  2.8 1.0 copy-start.4
  3.8 0.7 copy-start.9
  4.5 31.9 %copy-start.2 = (bf16[64,8192]{1,0:T(8,128)(2,1)S(1)}, bf16[64,8192]{1,0:T(8,128)(2,1)}, u32[]{:S(2)}) copy-start(bf16[64,8192]{1,0:T(8,128)(2,1)} %nope_ref.1) | copy-start | bytes 3145732
  4.5 31.9 %copy-start.3 = (bf16[64,4096]{1,0:T(8,128)(2,1)S(1)}, bf16[64,4096]{1,0:T(8,128)(2,1)}, u32[]{:S(2)}) copy-start(bf16[64,4096]{1,0:T(8,128)(2,1)} %pe_ref.1) | copy-start | bytes 1572868
  7.2 5.2 %collective-permute-start = (f32[64,640]{1,0:T(8,128)S(1)}, f32[64,640]{1,0:T(8,128)S(1)}, u32[]{:S(2)}, u32[]{:S(2)}) collective-permute-start(f32[64,640]{1,0:T(8,128)S(1)} %project.1.mine_ref), channel_id=1, source_target_pairs={{0,1},{1,0},{2,3},{3,2},{4,5},{5,4},{6,7},{7,6},{8,9},{9,8},{10,11... | collective-permute-start | bytes 491528 | tf_op jit(solution)/shard_map/ppermute | solution.py:402
  8.1 10.0 %copy-start.5 = (f32[64,128]{1,0:T(8,128)}, f32[64,128]{1,0:T(8,128)S(1)}, u32[]{:S(2)}) copy-start(f32[64,128]{1,0:T(8,128)S(1)} %get-tuple-element.14.sin_ref) | copy-start | bytes 98308
  8.1 10.0 %copy-start.7 = (f32[64,128]{1,0:T(8,128)}, f32[64,128]{1,0:T(8,128)S(1)}, u32[]{:S(2)}) copy-start(f32[64,128]{1,0:T(8,128)S(1)} %get-tuple-element.15.cos_ref) | copy-start | bytes 98308
  12.3 0.7 copy-start.10
  13.2 4.9 %collective-permute-start.1 = (bf16[64,640]{1,0:T(8,128)(2,1)S(1)}, bf16[64,640]{1,0:T(8,128)(2,1)S(1)}, u32[]{:S(2)}, u32[]{:S(2)}) collective-permute-start(bf16[64,640]{1,0:T(8,128)(2,1)S(1)} %finish.1), channel_id=1, source_target_pairs={{64,0},{66,2},{68,4},{70,6},{72,8},{74,10},{76,12},{78,14},{80,16}... | collective-permute-start | bytes 245768 | tf_op jit(solution)/shard_map/ppermute | solution.py:381
  18.2 5.4 %collective-permute-start.2 = (bf16[128,640]{1,0:T(8,128)(2,1)S(1)}, bf16[128,640]{1,0:T(8,128)(2,1)S(1)}, u32[]{:S(2)}, u32[]{:S(2)}) collective-permute-start(bf16[128,640]{1,0:T(8,128)(2,1)S(1)} %pad_maximum_fusion), channel_id=1, source_target_pairs={{16,0},{18,2},{20,4},{22,6},{24,8},{26,10},{28,12},{30,14},{32,16}... | collective-permute-start | bytes 491528 | tf_op jit(solution)/shard_map/ppermute | solution.py:381
  18.4 8.4 %collective-permute-start.4 = (bf16[128,640]{1,0:T(8,128)(2,1)S(1)}, bf16[128,640]{1,0:T(8,128)(2,1)S(1)}, u32[]{:S(2)}, u32[]{:S(2)}) collective-permute-start(bf16[128,640]{1,0:T(8,128)(2,1)S(1)} %pad_maximum_fusion), channel_id=1, source_target_pairs={{48,0},{50,2},{52,4},{54,6},{56,8},{58,10},{60,12},{62,14},{0,16},... | collective-permute-start | bytes 491528 | tf_op jit(solution)/shard_map/ppermute | solution.py:381
  21.0 5.8 %collective-permute-start.3 = (bf16[128,640]{1,0:T(8,128)(2,1)S(1)}, bf16[128,640]{1,0:T(8,128)(2,1)S(1)}, u32[]{:S(2)}, u32[]{:S(2)}) collective-permute-start(bf16[128,640]{1,0:T(8,128)(2,1)S(1)} %pad_maximum_fusion), channel_id=1, source_target_pairs={{32,0},{34,2},{36,4},{38,6},{40,8},{42,10},{44,12},{46,14},{48,16}... | collective-permute-start | bytes 491528 | tf_op jit(solution)/shard_map/ppermute | solution.py:381
  26.8 17.6 %collective-permute-start.8 = (bf16[512,640]{1,0:T(8,128)(2,1)S(1)}, bf16[512,640]{1,0:T(8,128)(2,1)S(1)}, u32[]{:S(2)}, u32[]{:S(2)}) collective-permute-start(bf16[512,640]{1,0:T(8,128)(2,1)S(1)} %constant_dynamic-update-slice_fusion.refs_2_.refs_0_), channel_id=1, source_target_pairs={{12,0},{14,2},{0,4},{2,6},{4,8},{6,10},{8,12},{10,14},{28,16},{30,... | collective-permute-start | bytes 1966088 | tf_op jit(solution)/shard_map/ppermute | solution.py:381
  28.2 20.7 %collective-permute-start.7 = (bf16[512,640]{1,0:T(8,128)(2,1)S(1)}, bf16[512,640]{1,0:T(8,128)(2,1)}, u32[]{:S(2)}, u32[]{:S(2)}) collective-permute-start(bf16[512,640]{1,0:T(8,128)(2,1)S(1)} %constant_dynamic-update-slice_fusion.refs_2_.refs_0_), channel_id=1, source_target_pairs={{4,0},{6,2},{8,4},{10,6},{12,8},{14,10},{0,12},{2,14},{20,16},{22,... | collective-permute-start | bytes 1966088 | tf_op jit(solution)/shard_map/ppermute | solution.py:381
  29.7 29.0 %collective-permute-start.5 = (bf16[512,640]{1,0:T(8,128)(2,1)S(1)}, bf16[512,640]{1,0:T(8,128)(2,1)S(1)}, u32[]{:S(2)}, u32[]{:S(2)}) collective-permute-start(bf16[512,640]{1,0:T(8,128)(2,1)S(1)} %constant_dynamic-update-slice_fusion.refs_2_.refs_0_), channel_id=1, source_target_pairs={{8,0},{10,2},{12,4},{14,6},{0,8},{2,10},{4,12},{6,14},{24,16},{26,... | collective-permute-start | bytes 1966088 | tf_op jit(solution)/shard_map/ppermute | solution.py:381
  31.3 29.3 %collective-permute-start.11 = (bf16[512,640]{1,0:T(8,128)(2,1)S(1)}, bf16[512,640]{1,0:T(8,128)(2,1)}, u32[]{:S(2)}, u32[]{:S(2)}) collective-permute-start(bf16[512,640]{1,0:T(8,128)(2,1)S(1)} %constant_dynamic-update-slice_fusion.refs_2_.refs_0_), channel_id=1, source_target_pairs={{2,0},{0,2},{6,4},{4,6},{10,8},{8,10},{14,12},{12,14},{18,16},{16,... | collective-permute-start | bytes 1966088 | tf_op jit(solution)/shard_map/ppermute | solution.py:381
  36.4 3.4 %copy-start = (bf16[64,128,512]{2,1,0:T(8,128)(2,1)S(1)}, bf16[64,128,512]{2,1,0:T(8,128)(2,1)}, u32[]{:S(2)}) copy-start(bf16[64,128,512]{2,1,0:T(8,128)(2,1)} %uk_ref.1) | copy-start | bytes 25165828
  39.8 0.8 copy-start.6
  40.5 0.8 copy-start.8
  41.3 2.6 %copy-start.12 = (s32[256]{0:T(256)S(1)}, s32[256]{0:T(256)}, u32[]{:S(2)}) copy-start(s32[256]{0:T(256)} %param.19) | copy-start | bytes 3076
  41.3 2.8 %copy-start.11 = (s32[4096]{0:T(1024)S(1)}, s32[4096]{0:T(1024)}, u32[]{:S(2)}) copy-start(s32[4096]{0:T(1024)} %param.18) | copy-start | bytes 49156
  44.4 31.4 %collective-permute-start.10 = (bf16[512,640]{1,0:T(8,128)(2,1)S(1)}, bf16[512,640]{1,0:T(8,128)(2,1)S(1)}, u32[]{:S(2)}, u32[]{:S(2)}) collective-permute-start(bf16[512,640]{1,0:T(8,128)(2,1)S(1)} %collective-permute-done.8.refs_3_), channel_id=1, source_target_pairs={{2,0},{0,2},{6,4},{4,6},{10,8},{8,10},{14,12},{12,14},{18,16},{16,... | collective-permute-start | bytes 1966088 | tf_op jit(solution)/shard_map/ppermute | solution.py:381
  48.9 26.9 %collective-permute-start.9 = (bf16[512,640]{1,0:T(8,128)(2,1)}, bf16[512,640]{1,0:T(8,128)(2,1)S(1)}, u32[]{:S(2)}, u32[]{:S(2)}) collective-permute-start(bf16[512,640]{1,0:T(8,128)(2,1)} %collective-permute-done.7.refs_2_.refs_1_), channel_id=1, source_target_pairs={{2,0},{0,2},{6,4},{4,6},{10,8},{8,10},{14,12},{12,14},{18,16},{16,... | collective-permute-start | bytes 1966088 | tf_op jit(solution)/shard_map/ppermute | solution.py:381
  58.7 17.1 %collective-permute-start.6 = (bf16[512,640]{1,0:T(8,128)(2,1)S(1)}, bf16[512,640]{1,0:T(8,128)(2,1)S(1)}, u32[]{:S(2)}, u32[]{:S(2)}) collective-permute-start(bf16[512,640]{1,0:T(8,128)(2,1)S(1)} %collective-permute-done.5.refs_2_), channel_id=1, source_target_pairs={{2,0},{0,2},{6,4},{4,6},{10,8},{8,10},{14,12},{12,14},{18,16},{16,... | collective-permute-start | bytes 1966088 | tf_op jit(solution)/shard_map/ppermute | solution.py:381
  75.8 31.4 %slice-start = ((s8[8388608]{0:T(1024)(128)(4,1)}), s8[4194304]{0:T(1024)(128)(4,1)S(1)}, s32[]{:S(2)}) async-start(s8[8388608]{0:T(1024)(128)(4,1)} %bitcast.5), calls=%async_computation | async-start | bytes 8388608
  78.4 28.8 %slice-start.1 = ((s8[8388608]{0:T(1024)(128)(4,1)}), s8[4194304]{0:T(1024)(128)(4,1)S(1)}, s32[]{:S(2)}) async-start(s8[8388608]{0:T(1024)(128)(4,1)} %bitcast.5), calls=%async_computation.1 | async-start | bytes 8388608
where the time goes:
time: 128 us; the launch traced here: 126 us
  Pallas kernels  70.5 us (55%)
  starting transfers between devices  30.3 us (24%)
  waiting for transfers between devices  13.6 us (11%)
  local copies, waits for them, and re-layouts  9.69 us (8%)
    pallas_call x3, Pallas kernels, attend(): pl.pallas_call(functools.partial(attend_kernel, offsets, first, last), ou...  62.5 us
    ppermute x11, starting transfers between devices, fetch(): return lax.ppermute(array, 'seq', pairs)  29.7 us
    unnamed x34, local copies, waits for them, and re-layouts  9.58 us
    ppermute x11, waiting for transfers between devices, fetch(): return lax.ppermute(array, 'seq', pairs)  9.42 us
    ppermute x1, waiting for transfers between devices, local(): theirs = lax.ppermute(mine, 'tensor', [(0, 1), (1, 0)])  4.19 us
    pallas_call x1, Pallas kernels, project(): pl.pallas_call(project_kernel, out_shape=jax.ShapeDtypeStruct((ROWS, WIDT...  2.61 us
    pallas_call x1, Pallas kernels, make_queries(): pl.pallas_call(queries_kernel, out_shape=jax.ShapeDtypeStruct((heads * RO...  2.59 us
  transfers between devices with their start and end apart: 12, of which 4 were waited for; matrix products, arithmetic and copies ran while one was open for 1% of the time, Pallas kernels for 14%

commit v1 on v0

--- a/solution.py
+++ b/solution.py
@@ -24,10 +24,12 @@
 SCALE = (NOPE + ROPE) ** (-0.5) * math.log2(math.e)
 
 ROWS = 64
-GROUP = 8
+PACK = 8
+GROUP = 16
 STEP = 256
 PARTS = 7
-ATTEND_MIB = 20
+ATTEND_MIB = 14
+COPY_STATE = False
 
 
 def params(mib, **kw):
@@ -40,42 +42,59 @@
     )
 
 
-def project_kernel(hidden_ref, gain_ref, down_ref, out_ref):
-    k = pl.program_id(0)
-
-    @pl.when(k == 0)
-    def _():
-        out_ref[...] = jnp.zeros_like(out_ref)
-
-    widened = hidden_ref[...].astype(jnp.float32)
-    normed = (widened * gain_ref[...].reshape(1, -1)).astype(jnp.bfloat16)
-    product = lax.dot_general(
-        normed, down_ref[...], (((1,), (1,)), ((), ())), preferred_element_type=jnp.float32
-    )
-    out_ref[:, : LATENT + ROPE] += product
-    squares = jnp.sum(widened * widened, axis=1, keepdims=True)
-    out_ref[:, LATENT + ROPE :] += jnp.broadcast_to(squares, (ROWS, WIDTH - LATENT - ROPE))
+def project_kernel(hidden_hbm, gain_hbm, down_hbm, out_ref, hidden, gain, down, sems):
+    tile = hidden.shape[1] // PARTS
+    first = pltpu.make_async_copy(hidden_hbm, hidden, sems.at[PARTS])
+    second = pltpu.make_async_copy(gain_hbm, gain, sems.at[PARTS + 1])
+    first.start()
+    second.start()
+    parts = []
+    for k in range(PARTS):
+        columns = slice(k * tile, (k + 1) * tile)
+        parts.append(
+            pltpu.make_async_copy(
+                down_hbm.at[:, columns], down.at[:, columns], sems.at[k]
+            )
+        )
+        parts[-1].start()
+    first.wait()
+    second.wait()
+    squares = jnp.zeros((ROWS, 1), jnp.float32)
+    for k in range(PARTS):
+        columns = slice(k * tile, (k + 1) * tile)
+        widened = hidden[:, columns].astype(jnp.float32)
+        normed = (widened * gain[columns].reshape(1, -1)).astype(jnp.bfloat16)
+        squares = squares + jnp.sum(widened * widened, axis=1, keepdims=True)
+        parts[k].wait()
+        product = lax.dot_general(
+            normed, down[:, columns], (((1,), (1,)), ((), ())), preferred_element_type=jnp.float32
+        )
+        if k == 0:
+            out_ref[:, : LATENT + ROPE] = product
+        else:
+            out_ref[:, : LATENT + ROPE] += product
+    out_ref[:, LATENT + ROPE :] = jnp.broadcast_to(squares, (ROWS, WIDTH - LATENT - ROPE))
 
 
 def project(hidden, attn_gain, kv_down):
     width = hidden.shape[1]
-    tile = width // PARTS
     return pl.pallas_call(
         project_kernel,
         out_shape=jax.ShapeDtypeStruct((ROWS, WIDTH), jnp.float32),
-        grid=(PARTS,),
-        in_specs=[
-            pl.BlockSpec((ROWS, tile), lambda k: (0, k)),
-            pl.BlockSpec((tile,), lambda k: (k,)),
-            pl.BlockSpec((LATENT + ROPE, tile), lambda k: (0, k)),
+        in_specs=[pl.BlockSpec(memory_space=pltpu.HBM)] * 3,
+        out_specs=pl.BlockSpec(memory_space=pltpu.VMEM),
+        scratch_shapes=[
+            pltpu.VMEM((ROWS, width), jnp.bfloat16),
+            pltpu.VMEM((width,), jnp.float32),
+            pltpu.VMEM((LATENT + ROPE, width), jnp.bfloat16),
+            pltpu.SemaphoreType.DMA((PARTS + 2,)),
         ],
-        out_specs=pl.BlockSpec((ROWS, WIDTH), lambda k: (0, 0)),
-        compiler_params=params(8, dimension_semantics=("arbitrary",)),
+        compiler_params=params(60),
         name="project",
     )(hidden, attn_gain, kv_down.T)
 
 
-def finish_kernel(mine_ref, theirs_ref, cos_ref, sin_ref, gain_ref, out_ref):
+def finish_kernel(scalars, mine_ref, theirs_ref, cos_ref, sin_ref, gain_ref, out_ref):
     total = mine_ref[...] + theirs_ref[...]
     squares = total[:, WIDTH - 1 :]
     scaled = total * lax.rsqrt(squares / D + EPSILON)
@@ -90,18 +109,36 @@
     out_ref[:, LATENT:] = turned.astype(jnp.bfloat16)
 
 
-def finish(mine, theirs, cosines, sines, kv_gain):
+def finish(scalars, mine, theirs, cosines, sines, kv_gain):
     return pl.pallas_call(
         finish_kernel,
         out_shape=jax.ShapeDtypeStruct((ROWS, WIDTH), jnp.bfloat16),
+        in_specs=[pl.BlockSpec(memory_space=pltpu.SMEM)]
+        + [pl.BlockSpec(memory_space=pltpu.VMEM)] * 5,
         compiler_params=params(4),
         name="finish",
-    )(mine, theirs, cosines, sines, kv_gain.reshape(1, -1))
+    )(scalars, mine, theirs, cosines, sines, kv_gain.reshape(1, -1))
+
+
+def join_kernel(*refs):
+    parts, out_ref = refs[:-1], refs[-1]
+    at = 0
+    for part in parts:
+        out_ref[at : at + part.shape[0], :] = part[...]
+        at += part.shape[0]
+
+
+def join(parts):
+    return pl.pallas_call(
+        join_kernel,
+        out_shape=jax.ShapeDtypeStruct((sum(p.shape[0] for p in parts), WIDTH), jnp.bfloat16),
+        compiler_params=params(4),
+    )(*parts)
 
 
 def queries_kernel(nope_ref, pe_ref, cos_ref, sin_ref, uk_ref, out_ref):
     lane = lax.broadcasted_iota(jnp.int32, (ROWS, 128), 1)
-    for pair in range(GROUP // 2):
+    for pair in range(PACK // 2):
         pe = pe_ref[:, pair * 128 : (pair + 1) * 128].astype(jnp.float32)
         turned = pe * cos_ref[...] + swap_halves(pe, lane) * sin_ref[...]
         for side in range(2):
@@ -121,15 +158,15 @@
     return pl.pallas_call(
         queries_kernel,
         out_shape=jax.ShapeDtypeStruct((heads * ROWS, WIDTH), jnp.bfloat16),
-        grid=(heads // GROUP,),
+        grid=(heads // PACK,),
         in_specs=[
-            pl.BlockSpec((ROWS, GROUP * NOPE), lambda g: (0, g)),
-            pl.BlockSpec((ROWS, GROUP * ROPE), lambda g: (0, g)),
+            pl.BlockSpec((ROWS, PACK * NOPE), lambda g: (0, g)),
+            pl.BlockSpec((ROWS, PACK * ROPE), lambda g: (0, g)),
             pl.BlockSpec((ROWS, 128), lambda g: (0, 0)),
             pl.BlockSpec((ROWS, 128), lambda g: (0, 0)),
-            pl.BlockSpec((GROUP, NOPE, LATENT), lambda g: (g, 0, 0)),
+            pl.BlockSpec((PACK, NOPE, LATENT), lambda g: (g, 0, 0)),
         ],
-        out_specs=pl.BlockSpec((GROUP * ROWS, WIDTH), lambda g: (g, 0)),
+        out_specs=pl.BlockSpec((PACK * ROWS, WIDTH), lambda g: (g, 0)),
         compiler_params=params(16, dimension_semantics=("arbitrary",)),
         name="queries",
     )(q_nope, q_pe, cosines, sines, w_uk)
@@ -150,14 +187,15 @@
     sets = [refs.pop(0) for _ in range(n)]
     if last:
         uv_ref = refs.pop(0)
+        others, refs = refs[:6], refs[6:]
     if not first:
         before, refs = refs[:3], refs[3:]
+    acc, m, l = refs[:3]
+    refs = refs[3:]
     if last:
-        out_ref = refs.pop(0)
-        kv, ids, counts, even, odd, acc, m, l = refs
-    else:
-        acc, m, l = refs[:3]
-        kv, ids, counts, even, odd = refs[3:]
+        out_ref, cache_ref = refs[:2]
+        refs = refs[2:]
+    kv, ids, counts, even, odd = refs
     me = scalars[3]
     blocks = STEP // ROWS
     rows = GROUP * ROWS
@@ -200,7 +238,8 @@
                 new[at, :] = old[at, :]
         return carry
 
-    lax.fori_loop(0, groups, ready, 0)
+    if first or COPY_STATE:
+        lax.fori_loop(0, groups, ready, 0)
 
     def keys_of(j):
         return kv[pl.ds(pl.multiple_of(j * STEP, STEP), STEP), :]
@@ -259,6 +298,21 @@
         lax.fori_loop(0, steps * (groups // 2), two, (jnp.int32(0), jnp.int32(0)))
 
     if last:
+        where = [(0, 0), (0, 1), (1, 0), (3, 0), (1, 1), (3, 1), (2, 0), (2, 1)]
+        for slot in range(ROWS // BLOCK):
+            group = scalars[4 + slot]
+            block = group // 4
+            dx, dz = (block // 32) ^ x, ((block // 8) - z) & 3
+            dy, dc = ((block // 2) - y) & 3, (block & 1) ^ c
+            row = pl.multiple_of((dz * 2 + dx) * ROWS + (group & 3) * BLOCK, BLOCK)
+            for source, (oy, oc) in zip([*others, *sets], where):
+
+                @pl.when((dy == oy) & (dc == oc))
+                def _(source=source, row=row, slot=slot):
+                    cache_ref[slot * BLOCK : (slot + 1) * BLOCK, :] = source[
+                        pl.ds(row, BLOCK), :
+                    ][:, : LATENT + ROPE]
+
         def give(g, carry):
             for head in range(GROUP):
                 at = pl.ds(pl.multiple_of(g * rows + head * ROWS, ROWS), ROWS)
@@ -272,19 +326,18 @@
         lax.fori_loop(0, groups, give, 0)
 
 
-def attend(scalars, queries, sets, offsets, state, w_uv):
+def attend(scalars, queries, sets, offsets, state=None, w_uv=None, others=()):
     first, last = state is None, w_uv is not None
     n = len(sets)
     rows = GROUP * ROWS
     total = queries.shape[0]
+    widths = (LATENT, 128, 128)
     operands = [queries, *sets]
     if last:
-        operands.append(w_uv)
-    widths = (LATENT, 128, 128)
+        operands += [w_uv, *others]
     aliases = {}
     if not first:
-        if not last:
-            aliases = {1 + len(operands) + i: i for i in range(len(widths))}
+        aliases = {1 + len(operands) + i: i for i in range(len(widths))}
         operands += list(state)
     room = 8 * n + 2 * STEP // ROWS
     scratch = [
@@ -295,19 +348,18 @@
         pltpu.VMEM((rows, STEP), jnp.float32),
     ]
     whole = pl.BlockSpec(memory_space=pltpu.VMEM)
+    out_shape = [jax.ShapeDtypeStruct((total, w), jnp.float32) for w in widths]
     if last:
-        out_shape = jax.ShapeDtypeStruct((ROWS, total // ROWS * VD), jnp.bfloat16)
-        out_specs = whole
-        scratch += [pltpu.VMEM((total, w), jnp.float32) for w in widths]
-    else:
-        out_shape = [jax.ShapeDtypeStruct((total, w), jnp.float32) for w in widths]
-        out_specs = [whole] * len(widths)
+        out_shape += [
+            jax.ShapeDtypeStruct((ROWS, total // ROWS * VD), jnp.bfloat16),
+            jax.ShapeDtypeStruct((ROWS, LATENT + ROPE), jnp.bfloat16),
+        ]
     flops = 2 * total * 8 * n * ROWS * (WIDTH + LATENT)
-    return pl.pallas_call(
+    out = pl.pallas_call(
         functools.partial(attend_kernel, offsets, first, last),
         out_shape=out_shape,
         in_specs=[pl.BlockSpec(memory_space=pltpu.SMEM)] + [whole] * len(operands),
-        out_specs=out_specs,
+        out_specs=[whole] * len(out_shape),
         scratch_shapes=scratch,
         input_output_aliases=aliases,
         compiler_params=params(ATTEND_MIB),
@@ -315,55 +367,7 @@
             flops=flops, transcendentals=total * 8 * n * ROWS, bytes_accessed=24 << 20
         ),
     )(scalars, *operands)
-
-
-def cache_kernel(scalars, *refs):
-    sets, (out_ref, buffer, sems) = refs[:8], refs[8:]
-    me = scalars[3]
-    x, z, y, c = me // 32, (me // 8) & 3, (me // 2) & 3, me & 1
-    for slot in range(ROWS // BLOCK):
-        group = scalars[4 + slot]
-        block = group // 4
-        dx, dz = (block // 32) ^ x, ((block // 8) - z) & 3
-        dy, dc = ((block // 2) - y) & 3, (block & 1) ^ c
-        row = (dz * 2 + dx) * ROWS + (group & 3) * BLOCK
-        which = dc * 4 + dy
-        for a in range(8):
-
-            @pl.when(which == a)
-            def _(a=a, row=row, slot=slot):
-                pltpu.make_async_copy(
-                    sets[a].at[pl.ds(pl.multiple_of(row, BLOCK), BLOCK), :],
-                    buffer.at[slot * BLOCK : (slot + 1) * BLOCK, :],
-                    sems.at[slot],
-                ).start()
-
-    for slot in range(ROWS // BLOCK):
-        pltpu.make_async_copy(
-            sets[0].at[:BLOCK, :],
-            buffer.at[slot * BLOCK : (slot + 1) * BLOCK, :],
-            sems.at[slot],
-        ).wait()
-    out_ref[...] = buffer[:, : LATENT + ROPE]
-
-
-def cache_rows(scalars, sets):
-    return pl.pallas_call(
-        cache_kernel,
-        out_shape=jax.ShapeDtypeStruct((ROWS, LATENT + ROPE), jnp.bfloat16),
-        grid_spec=pltpu.PrefetchScalarGridSpec(
-            num_scalar_prefetch=1,
-            grid=(),
-            in_specs=[pl.BlockSpec(memory_space=pl.ANY)] * 8,
-            out_specs=pl.BlockSpec(memory_space=pltpu.VMEM),
-            scratch_shapes=[
-                pltpu.VMEM((ROWS, WIDTH), jnp.bfloat16),
-                pltpu.SemaphoreType.DMA((ROWS // BLOCK,)),
-            ],
-        ),
-        compiler_params=params(4),
-        name="cache_rows",
-    )(scalars, *sets)
+    return out[3:] if last else out
 
 
 def shard_of(x, z, y, c):
@@ -401,29 +405,26 @@
     mine = project(hidden, attn_gain, kv_down)
     theirs = lax.ppermute(mine, "tensor", [(0, 1), (1, 0)])
     queries = make_queries(q_nope, q_pe, cosines, sines, w_uk)
-    own = finish(mine, theirs, cosines, sines, kv_gain)
-
-    two = jnp.concatenate([own, fetch(own, dx=1)], axis=0)
-    eight = jnp.concatenate([two] + [fetch(two, dz=d) for d in (1, 2, 3)], axis=0)
+    own = finish(scalars, mine, theirs, cosines, sines, kv_gain)
+
+    two = join([own, fetch(own, dx=1)])
+    eight = join([two] + [fetch(two, dz=d) for d in (1, 2, 3)])
     across = {0: eight}
     for d in (1, 3, 2):
         across[d] = fetch(eight, dy=d)
     beside = {d: fetch(across[d], dc=1) for d in (0, 1, 3, 2)}
 
-    state = attend(
-        scalars, queries, [across[0], beside[0]], [(0, 0), (0, 1)], None, None
-    )
-    state = attend(
+    state = attend(scalars, queries, [across[0], beside[0]], [(0, 0), (0, 1)])
+    state = attend(scalars, queries, [across[1], across[3]], [(1, 0), (3, 0)], state)
+    state = attend(scalars, queries, [beside[1], beside[3]], [(1, 1), (3, 1)], state)
+    attn_values, latent_cache = attend(
         scalars,
         queries,
-        [across[1], across[3], beside[1], beside[3]],
-        [(1, 0), (3, 0), (1, 1), (3, 1)],
+        [across[2], beside[2]],
+        [(2, 0), (2, 1)],
         state,
-        None,
-    )
-    attn_values = attend(scalars, queries, [across[2], beside[2]], [(2, 0), (2, 1)], state, w_uv)
-    latent_cache = cache_rows(
-        scalars, [across[d] for d in range(4)] + [beside[d] for d in range(4)]
+        w_uv,
+        [across[0], beside[0], across[1], across[3], beside[1], beside[3]],
     )
     return attn_values, latent_cache
 

time: 128 us -> 117 us (0.914)
  Pallas kernels: 70.5 us -> 63.2 us
  local copies, waits for them, and re-layouts: 9.69 us -> 4.42 us
    pallas_call x3 -> x4, Pallas kernels: 62.5 us -> 55.6 us  [attend(): pl.pallas_call(functools.partial(attend_kernel, offsets, first, last), ou...]
    unnamed x34 -> x18, local copies, waits for them, and re-layouts: 9.58 us -> 4.33 us
    pallas_call x1 -> x2, Pallas kernels: 2.56 us -> 0.07 us  [join(): pl.pallas_call(join_kernel, out_shape=jax.ShapeDtypeStruct((sum((p.shape[...]
    pallas_call x1, Pallas kernels: 2.61 us -> 4.24 us  [project(): pl.pallas_call(project_kernel, out_shape=jax.ShapeDtypeStruct((ROWS, WIDT...]
  transfers between devices with their start and end apart: 12 -> 12, of which waited for: 4 -> 5; matrix products, arithmetic and copies ran while one was open for 1% -> 1% of each run, Pallas kernels for 14% -> 37%
where the time goes in v1:
time: 117 us; the launch traced here: 115 us
  Pallas kernels  63.2 us (54%)
  starting transfers between devices  31.5 us (27%)
  waiting for transfers between devices  13.9 us (12%)
  local copies, waits for them, and re-layouts  4.42 us (4%)
    pallas_call x4, Pallas kernels, attend(): pl.pallas_call(functools.partial(attend_kernel, offsets, first, last), ou...  55.6 us
    ppermute x11, starting transfers between devices, fetch(): return lax.ppermute(array, 'seq', pairs)  30.9 us
    ppermute x11, waiting for transfers between devices, fetch(): return lax.ppermute(array, 'seq', pairs)  9.96 us
    unnamed x18, local copies, waits for them, and re-layouts  4.33 us
    pallas_call x1, Pallas kernels, project(): pl.pallas_call(project_kernel, out_shape=jax.ShapeDtypeStruct((ROWS, WIDT...  4.24 us
    ppermute x1, waiting for transfers between devices, local(): theirs = lax.ppermute(mine, 'tensor', [(0, 1), (1, 0)])  3.9 us
    pallas_call x1, Pallas kernels, make_queries(): pl.pallas_call(queries_kernel, out_shape=jax.ShapeDtypeStruct((heads * RO...  2.59 us
  transfers between devices with their start and end apart: 12, of which 5 were waited for; matrix products, arithmetic and copies ran while one was open for 1% of the time, Pallas kernels for 37%

profile of v1, /device:TPU:103, one launch (start us, length us, event | category | flops | bytes accessed | tf_op | source)
XLA Modules:
  0.0 114.6 jit_solution(12136744370387740638)
XLA Ops:
  0.7 4.2 %project.1.mine_ref = f32[64,640]{1,0:T(8,128)} custom-call(bf16[64,3584]{1,0:T(8,128)(2,1)} %hidden_hbm.1, f32[3584]{0:T(1024)} %gain_hbm.1, bf16[576,3584]{1,0:T(8,128)(2,1)} %bitcast.6), custom_call_target="tpu_custom_call" | custom-call | tf_op jit(solution)/shard_map/project/pallas_call | solution.py:81
  4.9 0.6 collective-permute-start
  5.6 0.1 mul.44
  5.7 0.2 convert_reduce_fusion
  5.9 0.2 fusion
  6.1 0.2 select_reduce_fusion
  6.3 0.1 pad_add_fusion.scalars.refs_0_
  6.4 3.9 %collective-permute-done.theirs_ref = f32[64,640]{1,0:T(8,128)S(1)} collective-permute-done((f32[64,640]{1,0:T(8,128)}, f32[64,640]{1,0:T(8,128)S(1)}, u32[]{:S(2)}, u32[]{:S(2)}) %collective-permute-start) | collective-permute-done | bytes 163872 | tf_op jit(solution)/shard_map/ppermute | solution.py:406
  10.3 0.9 copy-done.2
  11.2 0.8 finish.1.refs_0_
  12.0 1.2 %collective-permute-start.1 = (bf16[64,640]{1,0:T(8,128)(2,1)S(1)}, bf16[64,640]{1,0:T(8,128)(2,1)S(1)}, u32[]{:S(2)}, u32[]{:S(2)}) collective-permute-start(bf16[64,640]{1,0:T(8,128)(2,1)S(1)} %finish.1.refs_0_), channel_id=1, source_target_pairs={{64,0},{66,2},{68,4},{70,6},{72,8},{74,10},{76,12},{78,14},{80,16}... | collective-permute-start | bytes 245768 | tf_op jit(solution)/shard_map/ppermute | solution.py:385
  13.2 3.7 %collective-permute-done.1.refs_1_ = bf16[64,640]{1,0:T(8,128)(2,1)S(1)} collective-permute-done((bf16[64,640]{1,0:T(8,128)(2,1)S(1)}, bf16[64,640]{1,0:T(8,128)(2,1)S(1)}, u32[]{:S(2)}, u32[]{:S(2)}) %collective-permute-start.1) | collective-permute-done | bytes 81952 | tf_op jit(solution)/shard_map/ppermute | solution.py:385
  16.9 0.1 collective-permute-start.4
  17.0 1.9 %collective-permute-start.3 = (bf16[128,640]{1,0:T(8,128)(2,1)S(1)}, bf16[128,640]{1,0:T(8,128)(2,1)S(1)}, u32[]{:S(2)}, u32[]{:S(2)}) collective-permute-start(bf16[128,640]{1,0:T(8,128)(2,1)S(1)} %shard_map.113.refs_0_), channel_id=1, source_target_pairs={{32,0},{34,2},{36,4},{38,6},{40,8},{42,10},{44,12},{46,14},{48,16}... | collective-permute-start | bytes 491528 | tf_op jit(solution)/shard_map/ppermute | solution.py:385
  18.9 2.2 %collective-permute-done.4.refs_3_ = bf16[128,640]{1,0:T(8,128)(2,1)S(1)} collective-permute-done((bf16[128,640]{1,0:T(8,128)(2,1)S(1)}, bf16[128,640]{1,0:T(8,128)(2,1)S(1)}, u32[]{:S(2)}, u32[]{:S(2)}) %collective-permute-start.4) | collective-permute-done | bytes 163872 | tf_op jit(solution)/shard_map/ppermute | solution.py:385
  21.1 1.6 %collective-permute-done.3.refs_2_ = bf16[128,640]{1,0:T(8,128)(2,1)S(1)} collective-permute-done((bf16[128,640]{1,0:T(8,128)(2,1)S(1)}, bf16[128,640]{1,0:T(8,128)(2,1)S(1)}, u32[]{:S(2)}, u32[]{:S(2)}) %collective-permute-start.3) | collective-permute-done | bytes 163872 | tf_op jit(solution)/shard_map/ppermute | solution.py:385
  22.8 2.4 %collective-permute-done.2.refs_1_ = bf16[128,640]{1,0:T(8,128)(2,1)S(1)} collective-permute-done((bf16[128,640]{1,0:T(8,128)(2,1)S(1)}, bf16[128,640]{1,0:T(8,128)(2,1)S(1)}, u32[]{:S(2)}, u32[]{:S(2)}) %collective-permute-start.2) | collective-permute-done | bytes 163872 | tf_op jit(solution)/shard_map/ppermute | solution.py:385
  25.1 0.1 shard_map.114.refs_2_.refs_5_
  25.2 1.4 %collective-permute-start.9 = (bf16[512,640]{1,0:T(8,128)(2,1)S(1)}, bf16[512,640]{1,0:T(8,128)(2,1)S(1)}, u32[]{:S(2)}, u32[]{:S(2)}) collective-permute-start(bf16[512,640]{1,0:T(8,128)(2,1)S(1)} %shard_map.114.refs_2_.refs_5_), channel_id=1, source_target_pairs={{12,0},{14,2},{0,4},{2,6},{4,8},{6,10},{8,12},{10,14},{28,16},{30,... | collective-permute-start | bytes 1966088 | tf_op jit(solution)/shard_map/ppermute | solution.py:385
  26.6 1.5 %collective-permute-start.8 = (bf16[512,640]{1,0:T(8,128)(2,1)S(1)}, bf16[512,640]{1,0:T(8,128)(2,1)S(1)}, u32[]{:S(2)}, u32[]{:S(2)}) collective-permute-start(bf16[512,640]{1,0:T(8,128)(2,1)S(1)} %shard_map.114.refs_2_.refs_5_), channel_id=1, source_target_pairs={{4,0},{6,2},{8,4},{10,6},{12,8},{14,10},{0,12},{2,14},{20,16},{22,... | collective-permute-start | bytes 1966088 | tf_op jit(solution)/shard_map/ppermute | solution.py:385
  28.1 1.6 %collective-permute-start.5 = (bf16[512,640]{1,0:T(8,128)(2,1)S(1)}, bf16[512,640]{1,0:T(8,128)(2,1)S(1)}, u32[]{:S(2)}, u32[]{:S(2)}) collective-permute-start(bf16[512,640]{1,0:T(8,128)(2,1)S(1)} %shard_map.114.refs_2_.refs_5_), channel_id=1, source_target_pairs={{8,0},{10,2},{12,4},{14,6},{0,8},{2,10},{4,12},{6,14},{24,16},{26,... | collective-permute-start | bytes 1966088 | tf_op jit(solution)/shard_map/ppermute | solution.py:385
  29.7 4.6 %collective-permute-start.7 = (bf16[512,640]{1,0:T(8,128)(2,1)S(1)}, bf16[512,640]{1,0:T(8,128)(2,1)S(1)}, u32[]{:S(2)}, u32[]{:S(2)}) collective-permute-start(bf16[512,640]{1,0:T(8,128)(2,1)S(1)} %shard_map.114.refs_2_.refs_5_), channel_id=1, source_target_pairs={{2,0},{0,2},{6,4},{4,6},{10,8},{8,10},{14,12},{12,14},{18,16},{16,... | collective-permute-start | bytes 1966088 | tf_op jit(solution)/shard_map/ppermute | solution.py:385
  34.3 3.4 %copy-done = bf16[64,128,512]{2,1,0:T(8,128)(2,1)S(1)} copy-done((bf16[64,128,512]{2,1,0:T(8,128)(2,1)S(1)}, bf16[64,128,512]{2,1,0:T(8,128)(2,1)}, u32[]{:S(2)}) %copy-start) | copy-done | bytes 8388632
  37.6 2.6 %queries.1.refs_1_ = bf16[4096,640]{1,0:T(8,128)(2,1)S(1)} custom-call(bf16[64,8192]{1,0:T(8,128)(2,1)S(1)} %copy-done.1, bf16[64,4096]{1,0:T(8,128)(2,1)S(1)} %copy-done.3, f32[64,128]{1,0:T(8,128)S(1)} %get-tuple-element.25.cos_ref, f32[64,128]{1,0:T(8,128)S(1)} %get-tuple-element.24.sin_ref, bf16[64,128,512]{2,1,0:T(8,128)(2,1)S(1)} %copy-done), custom_call_target="tpu_custom_call" | custom-call | tf_op jit(solution)/shard_map/queries/pallas_call | solution.py:158
  40.3 6.5 %collective-permute-start.11 = (bf16[512,640]{1,0:T(8,128)(2,1)S(1)}, bf16[512,640]{1,0:T(8,128)(2,1)S(1)}, u32[]{:S(2)}, u32[]{:S(2)}) collective-permute-start(bf16[512,640]{1,0:T(8,128)(2,1)S(1)} %collective-permute-done.9.refs_3_.refs_8_), channel_id=1, source_target_pairs={{2,0},{0,2},{6,4},{4,6},{10,8},{8,10},{14,12},{12,14},{18,16},{16,... | collective-permute-start | bytes 1966088 | tf_op jit(solution)/shard_map/ppermute | solution.py:385
  46.7 10.4 %collective-permute-start.10 = (bf16[512,640]{1,0:T(8,128)(2,1)S(1)}, bf16[512,640]{1,0:T(8,128)(2,1)S(1)}, u32[]{:S(2)}, u32[]{:S(2)}) collective-permute-start(bf16[512,640]{1,0:T(8,128)(2,1)S(1)} %collective-permute-done.8.refs_2_.refs_7_), channel_id=1, source_target_pairs={{2,0},{0,2},{6,4},{4,6},{10,8},{8,10},{14,12},{12,14},{18,16},{16,... | collective-permute-start | bytes 1966088 | tf_op jit(solution)/shard_map/ppermute | solution.py:385
  57.1 1.8 %collective-permute-start.6 = (bf16[512,640]{1,0:T(8,128)(2,1)S(1)}, bf16[512,640]{1,0:T(8,128)(2,1)S(1)}, u32[]{:S(2)}, u32[]{:S(2)}) collective-permute-start(bf16[512,640]{1,0:T(8,128)(2,1)S(1)} %collective-permute-done.5.refs_2_), channel_id=1, source_target_pairs={{2,0},{0,2},{6,4},{4,6},{10,8},{8,10},{14,12},{12,14},{18,16},{16,... | collective-permute-start | bytes 1966088 | tf_op jit(solution)/shard_map/ppermute | solution.py:385
  58.9 13.6 %shard_map.115 = (f32[4096,512]{1,0:T(8,128)S(1)}, f32[4096,128]{1,0:T(8,128)S(1)}, f32[4096,128]{1,0:T(8,128)S(1)}) custom-call(s32[8]{0:T(128)S(1)} %pad_add_fusion.scalars.refs_0_, bf16[4096,640]{1,0:T(8,128)(2,1)S(1)} %queries.1.refs_1_, bf16[512,640]{1,0:T(8,128)(2,1)S(1)} %shard_map.114.refs_2_.refs_5_, ...), custom_call_target="tpu_custom_call" | custom-call | flops 9663676416 | bytes 25165824 | tf_op jit(solution)/shard_map/pallas_call | solution.py:358
  72.5 12.8 %shard_map.116 = (f32[4096,512]{1,0:T(8,128)S(1)}, f32[4096,128]{1,0:T(8,128)S(1)}, f32[4096,128]{1,0:T(8,128)S(1)}) custom-call(s32[8]{0:T(128)S(1)} %pad_add_fusion.scalars.refs_0_, bf16[4096,640]{1,0:T(8,128)(2,1)S(1)} %queries.1.refs_1_, ...), custom_call_target="tpu_custom_call", output_to_operand_aliasing={{0}: (4, {}), {1}: (5, {}), {2}: (6, {})} | custom-call | flops 9663676416 | bytes 25165824 | tf_op jit(solution)/shard_map/pallas_call | solution.py:358
  85.3 0.0 slice-start.1
  85.4 13.0 %shard_map.117 = (f32[4096,512]{1,0:T(8,128)S(1)}, f32[4096,128]{1,0:T(8,128)S(1)}, f32[4096,128]{1,0:T(8,128)S(1)}) custom-call(s32[8]{0:T(128)S(1)} %pad_add_fusion.scalars.refs_0_, bf16[4096,640]{1,0:T(8,128)(2,1)S(1)} %queries.1.refs_1_, ...), custom_call_target="tpu_custom_call", output_to_operand_aliasing={{0}: (4, {}), {1}: (5, {}), {2}: (6, {})} | custom-call | flops 9663676416 | bytes 25165824 | tf_op jit(solution)/shard_map/pallas_call | solution.py:358
  98.4 16.2 %shard_map.118 = (f32[4096,512]{1,0:T(8,128)S(1)}, f32[4096,128]{1,0:T(8,128)S(1)}, f32[4096,128]{1,0:T(8,128)S(1)}, bf16[64,8192]{1,0:T(8,128)(2,1)}, bf16[64,576]{1,0:T(8,128)(2,1)}) custom-call(s32[8]{0:T(128)S(1)} %pad_add_fusion.scalars.refs_0_, ...), custom_call_target="tpu_custom_call", output_to_operand_aliasing={{0}: (11, {}), {1}: (12, {}), {2}: (13, {})} | custom-call | flops 9663676416 | bytes 25165824 | tf_op jit(solution)/shard_map/pallas_call | solution.py:358
  (31 shorter events, 0.1 us)
Async XLA Ops:
  0.6 5.1 %copy-start.5 = (s32[4096]{0:T(1024)S(1)}, s32[4096]{0:T(1024)}, u32[]{:S(2)}) copy-start(s32[4096]{0:T(1024)} %param.18) | copy-start | bytes 49156
  0.6 5.5 %copy-start.6 = (s32[256]{0:T(256)S(1)}, s32[256]{0:T(256)}, u32[]{:S(2)}) copy-start(s32[256]{0:T(256)} %param.19) | copy-start | bytes 3076
  0.7 9.7 %copy-start.4 = (f32[512]{0:T(512)S(1)}, f32[512]{0:T(512)}, u32[]{:S(2)}) copy-start(f32[512]{0:T(512)} %param.13) | copy-start | bytes 6148
  0.7 33.6 %copy-start.3 = (bf16[64,4096]{1,0:T(8,128)(2,1)S(1)}, bf16[64,4096]{1,0:T(8,128)(2,1)}, u32[]{:S(2)}) copy-start(bf16[64,4096]{1,0:T(8,128)(2,1)} %pe_ref.1) | copy-start | bytes 1572868
  0.7 33.6 %copy-start.1 = (bf16[64,8192]{1,0:T(8,128)(2,1)S(1)}, bf16[64,8192]{1,0:T(8,128)(2,1)}, u32[]{:S(2)}) copy-start(bf16[64,8192]{1,0:T(8,128)(2,1)} %nope_ref.1) | copy-start | bytes 3145732
  4.9 5.4 %collective-permute-start = (f32[64,640]{1,0:T(8,128)}, f32[64,640]{1,0:T(8,128)S(1)}, u32[]{:S(2)}, u32[]{:S(2)}) collective-permute-start(f32[64,640]{1,0:T(8,128)} %project.1.mine_ref), channel_id=1, source_target_pairs={{0,1},{1,0},{2,3},{3,2},{4,5},{5,4},{6,7},{7,6},{8,9},{9,8},{10,11... | collective-permute-start | bytes 491528 | tf_op jit(solution)/shard_map/ppermute | solution.py:406
  10.3 0.9 copy-start.2
  12.0 4.9 %collective-permute-start.1 = (bf16[64,640]{1,0:T(8,128)(2,1)S(1)}, bf16[64,640]{1,0:T(8,128)(2,1)S(1)}, u32[]{:S(2)}, u32[]{:S(2)}) collective-permute-start(bf16[64,640]{1,0:T(8,128)(2,1)S(1)} %finish.1.refs_0_), channel_id=1, source_target_pairs={{64,0},{66,2},{68,4},{70,6},{72,8},{74,10},{76,12},{78,14},{80,16}... | collective-permute-start | bytes 245768 | tf_op jit(solution)/shard_map/ppermute | solution.py:385
  16.9 4.2 %collective-permute-start.4 = (bf16[128,640]{1,0:T(8,128)(2,1)S(1)}, bf16[128,640]{1,0:T(8,128)(2,1)S(1)}, u32[]{:S(2)}, u32[]{:S(2)}) collective-permute-start(bf16[128,640]{1,0:T(8,128)(2,1)S(1)} %shard_map.113.refs_0_), channel_id=1, source_target_pairs={{48,0},{50,2},{52,4},{54,6},{56,8},{58,10},{60,12},{62,14},{0,16},... | collective-permute-start | bytes 491528 | tf_op jit(solution)/shard_map/ppermute | solution.py:385
  17.0 5.8 %collective-permute-start.3 = (bf16[128,640]{1,0:T(8,128)(2,1)S(1)}, bf16[128,640]{1,0:T(8,128)(2,1)S(1)}, u32[]{:S(2)}, u32[]{:S(2)}) collective-permute-start(bf16[128,640]{1,0:T(8,128)(2,1)S(1)} %shard_map.113.refs_0_), channel_id=1, source_target_pairs={{32,0},{34,2},{36,4},{38,6},{40,8},{42,10},{44,12},{46,14},{48,16}... | collective-permute-start | bytes 491528 | tf_op jit(solution)/shard_map/ppermute | solution.py:385
  18.9 6.3 %collective-permute-start.2 = (bf16[128,640]{1,0:T(8,128)(2,1)S(1)}, bf16[128,640]{1,0:T(8,128)(2,1)S(1)}, u32[]{:S(2)}, u32[]{:S(2)}) collective-permute-start(bf16[128,640]{1,0:T(8,128)(2,1)S(1)} %shard_map.113.refs_0_), channel_id=1, source_target_pairs={{16,0},{18,2},{20,4},{22,6},{24,8},{26,10},{28,12},{30,14},{32,16}... | collective-permute-start | bytes 491528 | tf_op jit(solution)/shard_map/ppermute | solution.py:385
  25.2 15.0 %collective-permute-start.9 = (bf16[512,640]{1,0:T(8,128)(2,1)S(1)}, bf16[512,640]{1,0:T(8,128)(2,1)S(1)}, u32[]{:S(2)}, u32[]{:S(2)}) collective-permute-start(bf16[512,640]{1,0:T(8,128)(2,1)S(1)} %shard_map.114.refs_2_.refs_5_), channel_id=1, source_target_pairs={{12,0},{14,2},{0,4},{2,6},{4,8},{6,10},{8,12},{10,14},{28,16},{30,... | collective-permute-start | bytes 1966088 | tf_op jit(solution)/shard_map/ppermute | solution.py:385
  26.6 20.2 %collective-permute-start.8 = (bf16[512,640]{1,0:T(8,128)(2,1)S(1)}, bf16[512,640]{1,0:T(8,128)(2,1)S(1)}, u32[]{:S(2)}, u32[]{:S(2)}) collective-permute-start(bf16[512,640]{1,0:T(8,128)(2,1)S(1)} %shard_map.114.refs_2_.refs_5_), channel_id=1, source_target_pairs={{4,0},{6,2},{8,4},{10,6},{12,8},{14,10},{0,12},{2,14},{20,16},{22,... | collective-permute-start | bytes 1966088 | tf_op jit(solution)/shard_map/ppermute | solution.py:385
  28.1 29.0 %collective-permute-start.5 = (bf16[512,640]{1,0:T(8,128)(2,1)S(1)}, bf16[512,640]{1,0:T(8,128)(2,1)S(1)}, u32[]{:S(2)}, u32[]{:S(2)}) collective-permute-start(bf16[512,640]{1,0:T(8,128)(2,1)S(1)} %shard_map.114.refs_2_.refs_5_), channel_id=1, source_target_pairs={{8,0},{10,2},{12,4},{14,6},{0,8},{2,10},{4,12},{6,14},{24,16},{26,... | collective-permute-start | bytes 1966088 | tf_op jit(solution)/shard_map/ppermute | solution.py:385
  29.7 29.3 %collective-permute-start.7 = (bf16[512,640]{1,0:T(8,128)(2,1)S(1)}, bf16[512,640]{1,0:T(8,128)(2,1)S(1)}, u32[]{:S(2)}, u32[]{:S(2)}) collective-permute-start(bf16[512,640]{1,0:T(8,128)(2,1)S(1)} %shard_map.114.refs_2_.refs_5_), channel_id=1, source_target_pairs={{2,0},{0,2},{6,4},{4,6},{10,8},{8,10},{14,12},{12,14},{18,16},{16,... | collective-permute-start | bytes 1966088 | tf_op jit(solution)/shard_map/ppermute | solution.py:385
  34.3 3.4 %copy-start = (bf16[64,128,512]{2,1,0:T(8,128)(2,1)S(1)}, bf16[64,128,512]{2,1,0:T(8,128)(2,1)}, u32[]{:S(2)}) copy-start(bf16[64,128,512]{2,1,0:T(8,128)(2,1)} %uk_ref.1) | copy-start | bytes 25165828
  40.3 45.1 %collective-permute-start.11 = (bf16[512,640]{1,0:T(8,128)(2,1)S(1)}, bf16[512,640]{1,0:T(8,128)(2,1)S(1)}, u32[]{:S(2)}, u32[]{:S(2)}) collective-permute-start(bf16[512,640]{1,0:T(8,128)(2,1)S(1)} %collective-permute-done.9.refs_3_.refs_8_), channel_id=1, source_target_pairs={{2,0},{0,2},{6,4},{4,6},{10,8},{8,10},{14,12},{12,14},{18,16},{16,... | collective-permute-start | bytes 1966088 | tf_op jit(solution)/shard_map/ppermute | solution.py:385
  46.7 38.6 %collective-permute-start.10 = (bf16[512,640]{1,0:T(8,128)(2,1)S(1)}, bf16[512,640]{1,0:T(8,128)(2,1)S(1)}, u32[]{:S(2)}, u32[]{:S(2)}) collective-permute-start(bf16[512,640]{1,0:T(8,128)(2,1)S(1)} %collective-permute-done.8.refs_2_.refs_7_), channel_id=1, source_target_pairs={{2,0},{0,2},{6,4},{4,6},{10,8},{8,10},{14,12},{12,14},{18,16},{16,... | collective-permute-start | bytes 1966088 | tf_op jit(solution)/shard_map/ppermute | solution.py:385
  57.1 41.2 %collective-permute-start.6 = (bf16[512,640]{1,0:T(8,128)(2,1)S(1)}, bf16[512,640]{1,0:T(8,128)(2,1)S(1)}, u32[]{:S(2)}, u32[]{:S(2)}) collective-permute-start(bf16[512,640]{1,0:T(8,128)(2,1)S(1)} %collective-permute-done.5.refs_2_), channel_id=1, source_target_pairs={{2,0},{0,2},{6,4},{4,6},{10,8},{8,10},{14,12},{12,14},{18,16},{16,... | collective-permute-start | bytes 1966088 | tf_op jit(solution)/shard_map/ppermute | solution.py:385
  72.5 25.8 %slice-start = ((s8[8388608]{0:T(1024)(128)(4,1)}), s8[4194304]{0:T(1024)(128)(4,1)S(1)}, s32[]{:S(2)}) async-start(s8[8388608]{0:T(1024)(128)(4,1)} %bitcast.4), calls=%async_computation | async-start | bytes 8388608
  85.3 13.0 %slice-start.1 = ((s8[8388608]{0:T(1024)(128)(4,1)}), s8[4194304]{0:T(1024)(128)(4,1)S(1)}, s32[]{:S(2)}) async-start(s8[8388608]{0:T(1024)(128)(4,1)} %bitcast.4), calls=%async_computation.1 | async-start | bytes 8388608

commit v2 on v1

--- a/solution.py
+++ b/solution.py
@@ -28,8 +28,10 @@
 GROUP = 16
 STEP = 256
 PARTS = 7
-ATTEND_MIB = 14
-COPY_STATE = False
+ATTEND_MIB = 10
+WAIT = pl.CostEstimate(flops=5 * 10**9, transcendentals=0, bytes_accessed=1 << 20)
+PLACE, LIST, BEFORE, SCALARS = 0, 64, 136, 208
+SETS = ((0, 0), (0, 1), (1, 0), (3, 0), (1, 1), (3, 1), (2, 0), (2, 1))
 
 
 def params(mib, **kw):
@@ -94,13 +96,13 @@
     )(hidden, attn_gain, kv_down.T)
 
 
-def finish_kernel(scalars, mine_ref, theirs_ref, cos_ref, sin_ref, gain_ref, out_ref):
+def finish_kernel(mine_ref, theirs_ref, cos_ref, sin_ref, gain_ref, out_ref):
     total = mine_ref[...] + theirs_ref[...]
     squares = total[:, WIDTH - 1 :]
     scaled = total * lax.rsqrt(squares / D + EPSILON)
     raw = scaled[:, :LATENT]
     mean = jnp.mean(raw * raw, axis=1, keepdims=True)
-    latent = raw * lax.rsqrt(mean + EPSILON) * gain_ref[...]
+    latent = raw * lax.rsqrt(mean + EPSILON) * gain_ref[...].reshape(1, -1)
     out_ref[:, :LATENT] = latent.astype(jnp.bfloat16)
     key = scaled[:, LATENT:]
     lane = lax.broadcasted_iota(jnp.int32, key.shape, 1)
@@ -109,15 +111,14 @@
     out_ref[:, LATENT:] = turned.astype(jnp.bfloat16)
 
 
-def finish(scalars, mine, theirs, cosines, sines, kv_gain):
+def finish(mine, theirs, cosines, sines, kv_gain):
     return pl.pallas_call(
         finish_kernel,
         out_shape=jax.ShapeDtypeStruct((ROWS, WIDTH), jnp.bfloat16),
-        in_specs=[pl.BlockSpec(memory_space=pltpu.SMEM)]
-        + [pl.BlockSpec(memory_space=pltpu.VMEM)] * 5,
         compiler_params=params(4),
+        cost_estimate=WAIT,
         name="finish",
-    )(scalars, mine, theirs, cosines, sines, kv_gain.reshape(1, -1))
+    )(mine, theirs, cosines, sines, kv_gain)
 
 
 def join_kernel(*refs):
@@ -134,6 +135,41 @@
         out_shape=jax.ShapeDtypeStruct((sum(p.shape[0] for p in parts), WIDTH), jnp.bfloat16),
         compiler_params=params(4),
     )(*parts)
+
+
+def keep_kernel(plan, mine_ref, gain_ref, mine_out, gain_out):
+    mine_out[...] = mine_ref[...]
+    gain_out[...] = gain_ref[...]
+
+
+def keep(plan, mine, gain):
+    return pl.pallas_call(
+        keep_kernel,
+        out_shape=[jax.ShapeDtypeStruct(a.shape, a.dtype) for a in (mine, gain)],
+        in_specs=[pl.BlockSpec(memory_space=pltpu.SMEM)]
+        + [pl.BlockSpec(memory_space=pltpu.VMEM)] * 2,
+        out_specs=[pl.BlockSpec(memory_space=pltpu.VMEM)] * 2,
+        compiler_params=params(4),
+        cost_estimate=WAIT,
+        name="keep",
+    )(plan, mine, gain)
+
+
+def blank_kernel(plan, acc, m, l):
+    acc[...] = jnp.zeros_like(acc)
+    m[...] = jnp.full_like(m, FLOOR)
+    l[...] = jnp.zeros_like(l)
+
+
+def blank(plan, rows):
+    return pl.pallas_call(
+        blank_kernel,
+        out_shape=[jax.ShapeDtypeStruct((rows, w), jnp.float32) for w in (LATENT, 128, 128)],
+        in_specs=[pl.BlockSpec(memory_space=pltpu.SMEM)],
+        out_specs=[pl.BlockSpec(memory_space=pltpu.VMEM)] * 3,
+        compiler_params=params(4),
+        name="blank",
+    )(plan)
 
 
 def queries_kernel(nope_ref, pe_ref, cos_ref, sin_ref, uk_ref, out_ref):
@@ -172,74 +208,93 @@
     )(q_nope, q_pe, cosines, sines, w_uk)
 
 
-def start_of(scalars, position):
+def make_plan(me, starts, held):
+    x, z, y, c = me // 32, (me // 8) & 3, (me // 2) & 3, me & 1
+    index = jnp.arange(64, dtype=jnp.int32)
+    block = (
+        (x ^ (index & 1)) * 32
+        + ((z + (index // 2) % 4) & 3) * 8
+        + ((y + jnp.repeat(jnp.array([s[0] for s in SETS], jnp.int32), 8)) & 3) * 2
+        + (c ^ jnp.repeat(jnp.array([s[1] for s in SETS], jnp.int32), 8))
+    )
+    lowest = jnp.max(jnp.where(starts <= me * ROWS, starts, 0))
+    needed = (block <= me) & (block * ROWS + ROWS - 1 >= lowest)
+    upto = jnp.arange(72, dtype=jnp.int32)
+    before = jnp.sum(jnp.where(index[None, :] < upto[:, None], needed[None, :], False), axis=1, dtype=jnp.int32)
+    place = jnp.where(needed, before[:64], -1)
+    listed = place[None, :] == upto[:, None]
+    blocks = jnp.where(
+        upto < before[64], jnp.sum(jnp.where(listed, block[None, :], 0), axis=1), HEADS * 1024
+    )
+    return jnp.concatenate([place, blocks, before, starts, me[None], held])
+
+
+def plan_of(me, doc_ids, slot_table):
+    starts = jnp.sum(
+        (doc_ids[None, :] < jnp.arange(1, 4, dtype=jnp.int32)[:, None]).astype(jnp.int32), axis=1
+    )
+    slots = me * (ROWS // BLOCK) + jnp.arange(ROWS // BLOCK, dtype=jnp.int32)
+    groups = jnp.arange(slot_table.shape[0], dtype=jnp.int32)
+    held = jnp.sum(jnp.where(slot_table[None, :] == slots[:, None], groups[None, :], 0), axis=1)
+    return make_plan(me, starts, held)
+
+
+def start_of(plan, position):
     start = jnp.int32(0)
     for i in range(3):
-        start = jnp.maximum(start, jnp.where(scalars[i] <= position, scalars[i], 0))
+        first = plan[SCALARS + i]
+        start = jnp.maximum(start, jnp.where(first <= position, first, 0))
     return start
 
 
-def attend_kernel(offsets, first, last, *refs):
-    n = len(offsets)
+def attend_kernel(first_set, n, last, *refs):
     refs = list(refs)
-    scalars = refs.pop(0)
+    plan = refs.pop(0)
     q_ref = refs.pop(0)
     sets = [refs.pop(0) for _ in range(n)]
+    if first_set:
+        left = refs.pop(0)
     if last:
         uv_ref = refs.pop(0)
-        others, refs = refs[:6], refs[6:]
-    if not first:
-        before, refs = refs[:3], refs[3:]
+        others, refs = refs[:first_set], refs[first_set:]
+    refs = refs[3:]
     acc, m, l = refs[:3]
     refs = refs[3:]
     if last:
         out_ref, cache_ref = refs[:2]
         refs = refs[2:]
-    kv, ids, counts, even, odd = refs
-    me = scalars[3]
+    else:
+        left_out = refs.pop(0)
+    kv, even, odd = refs
+    me = plan[SCALARS + 3]
     blocks = STEP // ROWS
     rows = GROUP * ROWS
     groups = q_ref.shape[0] // rows
 
-    x, z, y, c = me // 32, (me // 8) & 3, (me // 2) & 3, me & 1
-    lowest = start_of(scalars, me * ROWS)
-    counts[0] = 0
-    for a, (dy, dc) in enumerate(offsets):
+    def rows_of(block):
+        return pl.ds(pl.multiple_of(block * ROWS, ROWS), ROWS)
+
+    base = plan[BEFORE + 8 * first_set] // blocks * blocks
+    if first_set:
+        for i in range(blocks - 1):
+            kv[i * ROWS : (i + 1) * ROWS, :] = left[i * ROWS : (i + 1) * ROWS, :]
+    for a in range(n):
         for b in range(8):
-            dz, dx = b // 2, b % 2
-            block = (x ^ dx) * 32 + ((z + dz) & 3) * 8 + ((y + dy) & 3) * 2 + (c ^ dc)
-            needed = (block <= me) & (block * ROWS + ROWS - 1 >= lowest)
-
-            @pl.when(needed)
-            def _(a=a, b=b, block=block):
-                at = counts[0]
-                ids[at] = block
-                kv[pl.ds(pl.multiple_of(at * ROWS, ROWS), ROWS), :] = sets[a][
-                    b * ROWS : (b + 1) * ROWS, :
-                ]
-                counts[0] = at + 1
-
-    found = counts[0]
-    for i in range(blocks - 1):
-        ids[found + i] = HEADS * 1024
-        kv[pl.ds(pl.multiple_of((found + i) * ROWS, ROWS), ROWS), :] = jnp.zeros(
-            (ROWS, WIDTH), jnp.bfloat16
-        )
-    steps = (found + blocks - 1) // blocks
-
-    def ready(g, carry):
-        at = pl.ds(pl.multiple_of(g * rows, rows), rows)
-        if first:
-            acc[at, :] = jnp.zeros((rows, LATENT), jnp.float32)
-            m[at, :] = jnp.full((rows, 128), FLOOR, jnp.float32)
-            l[at, :] = jnp.zeros((rows, 128), jnp.float32)
-        else:
-            for new, old in zip((acc, m, l), before):
-                new[at, :] = old[at, :]
-        return carry
-
-    if first or COPY_STATE:
-        lax.fori_loop(0, groups, ready, 0)
+            place = plan[PLACE + (first_set + a) * 8 + b]
+
+            @pl.when(place >= 0)
+            def _(a=a, b=b, place=place):
+                kv[rows_of(place - base), :] = sets[a][b * ROWS : (b + 1) * ROWS, :]
+
+    found = plan[BEFORE + 8 * (first_set + n)] - base
+    if last:
+        steps = (found + blocks - 1) // blocks
+        for i in range(blocks - 1):
+            kv[rows_of(found + i), :] = jnp.zeros((ROWS, WIDTH), jnp.bfloat16)
+    else:
+        steps = found // blocks
+        for i in range(blocks - 1):
+            left_out[i * ROWS : (i + 1) * ROWS, :] = kv[rows_of(steps * blocks + i), :]
 
     def keys_of(j):
         return kv[pl.ds(pl.multiple_of(j * STEP, STEP), STEP), :]
@@ -255,12 +310,13 @@
     def gather(g, j, scores):
         at = pl.ds(pl.multiple_of(g * rows, rows), rows)
         lane = lax.broadcasted_iota(jnp.int32, (ROWS, STEP), 1)
-        key_block = jnp.full((ROWS, STEP), ids[blocks * j], jnp.int32)
+        listed = LIST + base + blocks * j
+        key_block = jnp.full((ROWS, STEP), plan[listed], jnp.int32)
         for i in range(1, blocks):
-            key_block = jnp.where(lane >= i * ROWS, ids[blocks * j + i], key_block)
+            key_block = jnp.where(lane >= i * ROWS, plan[listed + i], key_block)
         key_position = key_block * ROWS + (lane & (ROWS - 1))
         position = me * ROWS + lax.broadcasted_iota(jnp.int32, (ROWS, STEP), 0)
-        allowed = (key_position <= position) & (key_position >= start_of(scalars, position))
+        allowed = (key_position <= position) & (key_position >= start_of(plan, position))
         s = jnp.where(allowed[None], scores[...].reshape(GROUP, ROWS, STEP), MASKED)
         s = s.reshape(rows, STEP)
         m_old = m[at, :]
@@ -298,14 +354,14 @@
         lax.fori_loop(0, steps * (groups // 2), two, (jnp.int32(0), jnp.int32(0)))
 
     if last:
-        where = [(0, 0), (0, 1), (1, 0), (3, 0), (1, 1), (3, 1), (2, 0), (2, 1)]
+        x, z, y, c = me // 32, (me // 8) & 3, (me // 2) & 3, me & 1
         for slot in range(ROWS // BLOCK):
-            group = scalars[4 + slot]
+            group = plan[SCALARS + 4 + slot]
             block = group // 4
             dx, dz = (block // 32) ^ x, ((block // 8) - z) & 3
             dy, dc = ((block // 2) - y) & 3, (block & 1) ^ c
             row = pl.multiple_of((dz * 2 + dx) * ROWS + (group & 3) * BLOCK, BLOCK)
-            for source, (oy, oc) in zip([*others, *sets], where):
+            for source, (oy, oc) in zip([*others, *sets], SETS):
 
                 @pl.when((dy == oy) & (dc == oc))
                 def _(source=source, row=row, slot=slot):
@@ -326,24 +382,23 @@
         lax.fori_loop(0, groups, give, 0)
 
 
-def attend(scalars, queries, sets, offsets, state=None, w_uv=None, others=()):
-    first, last = state is None, w_uv is not None
+def attend(plan, queries, sets, first_set, carried, w_uv=None, others=()):
+    last = w_uv is not None
+    *state, left = carried
     n = len(sets)
     rows = GROUP * ROWS
     total = queries.shape[0]
     widths = (LATENT, 128, 128)
     operands = [queries, *sets]
+    if first_set:
+        operands.append(left)
     if last:
         operands += [w_uv, *others]
-    aliases = {}
-    if not first:
-        aliases = {1 + len(operands) + i: i for i in range(len(widths))}
-        operands += list(state)
-    room = 8 * n + 2 * STEP // ROWS
+    aliases = {1 + len(operands) + i: i for i in range(len(widths))}
+    operands += list(state)
+    room = (8 * n + 2 * STEP // ROWS) * ROWS
     scratch = [
-        pltpu.VMEM((room * ROWS, WIDTH), jnp.bfloat16),
-        pltpu.SMEM((room,), jnp.int32),
-        pltpu.SMEM((4,), jnp.int32),
+        pltpu.VMEM((room, WIDTH), jnp.bfloat16),
         pltpu.VMEM((rows, STEP), jnp.float32),
         pltpu.VMEM((rows, STEP), jnp.float32),
     ]
@@ -354,9 +409,11 @@
             jax.ShapeDtypeStruct((ROWS, total // ROWS * VD), jnp.bfloat16),
             jax.ShapeDtypeStruct((ROWS, LATENT + ROPE), jnp.bfloat16),
         ]
+    else:
+        out_shape.append(jax.ShapeDtypeStruct((STEP - ROWS, WIDTH), jnp.bfloat16))
     flops = 2 * total * 8 * n * ROWS * (WIDTH + LATENT)
     out = pl.pallas_call(
-        functools.partial(attend_kernel, offsets, first, last),
+        functools.partial(attend_kernel, first_set, n, last),
         out_shape=out_shape,
         in_specs=[pl.BlockSpec(memory_space=pltpu.SMEM)] + [whole] * len(operands),
         out_specs=[whole] * len(out_shape),
@@ -366,7 +423,7 @@
         cost_estimate=pl.CostEstimate(
             flops=flops, transcendentals=total * 8 * n * ROWS, bytes_accessed=24 << 20
         ),
-    )(scalars, *operands)
+    )(plan, *operands)
     return out[3:] if last else out
 
 
@@ -386,7 +443,7 @@
 
 
 def local(hidden, attn_gain, kv_down, kv_gain, q_nope, q_pe, w_uk, w_uv, doc_ids, slot_table):
-    me = lax.axis_index("seq")
+    me = lax.axis_index("seq").astype(jnp.int32)
     positions = (me * ROWS + jnp.arange(ROWS, dtype=jnp.int32)).astype(jnp.float32)
     half = ROPE // 2
     frequency = jnp.exp(jnp.arange(half, dtype=jnp.float32) * (-2.0 * math.log(10000.0) / ROPE))
@@ -394,18 +451,14 @@
     sign = jnp.where((jnp.arange(128) & 63) < half, -1.0, 1.0).astype(jnp.float32)
     cosines, sines = jnp.cos(angle), jnp.sin(angle) * sign[None, :]
 
-    starts = jnp.sum(
-        (doc_ids[None, :] < jnp.arange(1, 4, dtype=jnp.int32)[:, None]).astype(jnp.int32), axis=1
-    )
-    slots = me * (ROWS // BLOCK) + jnp.arange(ROWS // BLOCK, dtype=jnp.int32)
-    groups = jnp.arange(slot_table.shape[0], dtype=jnp.int32)
-    held = jnp.sum(jnp.where(slot_table[None, :] == slots[:, None], groups[None, :], 0), axis=1)
-    scalars = jnp.concatenate([starts, me[None].astype(jnp.int32), held])
+    plan = plan_of(me, doc_ids, slot_table)
 
     mine = project(hidden, attn_gain, kv_down)
     theirs = lax.ppermute(mine, "tensor", [(0, 1), (1, 0)])
     queries = make_queries(q_nope, q_pe, cosines, sines, w_uk)
-    own = finish(scalars, mine, theirs, cosines, sines, kv_gain)
+    mine, kv_gain = keep(plan, mine, kv_gain)
+    own = finish(mine, theirs, cosines, sines, kv_gain)
+    state = blank(plan, queries.shape[0])
 
     two = join([own, fetch(own, dx=1)])
     eight = join([two] + [fetch(two, dz=d) for d in (1, 2, 3)])
@@ -414,17 +467,12 @@
         across[d] = fetch(eight, dy=d)
     beside = {d: fetch(across[d], dc=1) for d in (0, 1, 3, 2)}
 
-    state = attend(scalars, queries, [across[0], beside[0]], [(0, 0), (0, 1)])
-    state = attend(scalars, queries, [across[1], across[3]], [(1, 0), (3, 0)], state)
-    state = attend(scalars, queries, [beside[1], beside[3]], [(1, 1), (3, 1)], state)
+    sets = [beside[dy] if dc else across[dy] for dy, dc in SETS]
+    state = (*state, None)
+    for at, n in ((0, 1), (1, 1), (2, 2), (4, 2), (6, 1)):
+        state = attend(plan, queries, sets[at : at + n], at, state)
     attn_values, latent_cache = attend(
-        scalars,
-        queries,
-        [across[2], beside[2]],
-        [(2, 0), (2, 1)],
-        state,
-        w_uv,
-        [across[0], beside[0], across[1], across[3], beside[1], beside[3]],
+        plan, queries, sets[7:], 7, state, w_uv, sets[:7]
     )
     return attn_values, latent_cache
 

time: 117 us -> 111 us (0.949)
  starting transfers between devices: 31.5 us -> 28.3 us
  waiting for transfers between devices: 13.9 us -> 10.8 us
  local copies, waits for them, and re-layouts: 4.42 us -> 2.11 us
  other arithmetic: 0.7 us -> 2.8 us
    ppermute x1, waiting for transfers between devices: 3.9 us -> 0.01 us  [local(): theirs = lax.ppermute(mine, 'tensor', [(0, 1), (1, 0)])]
    unnamed x18 -> x24, local copies, waits for them, and re-layouts: 4.33 us -> 0.98 us
    ppermute x11, starting transfers between devices: 30.9 us -> 27.7 us  [fetch(): return lax.ppermute(array, 'seq', pairs)]
    pallas_call x4 -> x8, Pallas kernels: 55.6 us -> 56.4 us  [the longest x6 54.5 us: attend(): pl.pallas_call(functools.partial(attend_kernel, first_set, n, last), out_...]
  transfers between devices with their start and end apart: 12 -> 12, of which waited for: 5 -> 4; matrix products, arithmetic and copies ran while one was open for 1% -> 4% of each run, Pallas kernels for 37% -> 43%
where the time goes in v2:
time: 111 us; the launch traced here: 108 us
  Pallas kernels  63.4 us (57%)
  starting transfers between devices  28.3 us (25%)
  waiting for transfers between devices  10.8 us (10%)
  other arithmetic  2.8 us (3%)
  local copies, waits for them, and re-layouts  2.11 us (2%)
    pallas_call x6, Pallas kernels, attend(): pl.pallas_call(functools.partial(attend_kernel, first_set, n, last), out_...  54.5 us
    ppermute x11, starting transfers between devices, fetch(): return lax.ppermute(array, 'seq', pairs)  27.7 us
    ppermute x11, waiting for transfers between devices, fetch(): return lax.ppermute(array, 'seq', pairs)  10.8 us
    pallas_call x1, Pallas kernels, project(): pl.pallas_call(project_kernel, out_shape=jax.ShapeDtypeStruct((ROWS, WIDT...  4.15 us
    pallas_call x1, Pallas kernels, make_queries(): pl.pallas_call(queries_kernel, out_shape=jax.ShapeDtypeStruct((heads * RO...  2.59 us
  transfers between devices with their start and end apart: 12, of which 4 were waited for; matrix products, arithmetic and copies ran while one was open for 4% of the time, Pallas kernels for 43%

profile of v2, /device:TPU:103, one launch (start us, length us, event | category | flops | bytes accessed | tf_op | source)
XLA Modules:
  0.0 108.5 jit_solution(9749586854294260173)
XLA Ops:
  0.7 4.1 %project.1.mine_ref = f32[64,640]{1,0:T(8,128)} custom-call(bf16[64,3584]{1,0:T(8,128)(2,1)} %hidden_hbm.1, f32[3584]{0:T(1024)} %gain_hbm.1, bf16[576,3584]{1,0:T(8,128)(2,1)} %bitcast.7), custom_call_target="tpu_custom_call" | custom-call | tf_op jit(solution)/shard_map/project/pallas_call | solution.py:83
  4.8 0.6 collective-permute-start
  5.5 0.2 convert_reduce_fusion
  5.8 0.7 fusion.8
  6.8 0.6 compare_and_fusion
  7.5 0.7 slice.7
  8.6 0.6 compare_select_fusion.4
  9.3 0.9 copy-done.2
  10.2 0.6 keep.1
  10.8 0.2 fusion
  11.0 0.2 finish.1.refs_0_
  11.3 0.9 collective-permute-start.1
  12.2 4.0 %collective-permute-done.1.refs_1_ = bf16[64,640]{1,0:T(8,128)(2,1)S(1)} collective-permute-done((bf16[64,640]{1,0:T(8,128)(2,1)S(1)}, bf16[64,640]{1,0:T(8,128)(2,1)S(1)}, u32[]{:S(2)}, u32[]{:S(2)}) %collective-permute-start.1) | collective-permute-done | bytes 81952 | tf_op jit(solution)/shard_map/ppermute | solution.py:442
  16.2 1.9 %collective-permute-start.3 = (bf16[128,640]{1,0:T(8,128)(2,1)S(1)}, bf16[128,640]{1,0:T(8,128)(2,1)S(1)}, u32[]{:S(2)}, u32[]{:S(2)}) collective-permute-start(bf16[128,640]{1,0:T(8,128)(2,1)S(1)} %shard_map.131.refs_0_), channel_id=1, source_target_pairs={{32,0},{34,2},{36,4},{38,6},{40,8},{42,10},{44,12},{46,14},{48,16}... | collective-permute-start | bytes 491528 | tf_op jit(solution)/shard_map/ppermute | solution.py:442
  18.1 2.3 %collective-permute-done.4.refs_3_ = bf16[128,640]{1,0:T(8,128)(2,1)S(1)} collective-permute-done((bf16[128,640]{1,0:T(8,128)(2,1)S(1)}, bf16[128,640]{1,0:T(8,128)(2,1)S(1)}, u32[]{:S(2)}, u32[]{:S(2)}) %collective-permute-start.4) | collective-permute-done | bytes 163872 | tf_op jit(solution)/shard_map/ppermute | solution.py:442
  20.4 1.6 %collective-permute-done.3.refs_2_ = bf16[128,640]{1,0:T(8,128)(2,1)S(1)} collective-permute-done((bf16[128,640]{1,0:T(8,128)(2,1)S(1)}, bf16[128,640]{1,0:T(8,128)(2,1)S(1)}, u32[]{:S(2)}, u32[]{:S(2)}) %collective-permute-start.3) | collective-permute-done | bytes 163872 | tf_op jit(solution)/shard_map/ppermute | solution.py:442
  22.0 3.0 %collective-permute-done.2.refs_1_ = bf16[128,640]{1,0:T(8,128)(2,1)S(1)} collective-permute-done((bf16[128,640]{1,0:T(8,128)(2,1)S(1)}, bf16[128,640]{1,0:T(8,128)(2,1)S(1)}, u32[]{:S(2)}, u32[]{:S(2)}) %collective-permute-start.2) | collective-permute-done | bytes 163872 | tf_op jit(solution)/shard_map/ppermute | solution.py:442
  25.0 1.4 %collective-permute-start.9 = (bf16[512,640]{1,0:T(8,128)(2,1)S(1)}, bf16[512,640]{1,0:T(8,128)(2,1)S(1)}, u32[]{:S(2)}, u32[]{:S(2)}) collective-permute-start(bf16[512,640]{1,0:T(8,128)(2,1)S(1)} %shard_map.132.refs_2_.refs_5_), channel_id=1, source_target_pairs={{12,0},{14,2},{0,4},{2,6},{4,8},{6,10},{8,12},{10,14},{28,16},{30,... | collective-permute-start | bytes 1966088 | tf_op jit(solution)/shard_map/ppermute | solution.py:442
  26.4 1.5 %collective-permute-start.7 = (bf16[512,640]{1,0:T(8,128)(2,1)S(1)}, bf16[512,640]{1,0:T(8,128)(2,1)S(1)}, u32[]{:S(2)}, u32[]{:S(2)}) collective-permute-start(bf16[512,640]{1,0:T(8,128)(2,1)S(1)} %shard_map.132.refs_2_.refs_5_), channel_id=1, source_target_pairs={{4,0},{6,2},{8,4},{10,6},{12,8},{14,10},{0,12},{2,14},{20,16},{22,... | collective-permute-start | bytes 1966088 | tf_op jit(solution)/shard_map/ppermute | solution.py:442
  27.9 1.6 %collective-permute-start.5 = (bf16[512,640]{1,0:T(8,128)(2,1)S(1)}, bf16[512,640]{1,0:T(8,128)(2,1)S(1)}, u32[]{:S(2)}, u32[]{:S(2)}) collective-permute-start(bf16[512,640]{1,0:T(8,128)(2,1)S(1)} %shard_map.132.refs_2_.refs_5_), channel_id=1, source_target_pairs={{8,0},{10,2},{12,4},{14,6},{0,8},{2,10},{4,12},{6,14},{24,16},{26,... | collective-permute-start | bytes 1966088 | tf_op jit(solution)/shard_map/ppermute | solution.py:442
  29.5 3.9 %collective-permute-start.11 = (bf16[512,640]{1,0:T(8,128)(2,1)S(1)}, bf16[512,640]{1,0:T(8,128)(2,1)S(1)}, u32[]{:S(2)}, u32[]{:S(2)}) collective-permute-start(bf16[512,640]{1,0:T(8,128)(2,1)S(1)} %shard_map.132.refs_2_.refs_5_), channel_id=1, source_target_pairs={{2,0},{0,2},{6,4},{4,6},{10,8},{8,10},{14,12},{12,14},{18,16},{16,... | collective-permute-start | bytes 1966088 | tf_op jit(solution)/shard_map/ppermute | solution.py:442
  33.4 1.4 %blank.1 = (f32[4096,512]{1,0:T(8,128)S(1)}, f32[4096,128]{1,0:T(8,128)S(1)}, f32[4096,128]{1,0:T(8,128)S(1)}) custom-call(s32[216]{0:T(256)S(1)} %concatenate.3.plan.refs_0_), custom_call_target="tpu_custom_call" | custom-call | tf_op jit(solution)/shard_map/blank/pallas_call | solution.py:165
  34.8 2.6 %queries.1.refs_1_ = bf16[4096,640]{1,0:T(8,128)(2,1)S(1)} custom-call(bf16[64,8192]{1,0:T(8,128)(2,1)S(1)} %copy-done, bf16[64,4096]{1,0:T(8,128)(2,1)S(1)} %copy-done.1, f32[64,128]{1,0:T(8,128)S(1)} %get-tuple-element.59.cos_ref, f32[64,128]{1,0:T(8,128)S(1)} %get-tuple-element.58.sin_ref, bf16[64,128,512]{2,1,0:T(8,128)(2,1)S(1)} %bitcast.6), custom_call_target="tpu_custom_call" | custom-call | tf_op jit(solution)/shard_map/queries/pallas_call | solution.py:194
  37.4 4.9 %shard_map.133 = (f32[4096,512]{1,0:T(8,128)S(1)}, f32[4096,128]{1,0:T(8,128)S(1)}, f32[4096,128]{1,0:T(8,128)S(1)}, bf16[192,640]{1,0:T(8,128)(2,1)S(1)}) custom-call(s32[216]{0:T(256)S(1)} %concatenate.3.plan.refs_0_, bf16[4096,640]{1,0:T(8,128)(2,1)S(1)} %queries.1.refs_1_, ...), custom_call_target="tpu_custom_call", output_to_operand_aliasing={{0}: (3, {}), {1}: (4, {}), {2}: (5, {})} | custom-call | flops 4831838208 | bytes 25165824 | tf_op jit(solution)/shard_map/pallas_call | solution.py:415
  42.3 3.6 %collective-permute-start.10 = (bf16[512,640]{1,0:T(8,128)(2,1)S(1)}, bf16[512,640]{1,0:T(8,128)(2,1)S(1)}, u32[]{:S(2)}, u32[]{:S(2)}) collective-permute-start(bf16[512,640]{1,0:T(8,128)(2,1)S(1)} %collective-permute-done.9.refs_3_.refs_8_), channel_id=1, source_target_pairs={{2,0},{0,2},{6,4},{4,6},{10,8},{8,10},{14,12},{12,14},{18,16},{16,... | collective-permute-start | bytes 1966088 | tf_op jit(solution)/shard_map/ppermute | solution.py:442
  45.9 11.1 %collective-permute-start.8 = (bf16[512,640]{1,0:T(8,128)(2,1)S(1)}, bf16[512,640]{1,0:T(8,128)(2,1)S(1)}, u32[]{:S(2)}, u32[]{:S(2)}) collective-permute-start(bf16[512,640]{1,0:T(8,128)(2,1)S(1)} %collective-permute-done.7.refs_2_.refs_7_), channel_id=1, source_target_pairs={{2,0},{0,2},{6,4},{4,6},{10,8},{8,10},{14,12},{12,14},{18,16},{16,... | collective-permute-start | bytes 1966088 | tf_op jit(solution)/shard_map/ppermute | solution.py:442
  57.0 1.8 %collective-permute-start.6 = (bf16[512,640]{1,0:T(8,128)(2,1)S(1)}, bf16[512,640]{1,0:T(8,128)(2,1)S(1)}, u32[]{:S(2)}, u32[]{:S(2)}) collective-permute-start(bf16[512,640]{1,0:T(8,128)(2,1)S(1)} %collective-permute-done.5.refs_2_.refs_11_), channel_id=1, source_target_pairs={{2,0},{0,2},{6,4},{4,6},{10,8},{8,10},{14,12},{12,14},{18,16},{16,... | collective-permute-start | bytes 1966088 | tf_op jit(solution)/shard_map/ppermute | solution.py:442
  58.8 8.4 %shard_map.134 = (f32[4096,512]{1,0:T(8,128)S(1)}, f32[4096,128]{1,0:T(8,128)S(1)}, f32[4096,128]{1,0:T(8,128)S(1)}, bf16[192,640]{1,0:T(8,128)(2,1)S(1)}) custom-call(s32[216]{0:T(256)S(1)} %concatenate.3.plan.refs_0_, bf16[4096,640]{1,0:T(8,128)(2,1)S(1)} %queries.1.refs_1_, ...), custom_call_target="tpu_custom_call", output_to_operand_aliasing={{0}: (4, {}), {1}: (5, {}), {2}: (6, {})} | custom-call | flops 4831838208 | bytes 25165824 | tf_op jit(solution)/shard_map/pallas_call | solution.py:415
  67.2 8.7 %shard_map.135 = (f32[4096,512]{1,0:T(8,128)S(1)}, f32[4096,128]{1,0:T(8,128)S(1)}, f32[4096,128]{1,0:T(8,128)S(1)}, bf16[192,640]{1,0:T(8,128)(2,1)S(1)}) custom-call(s32[216]{0:T(256)S(1)} %concatenate.3.plan.refs_0_, bf16[4096,640]{1,0:T(8,128)(2,1)S(1)} %queries.1.refs_1_, ...), custom_call_target="tpu_custom_call", output_to_operand_aliasing={{0}: (5, {}), {1}: (6, {}), {2}: (7, {})} | custom-call | flops 9663676416 | bytes 25165824 | tf_op jit(solution)/shard_map/pallas_call | solution.py:415
  76.0 12.1 %shard_map.136 = (f32[4096,512]{1,0:T(8,128)S(1)}, f32[4096,128]{1,0:T(8,128)S(1)}, f32[4096,128]{1,0:T(8,128)S(1)}, bf16[192,640]{1,0:T(8,128)(2,1)S(1)}) custom-call(s32[216]{0:T(256)S(1)} %concatenate.3.plan.refs_0_, bf16[4096,640]{1,0:T(8,128)(2,1)S(1)} %queries.1.refs_1_, ...), custom_call_target="tpu_custom_call", output_to_operand_aliasing={{0}: (5, {}), {1}: (6, {}), {2}: (7, {})} | custom-call | flops 9663676416 | bytes 25165824 | tf_op jit(solution)/shard_map/pallas_call | solution.py:415
  88.1 8.4 %shard_map.137 = (f32[4096,512]{1,0:T(8,128)S(1)}, f32[4096,128]{1,0:T(8,128)S(1)}, f32[4096,128]{1,0:T(8,128)S(1)}, bf16[192,640]{1,0:T(8,128)(2,1)S(1)}) custom-call(s32[216]{0:T(256)S(1)} %concatenate.3.plan.refs_0_, bf16[4096,640]{1,0:T(8,128)(2,1)S(1)} %queries.1.refs_1_, ...), custom_call_target="tpu_custom_call", output_to_operand_aliasing={{0}: (4, {}), {1}: (5, {}), {2}: (6, {})} | custom-call | flops 4831838208 | bytes 25165824 | tf_op jit(solution)/shard_map/pallas_call | solution.py:415
  96.6 11.9 %shard_map.138 = (f32[4096,512]{1,0:T(8,128)S(1)}, f32[4096,128]{1,0:T(8,128)S(1)}, f32[4096,128]{1,0:T(8,128)S(1)}, bf16[64,8192]{1,0:T(8,128)(2,1)}, bf16[64,576]{1,0:T(8,128)(2,1)}) custom-call(s32[216]{0:T(256)S(1)} %concatenate.3.plan.refs_0_, ...), custom_call_target="tpu_custom_call", output_to_operand_aliasing={{0}: (12, {}), {1}: (13, {}), {2}: (14, {})} | custom-call | flops 4831838208 | bytes 25165824 | tf_op jit(solution)/shard_map/pallas_call | solution.py:415
  (55 shorter events, 1.1 us)
Async XLA Ops:
  0.6 4.9 %copy-start.4 = (s32[4096]{0:T(1024)S(1)}, s32[4096]{0:T(1024)}, u32[]{:S(2)}) copy-start(s32[4096]{0:T(1024)} %param.20) | copy-start | bytes 49156
  0.6 5.8 %copy-start.7 = (s32[8]{0:T(128)S(1)}, s32[8]{0:T(128)}, u32[]{:S(2)}) copy-start(s32[8]{0:T(128)} %constant.110.clone) | copy-start | bytes 100
  0.7 6.0 %copy-start.6 = (s32[8]{0:T(128)S(1)}, s32[8]{0:T(128)}, u32[]{:S(2)}) copy-start(s32[8]{0:T(128)} %constant.111.clone) | copy-start | bytes 100
  0.7 7.6 %copy-start.5 = (s32[256]{0:T(256)S(1)}, s32[256]{0:T(256)}, u32[]{:S(2)}) copy-start(s32[256]{0:T(256)} %param.21) | copy-start | bytes 3076
  0.7 8.6 %copy-start.3 = (f32[512]{0:T(512)S(1)}, f32[512]{0:T(512)}, u32[]{:S(2)}) copy-start(f32[512]{0:T(512)} %gain_ref.1) | copy-start | bytes 6148
  4.8 6.1 %collective-permute-start = (f32[64,640]{1,0:T(8,128)}, f32[64,640]{1,0:T(8,128)S(1)}, u32[]{:S(2)}, u32[]{:S(2)}) collective-permute-start(f32[64,640]{1,0:T(8,128)} %project.1.mine_ref), channel_id=1, source_target_pairs={{0,1},{1,0},{2,3},{3,2},{4,5},{5,4},{6,7},{7,6},{8,9},{9,8},{10,11... | collective-permute-start | bytes 491528 | tf_op jit(solution)/shard_map/ppermute | solution.py:457
  9.3 0.9 copy-start.2
  11.0 23.8 %slice-start.2 = ((s8[8388608]{0:T(1024)(128)(4,1)}), s8[4194304]{0:T(1024)(128)(4,1)S(1)}, s32[]{:S(2)}) async-start(s8[8388608]{0:T(1024)(128)(4,1)} %bitcast.5), calls=%async_computation.2 | async-start | bytes 8388608
  11.0 23.8 %slice-start.3 = ((s8[8388608]{0:T(1024)(128)(4,1)}), s8[4194304]{0:T(1024)(128)(4,1)S(1)}, s32[]{:S(2)}) async-start(s8[8388608]{0:T(1024)(128)(4,1)} %bitcast.5), calls=%async_computation.3 | async-start | bytes 8388608
  11.0 23.8 %copy-start.1 = (bf16[64,4096]{1,0:T(8,128)(2,1)S(1)}, bf16[64,4096]{1,0:T(8,128)(2,1)}, u32[]{:S(2)}) copy-start(bf16[64,4096]{1,0:T(8,128)(2,1)} %pe_ref.1) | copy-start | bytes 1572868
  11.3 23.5 %copy-start = (bf16[64,8192]{1,0:T(8,128)(2,1)S(1)}, bf16[64,8192]{1,0:T(8,128)(2,1)}, u32[]{:S(2)}) copy-start(bf16[64,8192]{1,0:T(8,128)(2,1)} %nope_ref.1) | copy-start | bytes 3145732
  11.3 4.9 %collective-permute-start.1 = (bf16[64,640]{1,0:T(8,128)(2,1)S(1)}, bf16[64,640]{1,0:T(8,128)(2,1)S(1)}, u32[]{:S(2)}, u32[]{:S(2)}) collective-permute-start(bf16[64,640]{1,0:T(8,128)(2,1)S(1)} %finish.1.refs_0_), channel_id=1, source_target_pairs={{64,0},{66,2},{68,4},{70,6},{72,8},{74,10},{76,12},{78,14},{80,16}... | collective-permute-start | bytes 245768 | tf_op jit(solution)/shard_map/ppermute | solution.py:442
  16.2 4.2 %collective-permute-start.4 = (bf16[128,640]{1,0:T(8,128)(2,1)S(1)}, bf16[128,640]{1,0:T(8,128)(2,1)S(1)}, u32[]{:S(2)}, u32[]{:S(2)}) collective-permute-start(bf16[128,640]{1,0:T(8,128)(2,1)S(1)} %shard_map.131.refs_0_), channel_id=1, source_target_pairs={{48,0},{50,2},{52,4},{54,6},{56,8},{58,10},{60,12},{62,14},{0,16},... | collective-permute-start | bytes 491528 | tf_op jit(solution)/shard_map/ppermute | solution.py:442
  16.2 5.8 %collective-permute-start.3 = (bf16[128,640]{1,0:T(8,128)(2,1)S(1)}, bf16[128,640]{1,0:T(8,128)(2,1)S(1)}, u32[]{:S(2)}, u32[]{:S(2)}) collective-permute-start(bf16[128,640]{1,0:T(8,128)(2,1)S(1)} %shard_map.131.refs_0_), channel_id=1, source_target_pairs={{32,0},{34,2},{36,4},{38,6},{40,8},{42,10},{44,12},{46,14},{48,16}... | collective-permute-start | bytes 491528 | tf_op jit(solution)/shard_map/ppermute | solution.py:442
  18.1 6.8 %collective-permute-start.2 = (bf16[128,640]{1,0:T(8,128)(2,1)S(1)}, bf16[128,640]{1,0:T(8,128)(2,1)S(1)}, u32[]{:S(2)}, u32[]{:S(2)}) collective-permute-start(bf16[128,640]{1,0:T(8,128)(2,1)S(1)} %shard_map.131.refs_0_), channel_id=1, source_target_pairs={{16,0},{18,2},{20,4},{22,6},{24,8},{26,10},{28,12},{30,14},{32,16}... | collective-permute-start | bytes 491528 | tf_op jit(solution)/shard_map/ppermute | solution.py:442
  25.0 17.2 %collective-permute-start.9 = (bf16[512,640]{1,0:T(8,128)(2,1)S(1)}, bf16[512,640]{1,0:T(8,128)(2,1)S(1)}, u32[]{:S(2)}, u32[]{:S(2)}) collective-permute-start(bf16[512,640]{1,0:T(8,128)(2,1)S(1)} %shard_map.132.refs_2_.refs_5_), channel_id=1, source_target_pairs={{12,0},{14,2},{0,4},{2,6},{4,8},{6,10},{8,12},{10,14},{28,16},{30,... | collective-permute-start | bytes 1966088 | tf_op jit(solution)/shard_map/ppermute | solution.py:442
  26.4 19.5 %collective-permute-start.7 = (bf16[512,640]{1,0:T(8,128)(2,1)S(1)}, bf16[512,640]{1,0:T(8,128)(2,1)S(1)}, u32[]{:S(2)}, u32[]{:S(2)}) collective-permute-start(bf16[512,640]{1,0:T(8,128)(2,1)S(1)} %shard_map.132.refs_2_.refs_5_), channel_id=1, source_target_pairs={{4,0},{6,2},{8,4},{10,6},{12,8},{14,10},{0,12},{2,14},{20,16},{22,... | collective-permute-start | bytes 1966088 | tf_op jit(solution)/shard_map/ppermute | solution.py:442
  27.9 29.0 %collective-permute-start.5 = (bf16[512,640]{1,0:T(8,128)(2,1)S(1)}, bf16[512,640]{1,0:T(8,128)(2,1)S(1)}, u32[]{:S(2)}, u32[]{:S(2)}) collective-permute-start(bf16[512,640]{1,0:T(8,128)(2,1)S(1)} %shard_map.132.refs_2_.refs_5_), channel_id=1, source_target_pairs={{8,0},{10,2},{12,4},{14,6},{0,8},{2,10},{4,12},{6,14},{24,16},{26,... | collective-permute-start | bytes 1966088 | tf_op jit(solution)/shard_map/ppermute | solution.py:442
  29.5 29.3 %collective-permute-start.11 = (bf16[512,640]{1,0:T(8,128)(2,1)S(1)}, bf16[512,640]{1,0:T(8,128)(2,1)S(1)}, u32[]{:S(2)}, u32[]{:S(2)}) collective-permute-start(bf16[512,640]{1,0:T(8,128)(2,1)S(1)} %shard_map.132.refs_2_.refs_5_), channel_id=1, source_target_pairs={{2,0},{0,2},{6,4},{4,6},{10,8},{8,10},{14,12},{12,14},{18,16},{16,... | collective-permute-start | bytes 1966088 | tf_op jit(solution)/shard_map/ppermute | solution.py:442
  42.3 33.7 %collective-permute-start.10 = (bf16[512,640]{1,0:T(8,128)(2,1)S(1)}, bf16[512,640]{1,0:T(8,128)(2,1)S(1)}, u32[]{:S(2)}, u32[]{:S(2)}) collective-permute-start(bf16[512,640]{1,0:T(8,128)(2,1)S(1)} %collective-permute-done.9.refs_3_.refs_8_), channel_id=1, source_target_pairs={{2,0},{0,2},{6,4},{4,6},{10,8},{8,10},{14,12},{12,14},{18,16},{16,... | collective-permute-start | bytes 1966088 | tf_op jit(solution)/shard_map/ppermute | solution.py:442
  45.9 30.1 %collective-permute-start.8 = (bf16[512,640]{1,0:T(8,128)(2,1)S(1)}, bf16[512,640]{1,0:T(8,128)(2,1)S(1)}, u32[]{:S(2)}, u32[]{:S(2)}) collective-permute-start(bf16[512,640]{1,0:T(8,128)(2,1)S(1)} %collective-permute-done.7.refs_2_.refs_7_), channel_id=1, source_target_pairs={{2,0},{0,2},{6,4},{4,6},{10,8},{8,10},{14,12},{12,14},{18,16},{16,... | collective-permute-start | bytes 1966088 | tf_op jit(solution)/shard_map/ppermute | solution.py:442
  57.0 39.6 %collective-permute-start.6 = (bf16[512,640]{1,0:T(8,128)(2,1)S(1)}, bf16[512,640]{1,0:T(8,128)(2,1)S(1)}, u32[]{:S(2)}, u32[]{:S(2)}) collective-permute-start(bf16[512,640]{1,0:T(8,128)(2,1)S(1)} %collective-permute-done.5.refs_2_.refs_11_), channel_id=1, source_target_pairs={{2,0},{0,2},{6,4},{4,6},{10,8},{8,10},{14,12},{12,14},{18,16},{16,... | collective-permute-start | bytes 1966088 | tf_op jit(solution)/shard_map/ppermute | solution.py:442
  88.1 8.5 %slice-start = ((s8[8388608]{0:T(1024)(128)(4,1)}), s8[4194304]{0:T(1024)(128)(4,1)S(1)}, s32[]{:S(2)}) async-start(s8[8388608]{0:T(1024)(128)(4,1)} %bitcast.3), calls=%async_computation | async-start | bytes 8388608
  88.1 8.5 %slice-start.1 = ((s8[8388608]{0:T(1024)(128)(4,1)}), s8[4194304]{0:T(1024)(128)(4,1)S(1)}, s32[]{:S(2)}) async-start(s8[8388608]{0:T(1024)(128)(4,1)} %bitcast.3), calls=%async_computation.1 | async-start | bytes 8388608

commit v3 on v2

--- a/solution.py
+++ b/solution.py
@@ -30,7 +30,7 @@
 PARTS = 7
 ATTEND_MIB = 10
 WAIT = pl.CostEstimate(flops=5 * 10**9, transcendentals=0, bytes_accessed=1 << 20)
-PLACE, LIST, BEFORE, SCALARS = 0, 64, 136, 208
+PLACE, LIST, DONE, SCALARS, LEFT = 0, 64, 136, 208, 7
 SETS = ((0, 0), (0, 1), (1, 0), (3, 0), (1, 1), (3, 1), (2, 0), (2, 1))
 
 
@@ -137,22 +137,21 @@
     )(*parts)
 
 
-def keep_kernel(plan, mine_ref, gain_ref, mine_out, gain_out):
+def keep_kernel(mine_ref, gain_ref, mine_out, gain_out):
     mine_out[...] = mine_ref[...]
     gain_out[...] = gain_ref[...]
 
 
-def keep(plan, mine, gain):
+def keep(mine, gain):
     return pl.pallas_call(
         keep_kernel,
         out_shape=[jax.ShapeDtypeStruct(a.shape, a.dtype) for a in (mine, gain)],
-        in_specs=[pl.BlockSpec(memory_space=pltpu.SMEM)]
-        + [pl.BlockSpec(memory_space=pltpu.VMEM)] * 2,
+        in_specs=[pl.BlockSpec(memory_space=pltpu.VMEM)] * 2,
         out_specs=[pl.BlockSpec(memory_space=pltpu.VMEM)] * 2,
         compiler_params=params(4),
         cost_estimate=WAIT,
         name="keep",
-    )(plan, mine, gain)
+    )(mine, gain)
 
 
 def blank_kernel(plan, acc, m, l):
@@ -208,35 +207,56 @@
     )(q_nope, q_pe, cosines, sines, w_uk)
 
 
-def make_plan(me, starts, held):
+def plan_kernel(me_ref, docs_ref, slots_ref, plan):
+    me = me_ref[0]
+
+    def count(mask, values):
+        return jnp.sum(jnp.where(mask, values, 0.0), axis=1, keepdims=True)[0, 0].astype(jnp.int32)
+
+    docs = docs_ref[...].reshape(1, -1)
+    slots = slots_ref[...].reshape(1, -1)
+    numbers = lax.broadcasted_iota(jnp.int32, slots.shape, 1).astype(jnp.float32)
+    for i in range(3):
+        plan[SCALARS + i] = count(docs <= i, jnp.ones(docs.shape, jnp.float32))
+    plan[SCALARS + 3] = me
+    for i in range(ROWS // BLOCK):
+        plan[SCALARS + 4 + i] = count(slots == me * (ROWS // BLOCK) + i, numbers)
+    for i in range(72):
+        plan[LIST + i] = HEADS * 1024
     x, z, y, c = me // 32, (me // 8) & 3, (me // 2) & 3, me & 1
-    index = jnp.arange(64, dtype=jnp.int32)
-    block = (
-        (x ^ (index & 1)) * 32
-        + ((z + (index // 2) % 4) & 3) * 8
-        + ((y + jnp.repeat(jnp.array([s[0] for s in SETS], jnp.int32), 8)) & 3) * 2
-        + (c ^ jnp.repeat(jnp.array([s[1] for s in SETS], jnp.int32), 8))
-    )
-    lowest = jnp.max(jnp.where(starts <= me * ROWS, starts, 0))
-    needed = (block <= me) & (block * ROWS + ROWS - 1 >= lowest)
-    upto = jnp.arange(72, dtype=jnp.int32)
-    before = jnp.sum(jnp.where(index[None, :] < upto[:, None], needed[None, :], False), axis=1, dtype=jnp.int32)
-    place = jnp.where(needed, before[:64], -1)
-    listed = place[None, :] == upto[:, None]
-    blocks = jnp.where(
-        upto < before[64], jnp.sum(jnp.where(listed, block[None, :], 0), axis=1), HEADS * 1024
-    )
-    return jnp.concatenate([place, blocks, before, starts, me[None], held])
-
-
-def plan_of(me, doc_ids, slot_table):
-    starts = jnp.sum(
-        (doc_ids[None, :] < jnp.arange(1, 4, dtype=jnp.int32)[:, None]).astype(jnp.int32), axis=1
-    )
-    slots = me * (ROWS // BLOCK) + jnp.arange(ROWS // BLOCK, dtype=jnp.int32)
-    groups = jnp.arange(slot_table.shape[0], dtype=jnp.int32)
-    held = jnp.sum(jnp.where(slot_table[None, :] == slots[:, None], groups[None, :], 0), axis=1)
-    return make_plan(me, starts, held)
+    lowest = start_of(plan, me * ROWS)
+    other = me ^ 1
+    lowest_there = start_of(plan, other * ROWS)
+    mine, theirs = jnp.int32(0), jnp.int32(0)
+    plan[DONE] = 0
+    for a, (dy, dc) in enumerate(SETS):
+        for b in range(8):
+            dz, dx = b // 2, b % 2
+            block = (x ^ dx) * 32 + ((z + dz) & 3) * 8 + ((y + dy) & 3) * 2 + (c ^ dc)
+            needed = (block <= me) & (block * ROWS + ROWS - 1 >= lowest)
+            plan[PLACE + 8 * a + b] = jnp.where(needed, mine, -1)
+            plan[LIST + jnp.where(needed, mine, 71)] = block
+            mine = mine + needed.astype(jnp.int32)
+            block = block ^ 1
+            there = (block <= other) & (block * ROWS + ROWS - 1 >= lowest_there)
+            theirs = theirs + there.astype(jnp.int32)
+        steps = mine // (STEP // ROWS)
+        plan[DONE + 8 * (a + 1)] = jnp.maximum(
+            jnp.minimum(steps, theirs // (STEP // ROWS)), steps - 1
+        )
+    plan[SCALARS + 8] = mine
+
+
+def make_plan(me, doc_ids, slot_table):
+    return pl.pallas_call(
+        plan_kernel,
+        out_shape=jax.ShapeDtypeStruct((224,), jnp.int32),
+        in_specs=[pl.BlockSpec(memory_space=pltpu.SMEM)]
+        + [pl.BlockSpec(memory_space=pltpu.VMEM)] * 2,
+        out_specs=pl.BlockSpec(memory_space=pltpu.SMEM),
+        compiler_params=params(4),
+        name="plan",
+    )(me[None], doc_ids, slot_table)
 
 
 def start_of(plan, position):
@@ -261,11 +281,11 @@
     acc, m, l = refs[:3]
     refs = refs[3:]
     if last:
-        out_ref, cache_ref = refs[:2]
-        refs = refs[2:]
+        out_hbm, cache_ref = refs[:2]
+        kv, even, odd, out_ref, sems = refs[2:]
     else:
         left_out = refs.pop(0)
-    kv, even, odd = refs
+        kv, even, odd = refs
     me = plan[SCALARS + 3]
     blocks = STEP // ROWS
     rows = GROUP * ROWS
@@ -274,9 +294,10 @@
     def rows_of(block):
         return pl.ds(pl.multiple_of(block * ROWS, ROWS), ROWS)
 
-    base = plan[BEFORE + 8 * first_set] // blocks * blocks
+    before = jnp.maximum(plan[DONE + 8 * first_set], 0)
+    base = before * blocks
     if first_set:
-        for i in range(blocks - 1):
+        for i in range(LEFT):
             kv[i * ROWS : (i + 1) * ROWS, :] = left[i * ROWS : (i + 1) * ROWS, :]
     for a in range(n):
         for b in range(8):
@@ -286,14 +307,14 @@
             def _(a=a, b=b, place=place):
                 kv[rows_of(place - base), :] = sets[a][b * ROWS : (b + 1) * ROWS, :]
 
-    found = plan[BEFORE + 8 * (first_set + n)] - base
     if last:
+        found = plan[SCALARS + 8] - base
         steps = (found + blocks - 1) // blocks
         for i in range(blocks - 1):
             kv[rows_of(found + i), :] = jnp.zeros((ROWS, WIDTH), jnp.bfloat16)
     else:
-        steps = found // blocks
-        for i in range(blocks - 1):
+        steps = jnp.maximum(plan[DONE + 8 * (first_set + n)], 0) - before
+        for i in range(LEFT):
             left_out[i * ROWS : (i + 1) * ROWS, :] = kv[rows_of(steps * blocks + i), :]
 
     def keys_of(j):
@@ -369,17 +390,22 @@
                         pl.ds(row, BLOCK), :
                     ][:, : LATENT + ROPE]
 
-        def give(g, carry):
-            for head in range(GROUP):
-                at = pl.ds(pl.multiple_of(g * rows + head * ROWS, ROWS), ROWS)
+        copies = []
+        for g in range(groups):
+            for head in range(g * GROUP, (g + 1) * GROUP):
+                at = slice(head * ROWS, (head + 1) * ROWS)
                 total = jnp.sum(l[at, :], axis=1, keepdims=True)
                 mixed = (acc[at, :] * (1.0 / total)).astype(jnp.bfloat16)
-                out_ref[:, pl.ds(pl.multiple_of((g * GROUP + head) * VD, VD), VD)] = jnp.dot(
-                    mixed, uv_ref[g * GROUP + head], preferred_element_type=jnp.float32
+                out_ref[:, head * VD : (head + 1) * VD] = jnp.dot(
+                    mixed, uv_ref[head], preferred_element_type=jnp.float32
                 ).astype(jnp.bfloat16)
-            return carry
-
-        lax.fori_loop(0, groups, give, 0)
+            columns = slice(g * GROUP * VD, (g + 1) * GROUP * VD)
+            copies.append(
+                pltpu.make_async_copy(out_ref.at[:, columns], out_hbm.at[:, columns], sems.at[g])
+            )
+            copies[-1].start()
+        for copy in copies:
+            copy.wait()
 
 
 def attend(plan, queries, sets, first_set, carried, w_uv=None, others=()):
@@ -396,27 +422,33 @@
         operands += [w_uv, *others]
     aliases = {1 + len(operands) + i: i for i in range(len(widths))}
     operands += list(state)
-    room = (8 * n + 2 * STEP // ROWS) * ROWS
+    room = (8 * n + 3 * STEP // ROWS) * ROWS
     scratch = [
         pltpu.VMEM((room, WIDTH), jnp.bfloat16),
         pltpu.VMEM((rows, STEP), jnp.float32),
         pltpu.VMEM((rows, STEP), jnp.float32),
     ]
     whole = pl.BlockSpec(memory_space=pltpu.VMEM)
+    out_specs = [whole] * (len(widths) + 1)
     out_shape = [jax.ShapeDtypeStruct((total, w), jnp.float32) for w in widths]
     if last:
         out_shape += [
             jax.ShapeDtypeStruct((ROWS, total // ROWS * VD), jnp.bfloat16),
             jax.ShapeDtypeStruct((ROWS, LATENT + ROPE), jnp.bfloat16),
         ]
+        out_specs[-1:] = [pl.BlockSpec(memory_space=pltpu.HBM), whole]
+        scratch += [
+            pltpu.VMEM((ROWS, total // ROWS * VD), jnp.bfloat16),
+            pltpu.SemaphoreType.DMA((total // rows,)),
+        ]
     else:
-        out_shape.append(jax.ShapeDtypeStruct((STEP - ROWS, WIDTH), jnp.bfloat16))
+        out_shape.append(jax.ShapeDtypeStruct((LEFT * ROWS, WIDTH), jnp.bfloat16))
     flops = 2 * total * 8 * n * ROWS * (WIDTH + LATENT)
     out = pl.pallas_call(
         functools.partial(attend_kernel, first_set, n, last),
         out_shape=out_shape,
         in_specs=[pl.BlockSpec(memory_space=pltpu.SMEM)] + [whole] * len(operands),
-        out_specs=[whole] * len(out_shape),
+        out_specs=out_specs,
         scratch_shapes=scratch,
         input_output_aliases=aliases,
         compiler_params=params(ATTEND_MIB),
@@ -451,20 +483,23 @@
     sign = jnp.where((jnp.arange(128) & 63) < half, -1.0, 1.0).astype(jnp.float32)
     cosines, sines = jnp.cos(angle), jnp.sin(angle) * sign[None, :]
 
-    plan = plan_of(me, doc_ids, slot_table)
-
     mine = project(hidden, attn_gain, kv_down)
     theirs = lax.ppermute(mine, "tensor", [(0, 1), (1, 0)])
     queries = make_queries(q_nope, q_pe, cosines, sines, w_uk)
-    mine, kv_gain = keep(plan, mine, kv_gain)
+    mine, kv_gain = keep(mine, kv_gain)
+    plan = make_plan(me, doc_ids, slot_table)
     own = finish(mine, theirs, cosines, sines, kv_gain)
     state = blank(plan, queries.shape[0])
 
     two = join([own, fetch(own, dx=1)])
-    eight = join([two] + [fetch(two, dz=d) for d in (1, 2, 3)])
-    across = {0: eight}
-    for d in (1, 3, 2):
-        across[d] = fetch(eight, dy=d)
+    over_z = [fetch(two, dz=d) for d in (1, 2, 3)]
+    early = {d: fetch(two, dy=d) for d in (1, 3)}
+    six = join(over_z)
+    late = {d: fetch(six, dy=d) for d in (1, 3)}
+    eight = join([two, six])
+    across = {0: eight, 2: fetch(eight, dy=2)}
+    for d in (1, 3):
+        across[d] = join([early[d], late[d]])
     beside = {d: fetch(across[d], dc=1) for d in (0, 1, 3, 2)}
 
     sets = [beside[dy] if dc else across[dy] for dy, dc in SETS]

time: 111 us -> 110 us (level)
  the two profiles are of different devices: /device:TPU:103 before, /device:TPU:117 now
where the time goes in v3:
time: 110 us
  Pallas kernels  68 us (62%)
  waiting for transfers between devices  23.1 us (21%)
  starting transfers between devices  16.8 us (15%)
    pallas_call x6, Pallas kernels, attend(): pl.pallas_call(functools.partial(attend_kernel, first_set, n, last), out_...  58.2 us
    ppermute x13, waiting for transfers between devices, fetch(): return lax.ppermute(array, 'seq', pairs)  20 us
    ppermute x13, starting transfers between devices, fetch(): return lax.ppermute(array, 'seq', pairs)  15.8 us
    pallas_call x1, Pallas kernels, project(): pl.pallas_call(project_kernel, out_shape=jax.ShapeDtypeStruct((ROWS, WIDT...  4.13 us
    ppermute x1, waiting for transfers between devices, local(): theirs = lax.ppermute(mine, 'tensor', [(0, 1), (1, 0)])  3.11 us
    pallas_call x1, Pallas kernels, make_queries(): pl.pallas_call(queries_kernel, out_shape=jax.ShapeDtypeStruct((heads * RO...  2.59 us
  transfers between devices with their start and end apart: 14, of which 8 were waited for; matrix products, arithmetic and copies ran while one was open for 0% of the time, Pallas kernels for 44%

profile of v3, /device:TPU:117, one launch (start us, length us, event | category | flops | bytes accessed | tf_op | source)
XLA Modules:
  0.0 110.3 jit_solution(1230893495092335932)
XLA Ops:
  0.6 4.1 %project.1.mine_ref = f32[64,640]{1,0:T(8,128)} custom-call(bf16[64,3584]{1,0:T(8,128)(2,1)} %hidden_hbm.1, f32[3584]{0:T(1024)} %gain_hbm.1, bf16[576,3584]{1,0:T(8,128)(2,1)} %bitcast.6), custom_call_target="tpu_custom_call" | custom-call | tf_op jit(solution)/shard_map/project/pallas_call | solution.py:83
  4.8 1.0 collective-permute-start
  5.9 0.9 copy-done.2
  6.8 0.2 fusion
  7.0 3.1 %collective-permute-done.theirs_ref = f32[64,640]{1,0:T(8,128)S(1)} collective-permute-done((f32[64,640]{1,0:T(8,128)}, f32[64,640]{1,0:T(8,128)S(1)}, u32[]{:S(2)}, u32[]{:S(2)}) %collective-permute-start) | collective-permute-done | bytes 163872 | tf_op jit(solution)/shard_map/ppermute | solution.py:487
  10.2 0.2 finish.1.refs_0_
  10.4 0.3 collective-permute-start.1
  10.7 4.6 %collective-permute-done.1.refs_1_ = bf16[64,640]{1,0:T(8,128)(2,1)S(1)} collective-permute-done((bf16[64,640]{1,0:T(8,128)(2,1)S(1)}, bf16[64,640]{1,0:T(8,128)(2,1)S(1)}, u32[]{:S(2)}, u32[]{:S(2)}) %collective-permute-start.1) | collective-permute-done | bytes 81952 | tf_op jit(solution)/shard_map/ppermute | solution.py:474
  15.4 1.9 %collective-permute-start.3 = (bf16[128,640]{1,0:T(8,128)(2,1)S(1)}, bf16[128,640]{1,0:T(8,128)(2,1)S(1)}, u32[]{:S(2)}, u32[]{:S(2)}) collective-permute-start(bf16[128,640]{1,0:T(8,128)(2,1)S(1)} %shard_map.113.refs_0_), channel_id=1, source_target_pairs={{32,0},{34,2},{36,4},{38,6},{40,8},{42,10},{44,12},{46,14},{48,16}... | collective-permute-start | bytes 491528 | tf_op jit(solution)/shard_map/ppermute | solution.py:474
  17.3 2.3 %collective-permute-done.4.refs_2_ = bf16[128,640]{1,0:T(8,128)(2,1)S(1)} collective-permute-done((bf16[128,640]{1,0:T(8,128)(2,1)S(1)}, bf16[128,640]{1,0:T(8,128)(2,1)S(1)}, u32[]{:S(2)}, u32[]{:S(2)}) %collective-permute-start.4) | collective-permute-done | bytes 163872 | tf_op jit(solution)/shard_map/ppermute | solution.py:474
  19.6 1.6 %collective-permute-done.3.refs_1_ = bf16[128,640]{1,0:T(8,128)(2,1)S(1)} collective-permute-done((bf16[128,640]{1,0:T(8,128)(2,1)S(1)}, bf16[128,640]{1,0:T(8,128)(2,1)S(1)}, u32[]{:S(2)}, u32[]{:S(2)}) %collective-permute-start.3) | collective-permute-done | bytes 163872 | tf_op jit(solution)/shard_map/ppermute | solution.py:474
  21.2 2.4 %collective-permute-done.2.refs_0_ = bf16[128,640]{1,0:T(8,128)(2,1)S(1)} collective-permute-done((bf16[128,640]{1,0:T(8,128)(2,1)S(1)}, bf16[128,640]{1,0:T(8,128)(2,1)S(1)}, u32[]{:S(2)}, u32[]{:S(2)}) %collective-permute-start.2) | collective-permute-done | bytes 163872 | tf_op jit(solution)/shard_map/ppermute | solution.py:474
  23.7 0.1 collective-permute-start.5
  23.8 4.0 %collective-permute-start.13 = (bf16[512,640]{1,0:T(8,128)(2,1)S(1)}, bf16[512,640]{1,0:T(8,128)(2,1)S(1)}, u32[]{:S(2)}, u32[]{:S(2)}) collective-permute-start(bf16[512,640]{1,0:T(8,128)(2,1)S(1)} %shard_map.115.refs_2_.refs_5_), channel_id=1, source_target_pairs={{2,0},{0,2},{6,4},{4,6},{10,8},{8,10},{14,12},{12,14},{18,16},{16,... | collective-permute-start | bytes 1966088 | tf_op jit(solution)/shard_map/ppermute | solution.py:474
  27.9 2.1 %collective-permute-start.7 = (bf16[128,640]{1,0:T(8,128)(2,1)S(1)}, bf16[128,640]{1,0:T(8,128)(2,1)S(1)}, u32[]{:S(2)}, u32[]{:S(2)}) collective-permute-start(bf16[128,640]{1,0:T(8,128)(2,1)S(1)} %shard_map.113.refs_0_), channel_id=1, source_target_pairs={{4,0},{6,2},{8,4},{10,6},{12,8},{14,10},{0,12},{2,14},{20,16},{22,... | collective-permute-start | bytes 491528 | tf_op jit(solution)/shard_map/ppermute | solution.py:474
  30.0 1.1 collective-permute-start.8
  31.1 0.4 collective-permute-start.11
  31.5 1.3 %plan.1.refs_0_ = s32[224]{0:T(256)S(1)} custom-call(s32[1]{0:T(128)} %bitcast.me_ref, s32[4096]{0:T(1024)S(1)} %copy-done.3, s32[256]{0:T(256)S(1)} %copy-done.4), custom_call_target="tpu_custom_call" | custom-call | tf_op jit(solution)/shard_map/plan/pallas_call | solution.py:251
  32.8 1.4 %blank.1 = (f32[4096,512]{1,0:T(8,128)S(1)}, f32[4096,128]{1,0:T(8,128)S(1)}, f32[4096,128]{1,0:T(8,128)S(1)}) custom-call(s32[224]{0:T(256)S(1)} %plan.1.refs_0_), custom_call_target="tpu_custom_call" | custom-call | tf_op jit(solution)/shard_map/blank/pallas_call | solution.py:164
  34.2 2.6 %queries.1.refs_1_ = bf16[4096,640]{1,0:T(8,128)(2,1)S(1)} custom-call(bf16[64,8192]{1,0:T(8,128)(2,1)S(1)} %copy-done, bf16[64,4096]{1,0:T(8,128)(2,1)S(1)} %copy-done.1, f32[64,128]{1,0:T(8,128)S(1)} %get-tuple-element.57.cos_ref, f32[64,128]{1,0:T(8,128)S(1)} %get-tuple-element.56.sin_ref, bf16[64,128,512]{2,1,0:T(8,128)(2,1)S(1)} %bitcast.5), custom_call_target="tpu_custom_call" | custom-call | tf_op jit(solution)/shard_map/queries/pallas_call | solution.py:193
  36.8 5.4 %collective-permute-done.7.refs_0_ = bf16[128,640]{1,0:T(8,128)(2,1)S(1)} collective-permute-done((bf16[128,640]{1,0:T(8,128)(2,1)S(1)}, bf16[128,640]{1,0:T(8,128)(2,1)S(1)}, u32[]{:S(2)}, u32[]{:S(2)}) %collective-permute-start.7) | collective-permute-done | bytes 163872 | tf_op jit(solution)/shard_map/ppermute | solution.py:474
  42.2 3.5 %collective-permute-start.10 = (bf16[128,640]{1,0:T(8,128)(2,1)S(1)}, bf16[128,640]{1,0:T(8,128)(2,1)S(1)}, u32[]{:S(2)}, u32[]{:S(2)}) collective-permute-start(bf16[128,640]{1,0:T(8,128)(2,1)S(1)} %shard_map.113.refs_0_), channel_id=1, source_target_pairs={{12,0},{14,2},{0,4},{2,6},{4,8},{6,10},{8,12},{10,14},{28,16},{30,... | collective-permute-start | bytes 491528 | tf_op jit(solution)/shard_map/ppermute | solution.py:474
  45.7 4.9 %shard_map.118 = (f32[4096,512]{1,0:T(8,128)S(1)}, f32[4096,128]{1,0:T(8,128)S(1)}, f32[4096,128]{1,0:T(8,128)S(1)}, bf16[448,640]{1,0:T(8,128)(2,1)S(1)}) custom-call(s32[224]{0:T(256)S(1)} %plan.1.refs_0_, bf16[4096,640]{1,0:T(8,128)(2,1)S(1)} %queries.1.refs_1_, ...), custom_call_target="tpu_custom_call", output_to_operand_aliasing={{0}: (3, {}), {1}: (4, {}), {2}: (5, {})} | custom-call | flops 4831838208 | bytes 25165824 | tf_op jit(solution)/shard_map/pallas_call | solution.py:447
  50.6 3.4 %collective-permute-done.8.refs_1_ = bf16[384,640]{1,0:T(8,128)(2,1)S(1)} collective-permute-done((bf16[384,640]{1,0:T(8,128)(2,1)S(1)}, bf16[384,640]{1,0:T(8,128)(2,1)S(1)}, u32[]{:S(2)}, u32[]{:S(2)}) %collective-permute-start.8) | collective-permute-done | bytes 491552 | tf_op jit(solution)/shard_map/ppermute | solution.py:474
  54.1 1.6 %collective-permute-start.9 = (bf16[512,640]{1,0:T(8,128)(2,1)S(1)}, bf16[512,640]{1,0:T(8,128)(2,1)S(1)}, u32[]{:S(2)}, u32[]{:S(2)}) collective-permute-start(bf16[512,640]{1,0:T(8,128)(2,1)S(1)} %shard_map.116.refs_2_.refs_7_), channel_id=1, source_target_pairs={{2,0},{0,2},{6,4},{4,6},{10,8},{8,10},{14,12},{12,14},{18,16},{16,... | collective-permute-start | bytes 1966088 | tf_op jit(solution)/shard_map/ppermute | solution.py:474
  55.6 0.3 collective-permute-done.10.refs_0_
  56.0 0.6 collective-permute-start.12
  56.7 8.7 %shard_map.119 = (f32[4096,512]{1,0:T(8,128)S(1)}, f32[4096,128]{1,0:T(8,128)S(1)}, f32[4096,128]{1,0:T(8,128)S(1)}, bf16[448,640]{1,0:T(8,128)(2,1)S(1)}) custom-call(s32[224]{0:T(256)S(1)} %plan.1.refs_0_, bf16[4096,640]{1,0:T(8,128)(2,1)S(1)} %queries.1.refs_1_, ...), custom_call_target="tpu_custom_call", output_to_operand_aliasing={{0}: (4, {}), {1}: (5, {}), {2}: (6, {})} | custom-call | flops 4831838208 | bytes 25165824 | tf_op jit(solution)/shard_map/pallas_call | solution.py:447
  65.4 12.2 %shard_map.120 = (f32[4096,512]{1,0:T(8,128)S(1)}, f32[4096,128]{1,0:T(8,128)S(1)}, f32[4096,128]{1,0:T(8,128)S(1)}, bf16[448,640]{1,0:T(8,128)(2,1)S(1)}) custom-call(s32[224]{0:T(256)S(1)} %plan.1.refs_0_, bf16[4096,640]{1,0:T(8,128)(2,1)S(1)} %queries.1.refs_1_, ...), custom_call_target="tpu_custom_call", output_to_operand_aliasing={{0}: (5, {}), {1}: (6, {}), {2}: (7, {})} | custom-call | flops 9663676416 | bytes 25165824 | tf_op jit(solution)/shard_map/pallas_call | solution.py:447
  77.6 12.2 %shard_map.121 = (f32[4096,512]{1,0:T(8,128)S(1)}, f32[4096,128]{1,0:T(8,128)S(1)}, f32[4096,128]{1,0:T(8,128)S(1)}, bf16[448,640]{1,0:T(8,128)(2,1)S(1)}) custom-call(s32[224]{0:T(256)S(1)} %plan.1.refs_0_, bf16[4096,640]{1,0:T(8,128)(2,1)S(1)} %queries.1.refs_1_, ...), custom_call_target="tpu_custom_call", output_to_operand_aliasing={{0}: (5, {}), {1}: (6, {}), {2}: (7, {})} | custom-call | flops 9663676416 | bytes 25165824 | tf_op jit(solution)/shard_map/pallas_call | solution.py:447
  89.8 4.9 %shard_map.122 = (f32[4096,512]{1,0:T(8,128)S(1)}, f32[4096,128]{1,0:T(8,128)S(1)}, f32[4096,128]{1,0:T(8,128)S(1)}, bf16[448,640]{1,0:T(8,128)(2,1)S(1)}) custom-call(s32[224]{0:T(256)S(1)} %plan.1.refs_0_, bf16[4096,640]{1,0:T(8,128)(2,1)S(1)} %queries.1.refs_1_, ...), custom_call_target="tpu_custom_call", output_to_operand_aliasing={{0}: (4, {}), {1}: (5, {}), {2}: (6, {})} | custom-call | flops 4831838208 | bytes 25165824 | tf_op jit(solution)/shard_map/pallas_call | solution.py:447
  94.8 15.4 %shard_map.123 = (f32[4096,512]{1,0:T(8,128)S(1)}, f32[4096,128]{1,0:T(8,128)S(1)}, f32[4096,128]{1,0:T(8,128)S(1)}, bf16[64,8192]{1,0:T(8,128)(2,1)}, bf16[64,576]{1,0:T(8,128)(2,1)}) custom-call(s32[224]{0:T(256)S(1)} %plan.1.refs_0_, bf16[4096,640]{1,0:T(8,128)(2,1)S(1)} %queries.1.refs_1_, ...), custom_call_target="tpu_custom_call", output_to_operand_aliasing={{0}: (12, {}), {1}: (13, {}), {2}: (14, {})} | custom-call | flops 4831838208 | bytes 25165824 | tf_op jit(solution)/shard_map/pallas_call | solution.py:447
  (41 shorter events, 0.6 us)
Async XLA Ops:
  0.6 5.3 %copy-start.5 = (f32[512]{0:T(512)S(1)}, f32[512]{0:T(512)}, u32[]{:S(2)}) copy-start(f32[512]{0:T(512)} %gain_ref.1) | copy-start | bytes 6148
  4.8 5.4 %collective-permute-start = (f32[64,640]{1,0:T(8,128)}, f32[64,640]{1,0:T(8,128)S(1)}, u32[]{:S(2)}, u32[]{:S(2)}) collective-permute-start(f32[64,640]{1,0:T(8,128)} %project.1.mine_ref), channel_id=1, source_target_pairs={{0,1},{1,0},{2,3},{3,2},{4,5},{5,4},{6,7},{7,6},{8,9},{9,8},{10,11... | collective-permute-start | bytes 491528 | tf_op jit(solution)/shard_map/ppermute | solution.py:487
  5.9 0.9 copy-start.2
  10.2 24.0 %slice-start.2 = ((s8[8388608]{0:T(1024)(128)(4,1)}), s8[4194304]{0:T(1024)(128)(4,1)S(1)}, s32[]{:S(2)}) async-start(s8[8388608]{0:T(1024)(128)(4,1)} %bitcast.4), calls=%async_computation.2 | async-start | bytes 8388608
  10.2 24.0 %slice-start.3 = ((s8[8388608]{0:T(1024)(128)(4,1)}), s8[4194304]{0:T(1024)(128)(4,1)S(1)}, s32[]{:S(2)}) async-start(s8[8388608]{0:T(1024)(128)(4,1)} %bitcast.4), calls=%async_computation.3 | async-start | bytes 8388608
  10.4 21.1 %copy-start.3 = (s32[4096]{0:T(1024)S(1)}, s32[4096]{0:T(1024)}, u32[]{:S(2)}) copy-start(s32[4096]{0:T(1024)} %docs_ref.1) | copy-start | bytes 49156
  10.4 21.1 %copy-start.4 = (s32[256]{0:T(256)S(1)}, s32[256]{0:T(256)}, u32[]{:S(2)}) copy-start(s32[256]{0:T(256)} %slots_ref.1) | copy-start | bytes 3076
  10.4 23.7 %copy-start = (bf16[64,8192]{1,0:T(8,128)(2,1)S(1)}, bf16[64,8192]{1,0:T(8,128)(2,1)}, u32[]{:S(2)}) copy-start(bf16[64,8192]{1,0:T(8,128)(2,1)} %nope_ref.1) | copy-start | bytes 3145732
  10.4 23.7 %copy-start.1 = (bf16[64,4096]{1,0:T(8,128)(2,1)S(1)}, bf16[64,4096]{1,0:T(8,128)(2,1)}, u32[]{:S(2)}) copy-start(bf16[64,4096]{1,0:T(8,128)(2,1)} %pe_ref.1) | copy-start | bytes 1572868
  10.4 4.9 %collective-permute-start.1 = (bf16[64,640]{1,0:T(8,128)(2,1)S(1)}, bf16[64,640]{1,0:T(8,128)(2,1)S(1)}, u32[]{:S(2)}, u32[]{:S(2)}) collective-permute-start(bf16[64,640]{1,0:T(8,128)(2,1)S(1)} %finish.1.refs_0_), channel_id=1, source_target_pairs={{64,0},{66,2},{68,4},{70,6},{72,8},{74,10},{76,12},{78,14},{80,16}... | collective-permute-start | bytes 245768 | tf_op jit(solution)/shard_map/ppermute | solution.py:474
  15.3 4.2 %collective-permute-start.4 = (bf16[128,640]{1,0:T(8,128)(2,1)S(1)}, bf16[128,640]{1,0:T(8,128)(2,1)S(1)}, u32[]{:S(2)}, u32[]{:S(2)}) collective-permute-start(bf16[128,640]{1,0:T(8,128)(2,1)S(1)} %shard_map.113.refs_0_), channel_id=1, source_target_pairs={{48,0},{50,2},{52,4},{54,6},{56,8},{58,10},{60,12},{62,14},{0,16},... | collective-permute-start | bytes 491528 | tf_op jit(solution)/shard_map/ppermute | solution.py:474
  15.4 5.8 %collective-permute-start.3 = (bf16[128,640]{1,0:T(8,128)(2,1)S(1)}, bf16[128,640]{1,0:T(8,128)(2,1)S(1)}, u32[]{:S(2)}, u32[]{:S(2)}) collective-permute-start(bf16[128,640]{1,0:T(8,128)(2,1)S(1)} %shard_map.113.refs_0_), channel_id=1, source_target_pairs={{32,0},{34,2},{36,4},{38,6},{40,8},{42,10},{44,12},{46,14},{48,16}... | collective-permute-start | bytes 491528 | tf_op jit(solution)/shard_map/ppermute | solution.py:474
  17.3 6.3 %collective-permute-start.2 = (bf16[128,640]{1,0:T(8,128)(2,1)S(1)}, bf16[128,640]{1,0:T(8,128)(2,1)S(1)}, u32[]{:S(2)}, u32[]{:S(2)}) collective-permute-start(bf16[128,640]{1,0:T(8,128)(2,1)S(1)} %shard_map.113.refs_0_), channel_id=1, source_target_pairs={{16,0},{18,2},{20,4},{22,6},{24,8},{26,10},{28,12},{30,14},{32,16}... | collective-permute-start | bytes 491528 | tf_op jit(solution)/shard_map/ppermute | solution.py:474
  23.7 32.9 %collective-permute-start.5 = (bf16[512,640]{1,0:T(8,128)(2,1)S(1)}, bf16[512,640]{1,0:T(8,128)(2,1)S(1)}, u32[]{:S(2)}, u32[]{:S(2)}) collective-permute-start(bf16[512,640]{1,0:T(8,128)(2,1)S(1)} %shard_map.115.refs_2_.refs_5_), channel_id=1, source_target_pairs={{8,0},{10,2},{12,4},{14,6},{0,8},{2,10},{4,12},{6,14},{24,16},{26,... | collective-permute-start | bytes 1966088 | tf_op jit(solution)/shard_map/ppermute | solution.py:474
  23.8 32.9 %collective-permute-start.13 = (bf16[512,640]{1,0:T(8,128)(2,1)S(1)}, bf16[512,640]{1,0:T(8,128)(2,1)S(1)}, u32[]{:S(2)}, u32[]{:S(2)}) collective-permute-start(bf16[512,640]{1,0:T(8,128)(2,1)S(1)} %shard_map.115.refs_2_.refs_5_), channel_id=1, source_target_pairs={{2,0},{0,2},{6,4},{4,6},{10,8},{8,10},{14,12},{12,14},{18,16},{16,... | collective-permute-start | bytes 1966088 | tf_op jit(solution)/shard_map/ppermute | solution.py:474
  27.9 14.3 %collective-permute-start.7 = (bf16[128,640]{1,0:T(8,128)(2,1)S(1)}, bf16[128,640]{1,0:T(8,128)(2,1)S(1)}, u32[]{:S(2)}, u32[]{:S(2)}) collective-permute-start(bf16[128,640]{1,0:T(8,128)(2,1)S(1)} %shard_map.113.refs_0_), channel_id=1, source_target_pairs={{4,0},{6,2},{8,4},{10,6},{12,8},{14,10},{0,12},{2,14},{20,16},{22,... | collective-permute-start | bytes 491528 | tf_op jit(solution)/shard_map/ppermute | solution.py:474
  30.0 24.0 %collective-permute-start.8 = (bf16[384,640]{1,0:T(8,128)(2,1)S(1)}, bf16[384,640]{1,0:T(8,128)(2,1)S(1)}, u32[]{:S(2)}, u32[]{:S(2)}) collective-permute-start(bf16[384,640]{1,0:T(8,128)(2,1)S(1)} %shard_map.114.refs_1_), channel_id=1, source_target_pairs={{4,0},{6,2},{8,4},{10,6},{12,8},{14,10},{0,12},{2,14},{20,16},{22,... | collective-permute-start | bytes 1474568 | tf_op jit(solution)/shard_map/ppermute | solution.py:474
  31.1 24.9 %collective-permute-start.11 = (bf16[384,640]{1,0:T(8,128)(2,1)S(1)}, bf16[384,640]{1,0:T(8,128)(2,1)S(1)}, u32[]{:S(2)}, u32[]{:S(2)}) collective-permute-start(bf16[384,640]{1,0:T(8,128)(2,1)S(1)} %shard_map.114.refs_1_), channel_id=1, source_target_pairs={{12,0},{14,2},{0,4},{2,6},{4,8},{6,10},{8,12},{10,14},{28,16},{30,... | collective-permute-start | bytes 1474568 | tf_op jit(solution)/shard_map/ppermute | solution.py:474
  42.2 13.8 %collective-permute-start.10 = (bf16[128,640]{1,0:T(8,128)(2,1)S(1)}, bf16[128,640]{1,0:T(8,128)(2,1)S(1)}, u32[]{:S(2)}, u32[]{:S(2)}) collective-permute-start(bf16[128,640]{1,0:T(8,128)(2,1)S(1)} %shard_map.113.refs_0_), channel_id=1, source_target_pairs={{12,0},{14,2},{0,4},{2,6},{4,8},{6,10},{8,12},{10,14},{28,16},{30,... | collective-permute-start | bytes 491528 | tf_op jit(solution)/shard_map/ppermute | solution.py:474
  54.1 23.5 %collective-permute-start.9 = (bf16[512,640]{1,0:T(8,128)(2,1)S(1)}, bf16[512,640]{1,0:T(8,128)(2,1)S(1)}, u32[]{:S(2)}, u32[]{:S(2)}) collective-permute-start(bf16[512,640]{1,0:T(8,128)(2,1)S(1)} %shard_map.116.refs_2_.refs_7_), channel_id=1, source_target_pairs={{2,0},{0,2},{6,4},{4,6},{10,8},{8,10},{14,12},{12,14},{18,16},{16,... | collective-permute-start | bytes 1966088 | tf_op jit(solution)/shard_map/ppermute | solution.py:474
  56.0 21.5 %collective-permute-start.12 = (bf16[512,640]{1,0:T(8,128)(2,1)S(1)}, bf16[512,640]{1,0:T(8,128)(2,1)S(1)}, u32[]{:S(2)}, u32[]{:S(2)}) collective-permute-start(bf16[512,640]{1,0:T(8,128)(2,1)S(1)} %shard_map.117.refs_3_.refs_8_), channel_id=1, source_target_pairs={{2,0},{0,2},{6,4},{4,6},{10,8},{8,10},{14,12},{12,14},{18,16},{16,... | collective-permute-start | bytes 1966088 | tf_op jit(solution)/shard_map/ppermute | solution.py:474
  56.6 38.1 %collective-permute-start.6 = (bf16[512,640]{1,0:T(8,128)(2,1)S(1)}, bf16[512,640]{1,0:T(8,128)(2,1)S(1)}, u32[]{:S(2)}, u32[]{:S(2)}) collective-permute-start(bf16[512,640]{1,0:T(8,128)(2,1)S(1)} %collective-permute-done.5.refs_2_.refs_11_), channel_id=1, source_target_pairs={{2,0},{0,2},{6,4},{4,6},{10,8},{8,10},{14,12},{12,14},{18,16},{16,... | collective-permute-start | bytes 1966088 | tf_op jit(solution)/shard_map/ppermute | solution.py:474
  89.8 5.0 %slice-start = ((s8[8388608]{0:T(1024)(128)(4,1)}), s8[4194304]{0:T(1024)(128)(4,1)S(1)}, s32[]{:S(2)}) async-start(s8[8388608]{0:T(1024)(128)(4,1)} %bitcast.2), calls=%async_computation | async-start | bytes 8388608
  89.8 5.0 %slice-start.1 = ((s8[8388608]{0:T(1024)(128)(4,1)}), s8[4194304]{0:T(1024)(128)(4,1)S(1)}, s32[]{:S(2)}) async-start(s8[8388608]{0:T(1024)(128)(4,1)} %bitcast.2), calls=%async_computation.1 | async-start | bytes 8388608

commit v4 on v3

--- a/solution.py
+++ b/solution.py
@@ -154,21 +154,20 @@
     )(mine, gain)
 
 
-def blank_kernel(plan, acc, m, l):
+def blank_kernel(acc, m, l):
     acc[...] = jnp.zeros_like(acc)
     m[...] = jnp.full_like(m, FLOOR)
     l[...] = jnp.zeros_like(l)
 
 
-def blank(plan, rows):
+def blank(rows):
     return pl.pallas_call(
         blank_kernel,
         out_shape=[jax.ShapeDtypeStruct((rows, w), jnp.float32) for w in (LATENT, 128, 128)],
-        in_specs=[pl.BlockSpec(memory_space=pltpu.SMEM)],
         out_specs=[pl.BlockSpec(memory_space=pltpu.VMEM)] * 3,
         compiler_params=params(4),
         name="blank",
-    )(plan)
+    )()
 
 
 def queries_kernel(nope_ref, pe_ref, cos_ref, sin_ref, uk_ref, out_ref):
@@ -489,7 +488,7 @@
     mine, kv_gain = keep(mine, kv_gain)
     plan = make_plan(me, doc_ids, slot_table)
     own = finish(mine, theirs, cosines, sines, kv_gain)
-    state = blank(plan, queries.shape[0])
+    state = blank(queries.shape[0])
 
     two = join([own, fetch(own, dx=1)])
     over_z = [fetch(two, dz=d) for d in (1, 2, 3)]

time: 110 us -> 115 us (1.045)
  Pallas kernels: 68 us -> 72.3 us
    pallas_call x6, Pallas kernels: 58.2 us -> 63 us  [attend(): pl.pallas_call(functools.partial(attend_kernel, first_set, n, last), out_...]
  transfers between devices with their start and end apart: 14 -> 14, of which waited for: 8 -> 8; matrix products, arithmetic and copies ran while one was open for 0% -> 0% of each run, Pallas kernels for 44% -> 45%
where the time goes in v4:
time: 115 us
  Pallas kernels  72.3 us (63%)
  waiting for transfers between devices  23.3 us (20%)
  starting transfers between devices  16.8 us (15%)
    pallas_call x6, Pallas kernels, attend(): pl.pallas_call(functools.partial(attend_kernel, first_set, n, last), out_...  63 us
    ppermute x13, waiting for transfers between devices, fetch(): return lax.ppermute(array, 'seq', pairs)  20.2 us
    ppermute x13, starting transfers between devices, fetch(): return lax.ppermute(array, 'seq', pairs)  15.8 us
    pallas_call x1, Pallas kernels, project(): pl.pallas_call(project_kernel, out_shape=jax.ShapeDtypeStruct((ROWS, WIDT...  4.13 us
    ppermute x1, waiting for transfers between devices, local(): theirs = lax.ppermute(mine, 'tensor', [(0, 1), (1, 0)])  3.11 us
    pallas_call x1, Pallas kernels, make_queries(): pl.pallas_call(queries_kernel, out_shape=jax.ShapeDtypeStruct((heads * RO...  2.59 us
  transfers between devices with their start and end apart: 14, of which 8 were waited for; matrix products, arithmetic and copies ran while one was open for 0% of the time, Pallas kernels for 45%

profile of v4, /device:TPU:117, one launch (start us, length us, event | category | flops | bytes accessed | tf_op | source)
XLA Modules:
  0.0 114.7 jit_solution(13938612181049294859)
XLA Ops:
  0.6 4.1 %project.1.mine_ref = f32[64,640]{1,0:T(8,128)} custom-call(bf16[64,3584]{1,0:T(8,128)(2,1)} %hidden_hbm.1, f32[3584]{0:T(1024)} %gain_hbm.1, bf16[576,3584]{1,0:T(8,128)(2,1)} %bitcast.6), custom_call_target="tpu_custom_call" | custom-call | tf_op jit(solution)/shard_map/project/pallas_call | solution.py:83
  4.8 1.0 collective-permute-start
  5.9 0.9 copy-done.2
  6.8 0.2 fusion
  7.0 3.1 %collective-permute-done.theirs_ref = f32[64,640]{1,0:T(8,128)S(1)} collective-permute-done((f32[64,640]{1,0:T(8,128)}, f32[64,640]{1,0:T(8,128)S(1)}, u32[]{:S(2)}, u32[]{:S(2)}) %collective-permute-start) | collective-permute-done | bytes 163872 | tf_op jit(solution)/shard_map/ppermute | solution.py:486
  10.2 0.2 finish.1.refs_0_
  10.4 0.3 collective-permute-start.1
  10.7 4.6 %collective-permute-done.1.refs_1_ = bf16[64,640]{1,0:T(8,128)(2,1)S(1)} collective-permute-done((bf16[64,640]{1,0:T(8,128)(2,1)S(1)}, bf16[64,640]{1,0:T(8,128)(2,1)S(1)}, u32[]{:S(2)}, u32[]{:S(2)}) %collective-permute-start.1) | collective-permute-done | bytes 81952 | tf_op jit(solution)/shard_map/ppermute | solution.py:473
  15.4 1.9 %collective-permute-start.3 = (bf16[128,640]{1,0:T(8,128)(2,1)S(1)}, bf16[128,640]{1,0:T(8,128)(2,1)S(1)}, u32[]{:S(2)}, u32[]{:S(2)}) collective-permute-start(bf16[128,640]{1,0:T(8,128)(2,1)S(1)} %shard_map.113.refs_0_), channel_id=1, source_target_pairs={{32,0},{34,2},{36,4},{38,6},{40,8},{42,10},{44,12},{46,14},{48,16}... | collective-permute-start | bytes 491528 | tf_op jit(solution)/shard_map/ppermute | solution.py:473
  17.3 2.3 %collective-permute-done.4.refs_2_ = bf16[128,640]{1,0:T(8,128)(2,1)S(1)} collective-permute-done((bf16[128,640]{1,0:T(8,128)(2,1)S(1)}, bf16[128,640]{1,0:T(8,128)(2,1)S(1)}, u32[]{:S(2)}, u32[]{:S(2)}) %collective-permute-start.4) | collective-permute-done | bytes 163872 | tf_op jit(solution)/shard_map/ppermute | solution.py:473
  19.6 1.6 %collective-permute-done.3.refs_1_ = bf16[128,640]{1,0:T(8,128)(2,1)S(1)} collective-permute-done((bf16[128,640]{1,0:T(8,128)(2,1)S(1)}, bf16[128,640]{1,0:T(8,128)(2,1)S(1)}, u32[]{:S(2)}, u32[]{:S(2)}) %collective-permute-start.3) | collective-permute-done | bytes 163872 | tf_op jit(solution)/shard_map/ppermute | solution.py:473
  21.2 2.4 %collective-permute-done.2.refs_0_ = bf16[128,640]{1,0:T(8,128)(2,1)S(1)} collective-permute-done((bf16[128,640]{1,0:T(8,128)(2,1)S(1)}, bf16[128,640]{1,0:T(8,128)(2,1)S(1)}, u32[]{:S(2)}, u32[]{:S(2)}) %collective-permute-start.2) | collective-permute-done | bytes 163872 | tf_op jit(solution)/shard_map/ppermute | solution.py:473
  23.7 0.1 collective-permute-start.5
  23.8 4.0 %collective-permute-start.13 = (bf16[512,640]{1,0:T(8,128)(2,1)S(1)}, bf16[512,640]{1,0:T(8,128)(2,1)S(1)}, u32[]{:S(2)}, u32[]{:S(2)}) collective-permute-start(bf16[512,640]{1,0:T(8,128)(2,1)S(1)} %shard_map.115.refs_2_.refs_5_), channel_id=1, source_target_pairs={{2,0},{0,2},{6,4},{4,6},{10,8},{8,10},{14,12},{12,14},{18,16},{16,... | collective-permute-start | bytes 1966088 | tf_op jit(solution)/shard_map/ppermute | solution.py:473
  27.9 2.1 %collective-permute-start.7 = (bf16[128,640]{1,0:T(8,128)(2,1)S(1)}, bf16[128,640]{1,0:T(8,128)(2,1)S(1)}, u32[]{:S(2)}, u32[]{:S(2)}) collective-permute-start(bf16[128,640]{1,0:T(8,128)(2,1)S(1)} %shard_map.113.refs_0_), channel_id=1, source_target_pairs={{4,0},{6,2},{8,4},{10,6},{12,8},{14,10},{0,12},{2,14},{20,16},{22,... | collective-permute-start | bytes 491528 | tf_op jit(solution)/shard_map/ppermute | solution.py:473
  30.0 1.1 collective-permute-start.8
  31.1 0.4 collective-permute-start.11
  31.5 0.8 blank.1
  32.3 1.3 %plan.1.refs_0_ = s32[224]{0:T(256)S(1)} custom-call(s32[1]{0:T(128)} %bitcast.me_ref, s32[4096]{0:T(1024)S(1)} %copy-done.3, s32[256]{0:T(256)S(1)} %copy-done.4), custom_call_target="tpu_custom_call" | custom-call | tf_op jit(solution)/shard_map/plan/pallas_call | solution.py:250
  33.6 2.6 %queries.1.refs_1_ = bf16[4096,640]{1,0:T(8,128)(2,1)S(1)} custom-call(bf16[64,8192]{1,0:T(8,128)(2,1)S(1)} %copy-done, bf16[64,4096]{1,0:T(8,128)(2,1)S(1)} %copy-done.1, f32[64,128]{1,0:T(8,128)S(1)} %get-tuple-element.57.cos_ref, f32[64,128]{1,0:T(8,128)S(1)} %get-tuple-element.56.sin_ref, bf16[64,128,512]{2,1,0:T(8,128)(2,1)S(1)} %bitcast.5), custom_call_target="tpu_custom_call" | custom-call | tf_op jit(solution)/shard_map/queries/pallas_call | solution.py:192
  36.2 5.9 %collective-permute-done.7.refs_0_ = bf16[128,640]{1,0:T(8,128)(2,1)S(1)} collective-permute-done((bf16[128,640]{1,0:T(8,128)(2,1)S(1)}, bf16[128,640]{1,0:T(8,128)(2,1)S(1)}, u32[]{:S(2)}, u32[]{:S(2)}) %collective-permute-start.7) | collective-permute-done | bytes 163872 | tf_op jit(solution)/shard_map/ppermute | solution.py:473
  42.2 3.5 %collective-permute-start.10 = (bf16[128,640]{1,0:T(8,128)(2,1)S(1)}, bf16[128,640]{1,0:T(8,128)(2,1)S(1)}, u32[]{:S(2)}, u32[]{:S(2)}) collective-permute-start(bf16[128,640]{1,0:T(8,128)(2,1)S(1)} %shard_map.113.refs_0_), channel_id=1, source_target_pairs={{12,0},{14,2},{0,4},{2,6},{4,8},{6,10},{8,12},{10,14},{28,16},{30,... | collective-permute-start | bytes 491528 | tf_op jit(solution)/shard_map/ppermute | solution.py:473
  45.7 5.3 %shard_map.118 = (f32[4096,512]{1,0:T(8,128)S(1)}, f32[4096,128]{1,0:T(8,128)S(1)}, f32[4096,128]{1,0:T(8,128)S(1)}, bf16[448,640]{1,0:T(8,128)(2,1)S(1)}) custom-call(s32[224]{0:T(256)S(1)} %plan.1.refs_0_, bf16[4096,640]{1,0:T(8,128)(2,1)S(1)} %queries.1.refs_1_, ...), custom_call_target="tpu_custom_call", output_to_operand_aliasing={{0}: (3, {}), {1}: (4, {}), {2}: (5, {})} | custom-call | flops 4831838208 | bytes 25165824 | tf_op jit(solution)/shard_map/pallas_call | solution.py:446
  51.0 3.0 %collective-permute-done.8.refs_1_ = bf16[384,640]{1,0:T(8,128)(2,1)S(1)} collective-permute-done((bf16[384,640]{1,0:T(8,128)(2,1)S(1)}, bf16[384,640]{1,0:T(8,128)(2,1)S(1)}, u32[]{:S(2)}, u32[]{:S(2)}) %collective-permute-start.8) | collective-permute-done | bytes 491552 | tf_op jit(solution)/shard_map/ppermute | solution.py:473
  54.1 1.6 %collective-permute-start.9 = (bf16[512,640]{1,0:T(8,128)(2,1)S(1)}, bf16[512,640]{1,0:T(8,128)(2,1)S(1)}, u32[]{:S(2)}, u32[]{:S(2)}) collective-permute-start(bf16[512,640]{1,0:T(8,128)(2,1)S(1)} %shard_map.116.refs_2_.refs_7_), channel_id=1, source_target_pairs={{2,0},{0,2},{6,4},{4,6},{10,8},{8,10},{14,12},{12,14},{18,16},{16,... | collective-permute-start | bytes 1966088 | tf_op jit(solution)/shard_map/ppermute | solution.py:473
  55.6 0.3 collective-permute-done.10.refs_0_
  56.0 0.6 collective-permute-start.12
  56.7 9.4 %shard_map.119 = (f32[4096,512]{1,0:T(8,128)S(1)}, f32[4096,128]{1,0:T(8,128)S(1)}, f32[4096,128]{1,0:T(8,128)S(1)}, bf16[448,640]{1,0:T(8,128)(2,1)S(1)}) custom-call(s32[224]{0:T(256)S(1)} %plan.1.refs_0_, bf16[4096,640]{1,0:T(8,128)(2,1)S(1)} %queries.1.refs_1_, ...), custom_call_target="tpu_custom_call", output_to_operand_aliasing={{0}: (4, {}), {1}: (5, {}), {2}: (6, {})} | custom-call | flops 4831838208 | bytes 25165824 | tf_op jit(solution)/shard_map/pallas_call | solution.py:446
  66.1 13.3 %shard_map.120 = (f32[4096,512]{1,0:T(8,128)S(1)}, f32[4096,128]{1,0:T(8,128)S(1)}, f32[4096,128]{1,0:T(8,128)S(1)}, bf16[448,640]{1,0:T(8,128)(2,1)S(1)}) custom-call(s32[224]{0:T(256)S(1)} %plan.1.refs_0_, bf16[4096,640]{1,0:T(8,128)(2,1)S(1)} %queries.1.refs_1_, ...), custom_call_target="tpu_custom_call", output_to_operand_aliasing={{0}: (5, {}), {1}: (6, {}), {2}: (7, {})} | custom-call | flops 9663676416 | bytes 25165824 | tf_op jit(solution)/shard_map/pallas_call | solution.py:446
  79.4 13.3 %shard_map.121 = (f32[4096,512]{1,0:T(8,128)S(1)}, f32[4096,128]{1,0:T(8,128)S(1)}, f32[4096,128]{1,0:T(8,128)S(1)}, bf16[448,640]{1,0:T(8,128)(2,1)S(1)}) custom-call(s32[224]{0:T(256)S(1)} %plan.1.refs_0_, bf16[4096,640]{1,0:T(8,128)(2,1)S(1)} %queries.1.refs_1_, ...), custom_call_target="tpu_custom_call", output_to_operand_aliasing={{0}: (5, {}), {1}: (6, {}), {2}: (7, {})} | custom-call | flops 9663676416 | bytes 25165824 | tf_op jit(solution)/shard_map/pallas_call | solution.py:446
  92.7 5.3 %shard_map.122 = (f32[4096,512]{1,0:T(8,128)S(1)}, f32[4096,128]{1,0:T(8,128)S(1)}, f32[4096,128]{1,0:T(8,128)S(1)}, bf16[448,640]{1,0:T(8,128)(2,1)S(1)}) custom-call(s32[224]{0:T(256)S(1)} %plan.1.refs_0_, bf16[4096,640]{1,0:T(8,128)(2,1)S(1)} %queries.1.refs_1_, ...), custom_call_target="tpu_custom_call", output_to_operand_aliasing={{0}: (4, {}), {1}: (5, {}), {2}: (6, {})} | custom-call | flops 4831838208 | bytes 25165824 | tf_op jit(solution)/shard_map/pallas_call | solution.py:446
  98.1 16.5 %shard_map.123 = (f32[4096,512]{1,0:T(8,128)S(1)}, f32[4096,128]{1,0:T(8,128)S(1)}, f32[4096,128]{1,0:T(8,128)S(1)}, bf16[64,8192]{1,0:T(8,128)(2,1)}, bf16[64,576]{1,0:T(8,128)(2,1)}) custom-call(s32[224]{0:T(256)S(1)} %plan.1.refs_0_, bf16[4096,640]{1,0:T(8,128)(2,1)S(1)} %queries.1.refs_1_, ...), custom_call_target="tpu_custom_call", output_to_operand_aliasing={{0}: (12, {}), {1}: (13, {}), {2}: (14, {})} | custom-call | flops 4831838208 | bytes 25165824 | tf_op jit(solution)/shard_map/pallas_call | solution.py:446
  (41 shorter events, 0.6 us)
Async XLA Ops:
  0.6 5.3 %copy-start.5 = (f32[512]{0:T(512)S(1)}, f32[512]{0:T(512)}, u32[]{:S(2)}) copy-start(f32[512]{0:T(512)} %gain_ref.1) | copy-start | bytes 6148
  4.8 5.4 %collective-permute-start = (f32[64,640]{1,0:T(8,128)}, f32[64,640]{1,0:T(8,128)S(1)}, u32[]{:S(2)}, u32[]{:S(2)}) collective-permute-start(f32[64,640]{1,0:T(8,128)} %project.1.mine_ref), channel_id=1, source_target_pairs={{0,1},{1,0},{2,3},{3,2},{4,5},{5,4},{6,7},{7,6},{8,9},{9,8},{10,11... | collective-permute-start | bytes 491528 | tf_op jit(solution)/shard_map/ppermute | solution.py:486
  5.9 0.9 copy-start.2
  10.2 23.4 %slice-start.2 = ((s8[8388608]{0:T(1024)(128)(4,1)}), s8[4194304]{0:T(1024)(128)(4,1)S(1)}, s32[]{:S(2)}) async-start(s8[8388608]{0:T(1024)(128)(4,1)} %bitcast.4), calls=%async_computation.2 | async-start | bytes 8388608
  10.2 23.5 %slice-start.3 = ((s8[8388608]{0:T(1024)(128)(4,1)}), s8[4194304]{0:T(1024)(128)(4,1)S(1)}, s32[]{:S(2)}) async-start(s8[8388608]{0:T(1024)(128)(4,1)} %bitcast.4), calls=%async_computation.3 | async-start | bytes 8388608
  10.4 21.9 %copy-start.3 = (s32[4096]{0:T(1024)S(1)}, s32[4096]{0:T(1024)}, u32[]{:S(2)}) copy-start(s32[4096]{0:T(1024)} %docs_ref.1) | copy-start | bytes 49156
  10.4 21.9 %copy-start.4 = (s32[256]{0:T(256)S(1)}, s32[256]{0:T(256)}, u32[]{:S(2)}) copy-start(s32[256]{0:T(256)} %slots_ref.1) | copy-start | bytes 3076
  10.4 23.2 %copy-start = (bf16[64,8192]{1,0:T(8,128)(2,1)S(1)}, bf16[64,8192]{1,0:T(8,128)(2,1)}, u32[]{:S(2)}) copy-start(bf16[64,8192]{1,0:T(8,128)(2,1)} %nope_ref.1) | copy-start | bytes 3145732
  10.4 23.2 %copy-start.1 = (bf16[64,4096]{1,0:T(8,128)(2,1)S(1)}, bf16[64,4096]{1,0:T(8,128)(2,1)}, u32[]{:S(2)}) copy-start(bf16[64,4096]{1,0:T(8,128)(2,1)} %pe_ref.1) | copy-start | bytes 1572868
  10.4 4.9 %collective-permute-start.1 = (bf16[64,640]{1,0:T(8,128)(2,1)S(1)}, bf16[64,640]{1,0:T(8,128)(2,1)S(1)}, u32[]{:S(2)}, u32[]{:S(2)}) collective-permute-start(bf16[64,640]{1,0:T(8,128)(2,1)S(1)} %finish.1.refs_0_), channel_id=1, source_target_pairs={{64,0},{66,2},{68,4},{70,6},{72,8},{74,10},{76,12},{78,14},{80,16}... | collective-permute-start | bytes 245768 | tf_op jit(solution)/shard_map/ppermute | solution.py:473
  15.3 4.2 %collective-permute-start.4 = (bf16[128,640]{1,0:T(8,128)(2,1)S(1)}, bf16[128,640]{1,0:T(8,128)(2,1)S(1)}, u32[]{:S(2)}, u32[]{:S(2)}) collective-permute-start(bf16[128,640]{1,0:T(8,128)(2,1)S(1)} %shard_map.113.refs_0_), channel_id=1, source_target_pairs={{48,0},{50,2},{52,4},{54,6},{56,8},{58,10},{60,12},{62,14},{0,16},... | collective-permute-start | bytes 491528 | tf_op jit(solution)/shard_map/ppermute | solution.py:473
  15.4 5.8 %collective-permute-start.3 = (bf16[128,640]{1,0:T(8,128)(2,1)S(1)}, bf16[128,640]{1,0:T(8,128)(2,1)S(1)}, u32[]{:S(2)}, u32[]{:S(2)}) collective-permute-start(bf16[128,640]{1,0:T(8,128)(2,1)S(1)} %shard_map.113.refs_0_), channel_id=1, source_target_pairs={{32,0},{34,2},{36,4},{38,6},{40,8},{42,10},{44,12},{46,14},{48,16}... | collective-permute-start | bytes 491528 | tf_op jit(solution)/shard_map/ppermute | solution.py:473
  17.3 6.3 %collective-permute-start.2 = (bf16[128,640]{1,0:T(8,128)(2,1)S(1)}, bf16[128,640]{1,0:T(8,128)(2,1)S(1)}, u32[]{:S(2)}, u32[]{:S(2)}) collective-permute-start(bf16[128,640]{1,0:T(8,128)(2,1)S(1)} %shard_map.113.refs_0_), channel_id=1, source_target_pairs={{16,0},{18,2},{20,4},{22,6},{24,8},{26,10},{28,12},{30,14},{32,16}... | collective-permute-start | bytes 491528 | tf_op jit(solution)/shard_map/ppermute | solution.py:473
  23.7 32.9 %collective-permute-start.5 = (bf16[512,640]{1,0:T(8,128)(2,1)S(1)}, bf16[512,640]{1,0:T(8,128)(2,1)S(1)}, u32[]{:S(2)}, u32[]{:S(2)}) collective-permute-start(bf16[512,640]{1,0:T(8,128)(2,1)S(1)} %shard_map.115.refs_2_.refs_5_), channel_id=1, source_target_pairs={{8,0},{10,2},{12,4},{14,6},{0,8},{2,10},{4,12},{6,14},{24,16},{26,... | collective-permute-start | bytes 1966088 | tf_op jit(solution)/shard_map/ppermute | solution.py:473
  23.8 32.9 %collective-permute-start.13 = (bf16[512,640]{1,0:T(8,128)(2,1)S(1)}, bf16[512,640]{1,0:T(8,128)(2,1)S(1)}, u32[]{:S(2)}, u32[]{:S(2)}) collective-permute-start(bf16[512,640]{1,0:T(8,128)(2,1)S(1)} %shard_map.115.refs_2_.refs_5_), channel_id=1, source_target_pairs={{2,0},{0,2},{6,4},{4,6},{10,8},{8,10},{14,12},{12,14},{18,16},{16,... | collective-permute-start | bytes 1966088 | tf_op jit(solution)/shard_map/ppermute | solution.py:473
  27.9 14.3 %collective-permute-start.7 = (bf16[128,640]{1,0:T(8,128)(2,1)S(1)}, bf16[128,640]{1,0:T(8,128)(2,1)S(1)}, u32[]{:S(2)}, u32[]{:S(2)}) collective-permute-start(bf16[128,640]{1,0:T(8,128)(2,1)S(1)} %shard_map.113.refs_0_), channel_id=1, source_target_pairs={{4,0},{6,2},{8,4},{10,6},{12,8},{14,10},{0,12},{2,14},{20,16},{22,... | collective-permute-start | bytes 491528 | tf_op jit(solution)/shard_map/ppermute | solution.py:473
  30.0 24.0 %collective-permute-start.8 = (bf16[384,640]{1,0:T(8,128)(2,1)S(1)}, bf16[384,640]{1,0:T(8,128)(2,1)S(1)}, u32[]{:S(2)}, u32[]{:S(2)}) collective-permute-start(bf16[384,640]{1,0:T(8,128)(2,1)S(1)} %shard_map.114.refs_1_), channel_id=1, source_target_pairs={{4,0},{6,2},{8,4},{10,6},{12,8},{14,10},{0,12},{2,14},{20,16},{22,... | collective-permute-start | bytes 1474568 | tf_op jit(solution)/shard_map/ppermute | solution.py:473
  31.1 24.9 %collective-permute-start.11 = (bf16[384,640]{1,0:T(8,128)(2,1)S(1)}, bf16[384,640]{1,0:T(8,128)(2,1)S(1)}, u32[]{:S(2)}, u32[]{:S(2)}) collective-permute-start(bf16[384,640]{1,0:T(8,128)(2,1)S(1)} %shard_map.114.refs_1_), channel_id=1, source_target_pairs={{12,0},{14,2},{0,4},{2,6},{4,8},{6,10},{8,12},{10,14},{28,16},{30,... | collective-permute-start | bytes 1474568 | tf_op jit(solution)/shard_map/ppermute | solution.py:473
  42.2 13.8 %collective-permute-start.10 = (bf16[128,640]{1,0:T(8,128)(2,1)S(1)}, bf16[128,640]{1,0:T(8,128)(2,1)S(1)}, u32[]{:S(2)}, u32[]{:S(2)}) collective-permute-start(bf16[128,640]{1,0:T(8,128)(2,1)S(1)} %shard_map.113.refs_0_), channel_id=1, source_target_pairs={{12,0},{14,2},{0,4},{2,6},{4,8},{6,10},{8,12},{10,14},{28,16},{30,... | collective-permute-start | bytes 491528 | tf_op jit(solution)/shard_map/ppermute | solution.py:473
  54.1 25.4 %collective-permute-start.9 = (bf16[512,640]{1,0:T(8,128)(2,1)S(1)}, bf16[512,640]{1,0:T(8,128)(2,1)S(1)}, u32[]{:S(2)}, u32[]{:S(2)}) collective-permute-start(bf16[512,640]{1,0:T(8,128)(2,1)S(1)} %shard_map.116.refs_2_.refs_7_), channel_id=1, source_target_pairs={{2,0},{0,2},{6,4},{4,6},{10,8},{8,10},{14,12},{12,14},{18,16},{16,... | collective-permute-start | bytes 1966088 | tf_op jit(solution)/shard_map/ppermute | solution.py:473
  56.0 23.4 %collective-permute-start.12 = (bf16[512,640]{1,0:T(8,128)(2,1)S(1)}, bf16[512,640]{1,0:T(8,128)(2,1)S(1)}, u32[]{:S(2)}, u32[]{:S(2)}) collective-permute-start(bf16[512,640]{1,0:T(8,128)(2,1)S(1)} %shard_map.117.refs_3_.refs_8_), channel_id=1, source_target_pairs={{2,0},{0,2},{6,4},{4,6},{10,8},{8,10},{14,12},{12,14},{18,16},{16,... | collective-permute-start | bytes 1966088 | tf_op jit(solution)/shard_map/ppermute | solution.py:473
  56.6 41.4 %collective-permute-start.6 = (bf16[512,640]{1,0:T(8,128)(2,1)S(1)}, bf16[512,640]{1,0:T(8,128)(2,1)S(1)}, u32[]{:S(2)}, u32[]{:S(2)}) collective-permute-start(bf16[512,640]{1,0:T(8,128)(2,1)S(1)} %collective-permute-done.5.refs_2_.refs_11_), channel_id=1, source_target_pairs={{2,0},{0,2},{6,4},{4,6},{10,8},{8,10},{14,12},{12,14},{18,16},{16,... | collective-permute-start | bytes 1966088 | tf_op jit(solution)/shard_map/ppermute | solution.py:473
  92.7 5.3 %slice-start = ((s8[8388608]{0:T(1024)(128)(4,1)}), s8[4194304]{0:T(1024)(128)(4,1)S(1)}, s32[]{:S(2)}) async-start(s8[8388608]{0:T(1024)(128)(4,1)} %bitcast.2), calls=%async_computation | async-start | bytes 8388608
  92.7 5.3 %slice-start.1 = ((s8[8388608]{0:T(1024)(128)(4,1)}), s8[4194304]{0:T(1024)(128)(4,1)S(1)}, s32[]{:S(2)}) async-start(s8[8388608]{0:T(1024)(128)(4,1)} %bitcast.2), calls=%async_computation.1 | async-start | bytes 8388608
